TPU v7x, 32 devices: a whole 2x2x4 slice. The times are simulated.
32 devices in a mesh: dp: 4 (over y, x), ctx: 8 (over z, core).
Axes of the slice: x: 2, y: 2, z: 4, core: 2. Of those that a mesh axis runs over, the one named last changes fastest.
Arguments:
- layer_input: bfloat16 [4, 1024, 2048], P('dp', 'ctx'), may hold values from -6 to 6
- cotangent: bfloat16 [4, 1024, 2048], P('dp', 'ctx'), may hold values from -6 to 6
- prefix: int32 [4], P('dp'), may hold values from 102 to 512
- w_query: float32 [2048, 2048], P(('dp', 'ctx')), may hold values from -0.125 to 0.125
- key_weight: float32 [2048, 1024], P(('dp', 'ctx')), may hold values from -0.125 to 0.125
- value_weight: float32 [2048, 1024], P(('dp', 'ctx')), may hold values from -0.125 to 0.125
- w_out: float32 [2048, 2048], P(('dp', 'ctx')), may hold values from -1.25 to 1.25
- w_gate: float32 [2048, 8192], P(('dp', 'ctx')), may hold values from -0.125 to 0.125
- w_up: float32 [2048, 8192], P(('dp', 'ctx')), may hold values from -0.125 to 0.125
- w_down: float32 [8192, 2048], P(('dp', 'ctx')), may hold values from -0.0625 to 0.0625
- attention_norm_gain: float32 [2048], P(('dp', 'ctx')), may hold values from 0.5 to 1.5
- feedforward_norm_gain: float32 [2048], P(('dp', 'ctx')), may hold values from 0.5 to 1.5
Outputs:
- output: bfloat16 [4, 1024, 2048], P('dp', 'ctx')
- input_grad: bfloat16 [4, 1024, 2048], P('dp', 'ctx')
- w_query_grad: float32 [2048, 2048], P(('dp', 'ctx'))
- w_key_grad: float32 [2048, 1024], P(('dp', 'ctx'))
- w_value_grad: float32 [2048, 1024], P(('dp', 'ctx'))
- w_out_grad: float32 [2048, 2048], P(('dp', 'ctx'))
- w_gate_grad: float32 [2048, 8192], P(('dp', 'ctx'))
- w_up_grad: float32 [2048, 8192], P(('dp', 'ctx'))
- w_down_grad: float32 [8192, 2048], P(('dp', 'ctx'))
- gain_attn_grad: float32 [2048], P(('dp', 'ctx'))
- gain_mlp_grad: float32 [2048], P(('dp', 'ctx'))
Inputs may be any that keep to these rules, and one draw needn't show every extreme that they name: `prefix`: the number of leading tokens of each sequence that attend to one another both ways.
All inputs are finite; a program needn't handle non-finite values.
Results may differ from a plain program's by a relative error of at most 0.025.
Values may be sent and summed in bfloat16 or wider, within the bound.
No kernel may reach another device: no remote copies, remote signals or barrier semaphores. Data moves between devices by JAX's collectives and lax.ppermute only.
A program may use at most 640 MiB of HBM per device.

v0:
```python
import jax
import jax.numpy as jnp
from jax import lax
from jax.sharding import PartitionSpec as P

FF = 8192
QUERY_HEADS = 8
KEY_VALUE_HEADS = 4
HEAD_SIZE = 256


NORM_EPSILON = 1e-06
THETA = 1000042.0


def rope_angles(token_positions, width):
    half_width = width // 2
    frequency = jnp.power(THETA, -(2.0 * jnp.arange(half_width, dtype=jnp.float32) / width))
    angles = token_positions.astype(jnp.float32)[:, None] * frequency[None, :]
    return (jnp.cos(angles)[:, None, :], jnp.sin(angles)[:, None, :])


def apply_rotary(vector, cosine_table, sines_lookup):
    half_width = vector.shape[-1] // 2
    first_half = vector[..., :half_width]
    second_half = vector[..., half_width:]
    return jnp.concatenate(
        [
            first_half * cosine_table - second_half * sines_lookup,
            second_half * cosine_table + first_half * sines_lookup,
        ],
        axis=-1,
    )


def reverse_rotary(vector, cosine_table, sines_lookup):
    half_width = vector.shape[-1] // 2
    first_half = vector[..., :half_width]
    second_half = vector[..., half_width:]
    return jnp.concatenate(
        [
            first_half * cosine_table + second_half * sines_lookup,
            second_half * cosine_table - first_half * sines_lookup,
        ],
        axis=-1,
    )


def norm_backward(d_normed, hat_values, gain_row, inverse):
    scaled = d_normed * gain_row
    return inverse * (scaled - hat_values * jnp.mean(scaled * hat_values, axis=-1, keepdims=True))


def column_product(left, right):
    return jnp.einsum("bd,bf->df", left, right, preferred_element_type=jnp.float32)


def local(
    layer_input,
    cotangent,
    prefix,
    w_query,
    key_weight,
    value_weight,
    w_out,
    w_gate,
    w_up,
    w_down,
    attention_norm_gain,
    feedforward_norm_gain,
):
    narrow_number_type = jnp.bfloat16
    wide_number_type = jnp.float32
    token_rows = layer_input.shape[1]
    query_group_width = QUERY_HEADS // KEY_VALUE_HEADS
    attention_score_scale = HEAD_SIZE ** (-0.5)
    input_rows_all = layer_input[0].astype(wide_number_type)
    first_row = lax.axis_index("ctx") * token_rows
    token_positions = first_row + jnp.arange(token_rows, dtype=jnp.int32)
    prefix_len = prefix[0]
    cosine_table, sines_lookup = rope_angles(token_positions, HEAD_SIZE)
    attn_kept = (
        lax.all_gather(w_query.astype(narrow_number_type), ("dp", "ctx"), axis=0, tiled=True),
        lax.all_gather(key_weight.astype(narrow_number_type), ("dp", "ctx"), axis=0, tiled=True),
        lax.all_gather(value_weight.astype(narrow_number_type), ("dp", "ctx"), axis=0, tiled=True),
        lax.all_gather(w_out.astype(narrow_number_type), ("dp", "ctx"), axis=0, tiled=True),
        lax.all_gather(
            attention_norm_gain.astype(narrow_number_type), ("dp", "ctx"), axis=0, tiled=True
        ),
    )
    query_w, key_matrix, value_w, out_w, attention_gain = attn_kept
    first_inverse_norm = lax.rsqrt(
        jnp.mean(input_rows_all * input_rows_all, axis=-1, keepdims=True) + NORM_EPSILON
    )
    first_standardized = input_rows_all * first_inverse_norm
    first_normalized = (first_standardized * attention_gain.astype(wide_number_type)).astype(
        narrow_number_type
    )
    query_rows = jnp.dot(
        first_normalized, query_w, preferred_element_type=wide_number_type
    ).reshape(token_rows, QUERY_HEADS, HEAD_SIZE)
    projected_keys = jnp.dot(
        first_normalized, key_matrix, preferred_element_type=wide_number_type
    ).reshape(token_rows, KEY_VALUE_HEADS, HEAD_SIZE)
    value_rows = jnp.dot(first_normalized, value_w, preferred_element_type=wide_number_type).astype(
        narrow_number_type
    )
    rotated_queries = apply_rotary(query_rows, cosine_table, sines_lookup).astype(
        narrow_number_type
    )
    rotated_keys = (
        apply_rotary(projected_keys, cosine_table, sines_lookup)
        .astype(narrow_number_type)
        .reshape(token_rows, KEY_VALUE_HEADS * HEAD_SIZE)
    )
    grouped_queries = rotated_queries.reshape(
        token_rows, KEY_VALUE_HEADS, query_group_width, HEAD_SIZE
    )

    def masked_scores(key_segment, start_row):
        segment_rows = key_segment.shape[0]
        columns = start_row + jnp.arange(segment_rows, dtype=jnp.int32)
        allowed = (columns[None, :] <= token_positions[:, None]) | (columns[None, :] < prefix_len)
        scores = (
            jnp.einsum(
                "bkgd,jkd->kgbj",
                grouped_queries,
                key_segment.reshape(segment_rows, KEY_VALUE_HEADS, HEAD_SIZE),
                preferred_element_type=wide_number_type,
            )
            * attention_score_scale
        )
        return jnp.where(allowed[None, None], scores, -jnp.inf)

    row_maximum = jnp.full(
        (KEY_VALUE_HEADS, query_group_width, token_rows), -1e30, wide_number_type
    )
    key_segment = lax.all_gather(rotated_keys, "ctx", axis=0, tiled=True)
    value_segment = lax.all_gather(value_rows, "ctx", axis=0, tiled=True)
    segment_rows = value_segment.shape[0]
    scores = masked_scores(key_segment, jnp.int32(0))
    new_peak = jnp.maximum(row_maximum, jnp.max(scores, axis=-1))
    soft_part = jnp.exp(scores - new_peak[..., None])
    row_denominator = jnp.sum(soft_part, axis=-1)
    weighted_values = jnp.einsum(
        "kgbj,jkd->bkgd",
        soft_part.astype(narrow_number_type),
        value_segment.reshape(segment_rows, KEY_VALUE_HEADS, HEAD_SIZE),
        preferred_element_type=wide_number_type,
    )
    row_maximum, row_denominator, weighted_values = (new_peak, row_denominator, weighted_values)
    log_total = row_maximum + jnp.log(row_denominator)
    attention_result = weighted_values / jnp.transpose(row_denominator, (2, 0, 1))[..., None]
    attn_out = attention_result.reshape(token_rows, QUERY_HEADS * HEAD_SIZE).astype(
        narrow_number_type
    )
    hidden_middle = input_rows_all + jnp.dot(
        attn_out, out_w, preferred_element_type=wide_number_type
    )
    mlp_kept = (
        lax.all_gather(w_gate.astype(narrow_number_type), ("dp", "ctx"), axis=0, tiled=True),
        lax.all_gather(w_up.astype(narrow_number_type), ("dp", "ctx"), axis=0, tiled=True),
        lax.all_gather(w_down.astype(narrow_number_type), ("dp", "ctx"), axis=0, tiled=True),
        lax.all_gather(
            feedforward_norm_gain.astype(narrow_number_type), ("dp", "ctx"), axis=0, tiled=True
        ),
    )
    gate_w, up_w, down_w, feedforward_gain = mlp_kept
    second_inverse_norm = lax.rsqrt(
        jnp.mean(hidden_middle * hidden_middle, axis=-1, keepdims=True) + NORM_EPSILON
    )
    second_standardized = hidden_middle * second_inverse_norm
    second_normalized = (second_standardized * feedforward_gain.astype(wide_number_type)).astype(
        narrow_number_type
    )
    gate_proj = jnp.dot(second_normalized, gate_w, preferred_element_type=wide_number_type)
    up_proj = jnp.dot(second_normalized, up_w, preferred_element_type=wide_number_type)
    hidden = (jax.nn.silu(gate_proj) * up_proj).astype(narrow_number_type)
    result = hidden_middle + jnp.dot(hidden, down_w, preferred_element_type=wide_number_type)
    output = result.astype(narrow_number_type)[None]
    gate_w, up_w, down_w, feedforward_gain = (
        lax.all_gather(w_gate.astype(narrow_number_type), ("dp", "ctx"), axis=0, tiled=True),
        lax.all_gather(w_up.astype(narrow_number_type), ("dp", "ctx"), axis=0, tiled=True),
        lax.all_gather(w_down.astype(narrow_number_type), ("dp", "ctx"), axis=0, tiled=True),
        lax.all_gather(
            feedforward_norm_gain.astype(narrow_number_type), ("dp", "ctx"), axis=0, tiled=True
        ),
    )
    d_out = cotangent[0]
    down_sum = lax.psum_scatter(
        column_product(hidden, d_out), ("dp", "ctx"), scatter_dimension=0, tiled=True
    )
    d_hidden = jnp.einsum("bd,fd->bf", d_out, down_w, preferred_element_type=wide_number_type)
    sigmoid_gate = jax.nn.sigmoid(gate_proj)
    d_gate = (d_hidden * up_proj * sigmoid_gate * (1.0 + gate_proj * (1.0 - sigmoid_gate))).astype(
        narrow_number_type
    )
    d_up = (d_hidden * gate_proj * sigmoid_gate).astype(narrow_number_type)
    second_normalized_gradient = jnp.einsum(
        "bf,df->bd", d_gate, gate_w, preferred_element_type=wide_number_type
    ) + jnp.einsum("bf,df->bd", d_up, up_w, preferred_element_type=wide_number_type)
    gate_and_up = jnp.concatenate([d_gate, d_up], axis=1)
    both_sum = lax.psum_scatter(
        column_product(second_normalized, gate_and_up),
        ("dp", "ctx"),
        scatter_dimension=0,
        tiled=True,
    )
    gate_sum = both_sum[:, :FF]
    up_sum = both_sum[:, FF:]
    feedforward_gain_part = jnp.sum(second_normalized_gradient * second_standardized, axis=0)
    middle_gradient = d_out.astype(wide_number_type) + norm_backward(
        second_normalized_gradient,
        second_standardized,
        feedforward_gain.astype(wide_number_type),
        second_inverse_norm,
    )
    query_w, key_matrix, value_w, out_w, attention_gain = (
        lax.all_gather(w_query.astype(narrow_number_type), ("dp", "ctx"), axis=0, tiled=True),
        lax.all_gather(key_weight.astype(narrow_number_type), ("dp", "ctx"), axis=0, tiled=True),
        lax.all_gather(value_weight.astype(narrow_number_type), ("dp", "ctx"), axis=0, tiled=True),
        lax.all_gather(w_out.astype(narrow_number_type), ("dp", "ctx"), axis=0, tiled=True),
        lax.all_gather(
            attention_norm_gain.astype(narrow_number_type), ("dp", "ctx"), axis=0, tiled=True
        ),
    )
    d_branch = middle_gradient.astype(narrow_number_type)
    out_sum = lax.psum_scatter(
        column_product(attn_out, d_branch), ("dp", "ctx"), scatter_dimension=0, tiled=True
    )
    attention_gradient = jnp.einsum(
        "bd,hd->bh", d_branch, out_w, preferred_element_type=wide_number_type
    ).astype(narrow_number_type)
    attention_group_gradient = attention_gradient.reshape(
        token_rows, KEY_VALUE_HEADS, query_group_width, HEAD_SIZE
    )
    delta_rows = jnp.transpose(
        jnp.sum(attention_group_gradient.astype(wide_number_type) * attention_result, axis=-1),
        (1, 2, 0),
    )
    gathered_keys, gathered_values = (
        lax.all_gather(rotated_keys, "ctx", axis=0, tiled=True),
        lax.all_gather(value_rows, "ctx", axis=0, tiled=True),
    )
    count_of_blocks = gathered_keys.shape[0] // token_rows
    stacked_key_blocks = gathered_keys.reshape(
        count_of_blocks, token_rows, KEY_VALUE_HEADS * HEAD_SIZE
    )
    stacked_value_blocks = gathered_values.reshape(
        count_of_blocks, token_rows, KEY_VALUE_HEADS, HEAD_SIZE
    )

    def back_step(d_query_sum, block_item):
        current_key_block, value_block, block_index = block_item
        scores = masked_scores(current_key_block, block_index * token_rows)
        soft_part = jnp.exp(scores - log_total[..., None])
        d_value_block = jnp.einsum(
            "kgbj,bkgd->jkd",
            soft_part.astype(narrow_number_type),
            attention_group_gradient,
            preferred_element_type=wide_number_type,
        )
        d_probs = jnp.einsum(
            "bkgd,jkd->kgbj",
            attention_group_gradient,
            value_block,
            preferred_element_type=wide_number_type,
        )
        d_scores = (soft_part * (d_probs - delta_rows[..., None])).astype(narrow_number_type)
        key_tensor_triple = current_key_block.reshape(token_rows, KEY_VALUE_HEADS, HEAD_SIZE)
        d_query_sum = d_query_sum + jnp.einsum(
            "kgbj,jkd->bkgd", d_scores, key_tensor_triple, preferred_element_type=wide_number_type
        )
        d_key_block = jnp.einsum(
            "kgbj,bkgd->jkd", d_scores, grouped_queries, preferred_element_type=wide_number_type
        )
        return (d_query_sum, (d_key_block, d_value_block))

    d_query_sum, (key_gradients, value_gradients) = lax.scan(
        back_step,
        jnp.zeros((token_rows, KEY_VALUE_HEADS, query_group_width, HEAD_SIZE), wide_number_type),
        (stacked_key_blocks, stacked_value_blocks, jnp.arange(count_of_blocks, dtype=jnp.int32)),
    )
    key_gradients = (
        key_gradients.reshape(count_of_blocks * token_rows, KEY_VALUE_HEADS * HEAD_SIZE)
        * attention_score_scale
    )
    value_gradients = value_gradients.reshape(
        count_of_blocks * token_rows, KEY_VALUE_HEADS * HEAD_SIZE
    )
    local_keys, own_values = (
        lax.psum_scatter(
            key_gradients.astype(jnp.bfloat16), "ctx", scatter_dimension=0, tiled=True
        ).astype(jnp.float32),
        lax.psum_scatter(
            value_gradients.astype(jnp.bfloat16), "ctx", scatter_dimension=0, tiled=True
        ).astype(jnp.float32),
    )
    d_key = (
        reverse_rotary(
            local_keys.reshape(token_rows, KEY_VALUE_HEADS, HEAD_SIZE), cosine_table, sines_lookup
        )
        .reshape(token_rows, KEY_VALUE_HEADS * HEAD_SIZE)
        .astype(narrow_number_type)
    )
    d_value = own_values.astype(narrow_number_type)
    d_query = reverse_rotary(
        (d_query_sum * attention_score_scale).reshape(token_rows, QUERY_HEADS, HEAD_SIZE),
        cosine_table,
        sines_lookup,
    )
    d_query = d_query.reshape(token_rows, QUERY_HEADS * HEAD_SIZE).astype(narrow_number_type)
    d_projected = jnp.concatenate([d_query, d_key, d_value], axis=1)
    projection_total = lax.psum_scatter(
        column_product(first_normalized, d_projected),
        ("dp", "ctx"),
        scatter_dimension=0,
        tiled=True,
    )
    query_sum = projection_total[:, : QUERY_HEADS * HEAD_SIZE]
    key_gradient_sum = projection_total[
        :, QUERY_HEADS * HEAD_SIZE : QUERY_HEADS * HEAD_SIZE + KEY_VALUE_HEADS * HEAD_SIZE
    ]
    value_gradient_sum = projection_total[
        :, QUERY_HEADS * HEAD_SIZE + KEY_VALUE_HEADS * HEAD_SIZE :
    ]
    first_normalized_gradient = (
        jnp.einsum("bh,dh->bd", d_query, query_w, preferred_element_type=wide_number_type)
        + jnp.einsum("bh,dh->bd", d_key, key_matrix, preferred_element_type=wide_number_type)
        + jnp.einsum("bh,dh->bd", d_value, value_w, preferred_element_type=wide_number_type)
    )
    attention_gain_part = jnp.sum(first_normalized_gradient * first_standardized, axis=0)
    gradient_of_input = middle_gradient + norm_backward(
        first_normalized_gradient,
        first_standardized,
        attention_gain.astype(wide_number_type),
        first_inverse_norm,
    )
    attn_gain_sum, mlp_gain_sum = (
        lax.psum_scatter(attention_gain_part, ("dp", "ctx"), scatter_dimension=0, tiled=True),
        lax.psum_scatter(feedforward_gain_part, ("dp", "ctx"), scatter_dimension=0, tiled=True),
    )
    input_grad = gradient_of_input.astype(narrow_number_type)[None]
    return (
        output,
        input_grad,
        query_sum,
        key_gradient_sum,
        value_gradient_sum,
        out_sum,
        gate_sum,
        up_sum,
        down_sum,
        attn_gain_sum,
        mlp_gain_sum,
    )


def solution(mesh):
    in_specs = (
        P("dp", "ctx", None),
        P("dp", "ctx", None),
        P("dp"),
        P(("dp", "ctx"), None),
        P(("dp", "ctx"), None),
        P(("dp", "ctx"), None),
        P(("dp", "ctx"), None),
        P(("dp", "ctx"), None),
        P(("dp", "ctx"), None),
        P(("dp", "ctx"), None),
        P(("dp", "ctx")),
        P(("dp", "ctx")),
    )
    out_specs = (
        P("dp", "ctx", None),
        P("dp", "ctx", None),
        P(("dp", "ctx"), None),
        P(("dp", "ctx"), None),
        P(("dp", "ctx"), None),
        P(("dp", "ctx"), None),
        P(("dp", "ctx"), None),
        P(("dp", "ctx"), None),
        P(("dp", "ctx"), None),
        P(("dp", "ctx")),
        P(("dp", "ctx")),
    )
    return jax.shard_map(local, mesh=mesh, in_specs=in_specs, out_specs=out_specs, check_vma=False)
```

profile of v0, /device:TPU:0, one launch (start us, length us, event | category | flops | bytes accessed | tf_op | source)
XLA Modules:
  0.0 4301.4 jit_solution(16916294150234120928)
XLA Ops:
  12.4 42.2 all-reduce.6
  55.8 20.7 all-gather.10.cloned.1.call-done
  76.5 3.8 convolution_convert_fusion.1
  80.8 60.0 %all-gather.14.cloned.1.call-done = bf16[2048,1024]{1,0:T(8,128)(2,1)} async-done(((bf16[64,1024]{1,0:T(8,128)(2,1)}), bf16[2048,1024]{1,0:T(8,128)(2,1)}) %all-gather.14.cloned.1.call-update) | async-done | bytes 4194320 | tf_op jit(solution)/shard_map/all_gather | solution.py:84
  140.8 6.5 copy.54
  147.4 4.0 fusion.68
  152.4 1.8 convert_element_type.161
  157.3 2.8 convert_element_type.169
  162.3 8.3 all-gather.12.cloned.1.call-done
  170.7 4.5 reshape.288
  175.2 3.9 copy.80
  179.1 23.9 all-gather.16.cloned.1.call-done
  203.1 3.3 copy_bitcast_fusion.2
  206.4 76.6 %all-gather.18.cloned.1.call-done = bf16[2048,2048]{1,0:T(8,128)(2,1)} async-done(((bf16[64,2048]{1,0:T(8,128)(2,1)}), bf16[2048,2048]{1,0:T(8,128)(2,1)}) %all-gather.18.cloned.1.call-update) | async-done | bytes 8388624 | tf_op jit(solution)/shard_map/all_gather | solution.py:83
  283.0 12.5 copy.56
  295.5 6.4 fusion.66
  304.2 2.4 fusion.81
  306.6 55.7 %all-gather.20.cloned.1.call-done = bf16[2048,2048]{1,0:T(8,128)(2,1)} async-done(((bf16[64,2048]{1,0:T(8,128)(2,1)}), bf16[2048,2048]{1,0:T(8,128)(2,1)}) %all-gather.20.cloned.1.call-update) | async-done | bytes 8388624 | tf_op jit(solution)/shard_map/all_gather | solution.py:86
  362.3 4.9 multiply_reduce_fusion.3
  367.4 191.8 %all-gather.24.cloned.1.call-done = bf16[2048,8192]{1,0:T(8,128)(2,1)} async-done(((bf16[64,8192]{1,0:T(8,128)(2,1)}), bf16[2048,8192]{1,0:T(8,128)(2,1)}) %all-gather.24.cloned.1.call-update) | async-done | bytes 33554448 | tf_op jit(solution)/shard_map/all_gather | solution.py:162
  559.2 17.6 fusion.83
  576.8 179.0 %all-gather.22.cloned.1.call-done = bf16[2048,8192]{1,0:T(8,128)(2,1)} async-done(((bf16[64,8192]{1,0:T(8,128)(2,1)}), bf16[2048,8192]{1,0:T(8,128)(2,1)}) %all-gather.22.cloned.1.call-update) | async-done | bytes 33554448 | tf_op jit(solution)/shard_map/all_gather | solution.py:161
  755.8 18.2 fusion.82
  774.0 177.8 %all-gather.26.cloned.1.call-done = bf16[8192,2048]{1,0:T(8,128)(2,1)} async-done(((bf16[256,2048]{1,0:T(8,128)(2,1)}), bf16[8192,2048]{1,0:T(8,128)(2,1)}) %all-gather.26.cloned.1.call-update) | async-done | bytes 33554448 | tf_op jit(solution)/shard_map/all_gather | solution.py:163
  951.8 20.9 multiply_convert_fusion.1
  972.7 16.3 fusion.84
  989.0 18.5 multiply_reduce_fusion
  1010.1 6.3 convolution_convert_fusion
  1018.2 57.0 %while.15 = (s32[]{:T(128)}, f32[128,4,2,256]{0,3,2,1:T(8,128)S(1)}, f32[8,128,4,256]{3,1,2,0:T(8,128)}, bf16[8,128,4,256]{3,1,2,0:T(8,128)(2,1)}, bf16[8,128,10...) while((s32[]{:T(128)}, ...), condition=%wide.region_7.8_spmd.clone, body=%wide.region_6.7_spmd.clone.sunk | while | flops 337019392 | bytes 9480671 | solution.py:279
  1075.2 2.7 multiply_convert_fusion
  1079.6 1.8 copy.97
  1081.5 3.2 copy.90
  1084.7 1.9 copy.98
  1086.7 46.6 %fusion.13 = f32[2048,16384]{1,0:T(8,128)} fusion(bf16[128,2048]{1,0:T(8,128)(2,1)S(1)} %copy-done.9, bf16[128,8192]{1,0:T(8,128)(2,1)} %get-tuple-element.205, bf16[128,8192]{1,0:T(8,128)(2,1)} %get-tuple-element.206), kind=kOutput, calls=%fused_computation.24 | convolution fusion | flops 8598323200 | bytes 138936320 | tf_op jit(solution)/shard_map/bd,bf->df/dot_general | solution.py:55
  1136.5 15.8 reduce-scatter.18.cloned.1.call-done
  1153.4 15.5 fusion.47
  1170.3 8.1 fusion.63
  1179.4 26.0 fusion.58
  1205.4 6.6 fusion.85
  1212.0 18.2 fusion.21
  1234.3 39.6 all-reduce.5
  1276.2 1759.5 %all-reduce.9.cloned.1.call-done = f32[2048,16384]{1,0:T(8,128)} async-done(((f32[2048,16384]{1,0:T(8,128)}), f32[2048,16384]{1,0:T(8,128)}) %all-reduce.9.cloned.1.call-update) | async-done | bytes 134217744
  3035.8 4.9 fusion.78
  3040.7 357.8 %reduce-scatter.10.cloned.1.call-done = f32[64,4096]{1,0:T(8,128)} async-done(((f32[2048,4096]{1,0:T(8,128)}), f32[64,4096]{1,0:T(8,128)}) %reduce-scatter.10.cloned.1.call-update) | async-done | bytes 1048592 | tf_op jit(solution)/shard_map/reduce_scatter | solution.py:314
  3398.5 1.9 slice.60
  3400.4 1.9 fusion.79
  3402.3 182.2 %reduce-scatter.12.cloned.1.call-done = f32[64,2048]{1,0:T(8,128)} async-done(((f32[2048,2048]{1,0:T(8,128)}), f32[64,2048]{1,0:T(8,128)}) %reduce-scatter.12.cloned.1.call-update) | async-done | bytes 524304 | tf_op jit(solution)/shard_map/reduce_scatter | solution.py:228
  3584.5 709.9 %reduce-scatter.14.cloned.1.call-done = f32[256,2048]{1,0:T(8,128)} async-done(((f32[8192,2048]{1,0:T(8,128)}), f32[256,2048]{1,0:T(8,128)}) %reduce-scatter.14.cloned.1.call-update) | async-done | bytes 2097168 | tf_op jit(solution)/shard_map/reduce_scatter | solution.py:190
  (234 shorter events, 85.1 us)
Async XLA Ops:
  7.2 69.3 %all-gather.10.cloned.1.call-start = ((), (), s32[]{:S(2)}) async-start(), calls=%async_computation.5 | async-start | bytes 4325376 | tf_op jit(solution)/shard_map/all_gather | solution.py:85
  8.9 131.9 %all-gather.14.cloned.1.call-start = ((), (), s32[]{:S(2)}) async-start(), calls=%async_computation.7 | async-start | bytes 4325376 | tf_op jit(solution)/shard_map/all_gather | solution.py:84
  10.6 160.1 %all-gather.12.cloned.1.call-start = ((), (), s32[]{:S(2)}) async-start(), calls=%async_computation.6 | async-start | bytes 2359296 | tf_op jit(solution)/shard_map/all_gather | solution.py:139
  54.6 240.9 %copy-start.22 = (f32[2048]{0:T(1024)}, f32[2048]{0:T(1024)S(1)}, u32[]{:S(2)}) copy-start(f32[2048]{0:T(1024)S(1)} %convert_element_type.151) | copy-start | bytes 24580
  55.8 239.6 %copy-start.25 = (f32[128]{0:T(128)}, f32[128]{0:T(128)S(1)}, u32[]{:S(2)}) copy-start(f32[128]{0:T(128)S(1)} %add_rsqrt_fusion.1) | copy-start | bytes 1540
  80.4 122.7 %all-gather.16.cloned.1.call-start = ((), (), s32[]{:S(2)}) async-start(), calls=%async_computation.8 | async-start | bytes 2359296 | tf_op jit(solution)/shard_map/all_gather | solution.py:138
  80.8 221.2 %copy-start.17 = (f32[128,128]{1,0:T(8,128)}, f32[128,128]{1,0:T(8,128)S(1)}, u32[]{:S(2)}) copy-start(f32[128,128]{1,0:T(8,128)S(1)} %get-tuple-element.220) | copy-start | bytes 196612
  80.8 221.2 %copy-start.19 = (f32[128,128]{1,0:T(8,128)}, f32[128,128]{1,0:T(8,128)S(1)}, u32[]{:S(2)}) copy-start(f32[128,128]{1,0:T(8,128)S(1)} %get-tuple-element.221) | copy-start | bytes 196612
  140.8 6.6 copy-start
  147.4 8.7 copy-start.13
  152.3 130.6 %all-gather.18.cloned.1.call-start = ((), (), s32[]{:S(2)}) async-start(), calls=%async_computation.9 | async-start | bytes 8650752 | tf_op jit(solution)/shard_map/all_gather | solution.py:83
  154.2 208.1 %all-gather.20.cloned.1.call-start = ((), (), s32[]{:S(2)}) async-start(), calls=%async_computation.10 | async-start | bytes 8650752 | tf_op jit(solution)/shard_map/all_gather | solution.py:86
  156.0 403.2 %all-gather.24.cloned.1.call-start = ((), (), s32[]{:S(2)}) async-start(), calls=%async_computation.12 | async-start | bytes 34603008 | tf_op jit(solution)/shard_map/all_gather | solution.py:162
  157.2 3.0 copy-start.14
  157.2 598.6 %all-gather.22.cloned.1.call-start = ((), (), s32[]{:S(2)}) async-start(), calls=%async_computation.11 | async-start | bytes 34603008 | tf_op jit(solution)/shard_map/all_gather | solution.py:161
  160.1 791.7 %all-gather.26.cloned.1.call-start = ((), (), s32[]{:S(2)}) async-start(), calls=%async_computation.13 | async-start | bytes 34603008 | tf_op jit(solution)/shard_map/all_gather | solution.py:163
  161.3 973.4 %reduce-scatter.16.cloned.1.call-start = ((), (), s32[]{:S(2)}) async-start(), calls=%async_computation.17 | async-start | bytes 2359296
  295.5 6.7 copy-start.15
  302.2 2.1 copy-start.16
  367.2 640.4 %copy-start.2 = (f32[128,2048]{1,0:T(8,128)}, f32[128,2048]{1,0:T(8,128)S(1)}, u32[]{:S(2)}) copy-start(f32[128,2048]{1,0:T(8,128)S(1)} %get-tuple-element.227) | copy-start | bytes 3145732
  367.4 388.4 %copy-start.8 = (bf16[128,2048]{1,0:T(8,128)(2,1)}, bf16[128,2048]{1,0:T(8,128)(2,1)S(1)}, u32[]{:S(2)}) copy-start(bf16[128,2048]{1,0:T(8,128)(2,1)S(1)} %multiply_convert_fusion.4) | copy-start | bytes 1572868
  989.0 18.5 copy-start.11
  1009.1 1.0 copy-start.5
  1081.4 70.8 %reduce-scatter.18.cloned.1.call-start = ((), (), s32[]{:S(2)}) async-start(), calls=%async_computation.18 | async-start | bytes 2359296
  1084.7 2.0 copy-start.9
  1086.6 1949.2 %all-reduce.9.cloned.1.call-start = ((), (), s32[]{:S(2)}) async-start(), calls=%async_computation.19 | async-start | bytes 268435456
  1133.3 0.8 copy-start.18
  1133.3 0.9 copy-start.20
  1133.3 2265.2 %reduce-scatter.10.cloned.1.call-start = ((), (), s32[]{:S(2)}) async-start(), calls=%async_computation.14 | async-start | bytes 34603008 | tf_op jit(solution)/shard_map/reduce_scatter | solution.py:314
  1134.2 19.2 copy-start.1
  1134.2 19.2 copy-start.23
  1134.2 19.2 copy-start.26
  1168.9 1.2 copy-start.6
  1168.9 1.4 copy-start.10
  1168.9 2415.5 %reduce-scatter.12.cloned.1.call-start = ((), (), s32[]{:S(2)}) async-start(), calls=%async_computation.15 | async-start | bytes 17301504 | tf_op jit(solution)/shard_map/reduce_scatter | solution.py:228
  1178.4 1.1 copy-start.12
  1178.4 3116.0 %reduce-scatter.14.cloned.1.call-start = ((), (), s32[]{:S(2)}) async-start(), calls=%async_computation.16 | async-start | bytes 69206016 | tf_op jit(solution)/shard_map/reduce_scatter | solution.py:190
  1205.4 6.6 copy-start.3
  1212.0 18.3 copy-start.7
  1230.3 2.3 copy-start.4
  1230.3 2.3 copy-start.21
  1232.6 1.7 copy-start.24
Sparse Core Ops, SparseCore 0:
  11.6 64.8 all-gather.9
  80.1 60.6 all-gather.13
  143.0 27.6 all-gather.11
  172.7 30.3 all-gather.15
  206.5 76.4 all-gather.17
  286.4 75.8 all-gather.19
  365.8 193.3 all-gather.23
  562.8 192.9 all-gather.21
  758.8 192.9 all-gather.25
  1081.6 33.9 reduce-scatter.15
  1117.9 34.3 reduce-scatter.17
  1158.5 1877.2 all-reduce.8
  3038.1 360.4 reduce-scatter.9
  3401.3 183.1 reduce-scatter.11
  3587.2 707.1 reduce-scatter.13
where the time goes:
time: 4310 us; the launch traced here: 4300 us
  waiting for transfers between devices  3820 us (89%)
  matrix products  269 us (6%)
  blocking collectives  81.8 us (2%)
  local copies, waits for them, and re-layouts  79.1 us (2%)
    unnamed x18, waiting for transfers between devices  1780 us
    reduce_scatter x1, waiting for transfers between devices, local(): lax.psum_scatter(column_product(hidden, d_out), ('dp', 'ctx'), scatter_di...  710 us
    reduce_scatter x1, waiting for transfers between devices, local(): lax.psum_scatter(column_product(first_normalized, d_projected), ('dp', 'c...  358 us
    all_gather x1, waiting for transfers between devices, local(): lax.all_gather(w_up.astype(narrow_number_type), ('dp', 'ctx'), axis=0, ti...  192 us
    reduce_scatter x1, waiting for transfers between devices, local(): lax.psum_scatter(column_product(attn_out, d_branch), ('dp', 'ctx'), scatt...  182 us
    all_gather x1, waiting for transfers between devices, local(): lax.all_gather(w_gate.astype(narrow_number_type), ('dp', 'ctx'), axis=0,...  179 us
    all_gather x1, waiting for transfers between devices, local(): lax.all_gather(w_down.astype(narrow_number_type), ('dp', 'ctx'), axis=0,...  178 us
    dot_general x4, matrix products, column_product(): jnp.einsum('bd,bf->df', left, right, preferred_element_type=jnp.float32)  96.2 us
  transfers between devices with their start and end apart: 15, of which 14 were waited for; matrix products, arithmetic and copies ran while one was open for 6% of the time, Pallas kernels for 0%

commit v1 on v0

--- a/solution.py
+++ b/solution.py
@@ -55,7 +55,7 @@
     return jnp.einsum("bd,bf->df", left, right, preferred_element_type=jnp.float32)
 
 
-def local(
+def gathered_local(
     layer_input,
     cotangent,
     prefix,
@@ -355,8 +355,209 @@
         mlp_gain_sum,
     )
 
+def swap_cores(values):
+    size = lax.axis_size("ctx")
+    return lax.ppermute(values, "ctx", [(i, i ^ 1) for i in range(size)])
+
+
+def gather_ctx(rows):
+    return lax.all_gather(rows, "ctx", axis=0, tiled=True)
+
+
+def scatter_ctx(partial):
+    return lax.psum_scatter(partial, "ctx", scatter_dimension=0, tiled=True).astype(jnp.float32)
+
+
+def gather_dp(rows):
+    return lax.all_gather(rows, "dp", axis=0, tiled=True)
+
+
+def scatter_dp(partial):
+    return lax.psum_scatter(partial, "dp", scatter_dimension=0, tiled=True)
+
+
+def exchange_ctx(blocks):
+    return lax.all_to_all(blocks, "ctx", 0, 0, tiled=True)
+
+
+def out_weight_moves(n_dp, n_ctx):
+    per_head = n_dp * n_ctx // QUERY_HEADS
+    moves = []
+    for block in range(n_dp * n_ctx):
+        head, part = divmod(block, per_head)
+        moves.append((block, part * n_ctx + head))
+    return moves
+
+
+def head_local(
+    layer_input,
+    cotangent,
+    prefix,
+    w_query,
+    key_weight,
+    value_weight,
+    w_out,
+    w_gate,
+    w_up,
+    w_down,
+    attention_norm_gain,
+    feedforward_norm_gain,
+):
+    low = jnp.bfloat16
+    wide = jnp.float32
+    n_dp = lax.axis_size("dp")
+    n_ctx = lax.axis_size("ctx")
+    core = lax.axis_index("ctx") % 2
+    rows = w_query.shape[0]
+    seq_rows = layer_input.shape[1] * n_ctx
+    ff_part = w_down.shape[0]
+
+    def dot(left, right):
+        return jnp.dot(left, right, preferred_element_type=wide)
+
+    def dot_t(left, right):
+        return lax.dot_general(left, right, (((1,), (1,)), ((), ())), preferred_element_type=wide)
+
+    def t_dot(left, right):
+        return lax.dot_general(left, right, (((0,), (0,)), ((), ())), preferred_element_type=wide)
+
+    def lowered(weight):
+        return weight.astype(low).astype(wide)
+
+    x_rows = layer_input[0].astype(wide)
+    d_out = cotangent[0]
+    gain_a = lowered(attention_norm_gain)[:, None]
+    gain_m = lowered(feedforward_norm_gain)[:, None]
+    low_q, low_k, low_v = lowered(w_query), lowered(key_weight), lowered(value_weight)
+    low_g, low_u = lowered(w_gate), lowered(w_up)
+
+    inverse1 = lax.rsqrt(jnp.mean(x_rows * x_rows, axis=-1, keepdims=True) + NORM_EPSILON)
+    hat1 = x_rows * inverse1
+    all_hat1 = gather_ctx(hat1.astype(low))
+
+    q_cols = (low_q * gain_a).astype(low).reshape(rows, n_ctx, 1, HEAD_SIZE)
+    k_cols = (low_k * gain_a).astype(low).reshape(rows, n_ctx // 2, 1, 1, HEAD_SIZE)
+    v_cols = (low_v * gain_a).astype(low).reshape(rows, n_ctx // 2, 1, 1, HEAD_SIZE)
+    kv_cols = jnp.concatenate([k_cols, v_cols], axis=2).reshape(rows, n_ctx, 1, HEAD_SIZE)
+    proj = jnp.concatenate([q_cols, kv_cols], axis=2).reshape(rows, n_ctx, 2 * HEAD_SIZE)
+    proj = exchange_ctx(proj.transpose(1, 0, 2)).reshape(n_ctx * rows, 2 * HEAD_SIZE)
+    proj = gather_dp(proj)
+    moves = out_weight_moves(n_dp, n_ctx)
+    out_w = gather_dp(lax.ppermute(w_out.astype(low), ("dp", "ctx"), moves))
+
+    def ff_columns(weight):
+        blocks = (weight * gain_m).astype(low).reshape(rows, n_dp, n_ctx, ff_part)
+        return blocks.transpose(2, 0, 1, 3).reshape(n_ctx, rows, n_dp * ff_part)
+
+    gate_up = jnp.concatenate([ff_columns(low_g), ff_columns(low_u)], axis=2)
+    gate_up = exchange_ctx(gate_up).reshape(n_ctx * rows, 2 * n_dp * ff_part)
+    gate_up_w = gather_dp(gate_up)
+    down_w = gather_dp(w_down.astype(low))
+    all_cot = gather_ctx(d_out)
+
+    positions = jnp.arange(seq_rows, dtype=jnp.int32)
+    cosine, sine = rope_angles(positions, HEAD_SIZE)
+    cosine, sine = cosine[:, 0], sine[:, 0]
+    half = HEAD_SIZE // 2
+
+    def rotate(v, turn):
+        a, b = v[:, :half], v[:, half:]
+        return jnp.concatenate([a * cosine - turn * b * sine, b * cosine + turn * a * sine], axis=1)
+
+    qkv = dot(all_hat1, proj)
+    scale = HEAD_SIZE ** (-0.5)
+    q_rot = (rotate(qkv[:, :HEAD_SIZE], 1.0) * scale).astype(low)
+    own = qkv[:, HEAD_SIZE:]
+    own = jnp.where(core == 0, rotate(own, 1.0), own).astype(low)
+    other = swap_cores(own)
+    keys = jnp.where(core == 0, own, other)
+    values = jnp.where(core == 0, other, own)
+    allowed = (positions[None, :] <= positions[:, None]) | (positions[None, :] < prefix[0])
+    scores = jnp.where(allowed, dot_t(q_rot, keys), -1e30)
+    peak = jnp.max(scores, axis=-1, keepdims=True)
+    weights = jnp.exp(scores - peak)
+    total = jnp.sum(weights, axis=-1, keepdims=True)
+    attended = dot(weights.astype(low), values) / total
+    attn = attended.astype(low)
+    middle = x_rows + scatter_ctx(dot(attn, out_w).astype(low))
+
+    inverse2 = lax.rsqrt(jnp.mean(middle * middle, axis=-1, keepdims=True) + NORM_EPSILON)
+    hat2 = middle * inverse2
+    all_hat2 = gather_ctx(hat2.astype(low))
+    width = n_dp * ff_part
+    gate = dot(all_hat2, gate_up_w[:, :width])
+    up = dot(all_hat2, gate_up_w[:, width:])
+    sig = jax.nn.sigmoid(gate)
+    silu = gate * sig
+    hidden = (silu * up).astype(low)
+    output = (middle + scatter_ctx(dot(hidden, down_w).astype(low))).astype(low)[None]
+
+    d_hidden = dot_t(all_cot, down_w)
+    d_gate = (d_hidden * up * sig * (1.0 + gate * (1.0 - sig))).astype(low)
+    d_up = (d_hidden * silu).astype(low)
+    d_gate_up = jnp.concatenate([d_gate, d_up], axis=1)
+    e2 = scatter_ctx(dot_t(d_gate_up, gate_up_w).astype(low))
+    down_sum = scatter_dp(t_dot(hidden, all_cot).astype(low)).astype(wide)
+    gate_up_sum = scatter_dp(t_dot(all_hat2, d_gate_up).astype(low))
+    gate_up_sum = exchange_ctx(gate_up_sum.reshape(n_ctx, rows, 2 * width)).astype(wide)
+
+    def ff_rows(part):
+        blocks = part.reshape(n_ctx, rows, n_dp, ff_part).transpose(1, 2, 0, 3)
+        return blocks.reshape(rows, n_dp * n_ctx * ff_part)
+
+    raw_gate = ff_rows(gate_up_sum[:, :, :width])
+    raw_up = ff_rows(gate_up_sum[:, :, width:])
+    gain_mlp = jnp.sum(raw_gate * low_g, axis=1) + jnp.sum(raw_up * low_u, axis=1)
+    gate_sum, up_sum = raw_gate * gain_m, raw_up * gain_m
+    d_middle = d_out.astype(wide) + inverse2 * (
+        e2 - hat2 * jnp.mean(e2 * hat2, axis=-1, keepdims=True)
+    )
+
+    all_branch = gather_ctx(d_middle.astype(low))
+    out_sum = scatter_dp(t_dot(attn, all_branch).astype(low))
+    out_sum = lax.ppermute(out_sum, ("dp", "ctx"), [(b, a) for a, b in moves]).astype(wide)
+    d_attn = dot_t(all_branch, out_w).astype(low)
+    delta = jnp.sum(d_attn.astype(wide) * attended, axis=-1, keepdims=True)
+    probs = weights / total
+    d_scores = (probs * (dot_t(d_attn, values) - delta)).astype(low)
+    d_query = rotate(dot(d_scores, keys) * scale, -1.0)
+    dk_part = t_dot(d_scores, q_rot)
+    dv_part = t_dot(probs.astype(low), d_attn)
+    mine = jnp.where(core == 0, dk_part, dv_part)
+    mine = mine + swap_cores(jnp.where(core == 0, dv_part, dk_part).astype(low)).astype(wide)
+    mine = jnp.where(core == 0, rotate(mine, -1.0), mine)
+    d_proj = jnp.concatenate([d_query, mine], axis=1).astype(low)
+    e1 = scatter_ctx(dot_t(d_proj, proj).astype(low))
+    proj_sum = scatter_dp(t_dot(all_hat1, d_proj).astype(low))
+    proj_sum = exchange_ctx(proj_sum.reshape(n_ctx, rows, 2 * HEAD_SIZE)).astype(wide)
+    proj_sum = proj_sum.transpose(1, 0, 2)
+    raw_q = proj_sum[:, :, :HEAD_SIZE].reshape(rows, n_ctx * HEAD_SIZE)
+    kv_sum = proj_sum[:, :, HEAD_SIZE:].reshape(rows, n_ctx // 2, 2, HEAD_SIZE)
+    raw_k = kv_sum[:, :, 0].reshape(rows, n_ctx // 2 * HEAD_SIZE)
+    raw_v = kv_sum[:, :, 1].reshape(rows, n_ctx // 2 * HEAD_SIZE)
+    gain_attn = (
+        jnp.sum(raw_q * low_q, axis=1)
+        + jnp.sum(raw_k * low_k, axis=1)
+        + jnp.sum(raw_v * low_v, axis=1)
+    )
+    d_input = d_middle + inverse1 * (e1 - hat1 * jnp.mean(e1 * hat1, axis=-1, keepdims=True))
+    return (
+        output,
+        d_input.astype(low)[None],
+        raw_q * gain_a,
+        raw_k * gain_a,
+        raw_v * gain_a,
+        out_sum,
+        gate_sum,
+        up_sum,
+        down_sum,
+        gain_attn,
+        gain_mlp,
+    )
+
 
 def solution(mesh):
+    local = head_local if mesh.shape["ctx"] == QUERY_HEADS else gathered_local
     in_specs = (
         P("dp", "ctx", None),
         P("dp", "ctx", None),

time: 4310 us -> 965 us (0.22)
  waiting for transfers between devices: 3820 us -> 643 us
  matrix products: 269 us -> 114 us
  local copies, waits for them, and re-layouts: 79.1 us -> 25.6 us
    unnamed x18 -> x16, waiting for transfers between devices: 1780 us -> 0.77 us
    reduce_scatter x3 -> x8, waiting for transfers between devices: 1250 us -> 253 us  [the longest x4 129 us: scatter_dp(): return lax.psum_scatter(partial, 'dp', scatter_dimension=0, tiled=True)]
    all_gather x9 -> x8, waiting for transfers between devices: 794 us -> 365 us  [the longest x4 187 us: gather_dp(): return lax.all_gather(rows, 'dp', axis=0, tiled=True)]
    dot_general x60 -> x19, matrix products: 269 us -> 114 us  [the longest x7 41.9 us: dot(): return jnp.dot(left, right, preferred_element_type=wide)]
    all_to_all x0 -> x2, blocking collectives: none -> 101 us  [exchange_ctx(): return lax.all_to_all(blocks, 'ctx', 0, 0, tiled=True)]
    unnamed x2 -> x0, blocking collectives: 81.8 us -> none
  transfers between devices with their start and end apart: 15 -> 22, of which waited for: 14 -> 16; matrix products, arithmetic and copies ran while one was open for 6% -> 14% of each run, Pallas kernels for 0% -> 0%
where the time goes in v1:
time: 965 us; the launch traced here: 956 us
  waiting for transfers between devices  643 us (67%)
  matrix products  114 us (12%)
  blocking collectives  101 us (10%)
  other arithmetic  44.1 us (5%)
  local copies, waits for them, and re-layouts  25.6 us (3%)
  between operations  15.8 us (2%)
  starting transfers between devices  13.4 us (1%)
    all_gather x4, waiting for transfers between devices, gather_dp(): return lax.all_gather(rows, 'dp', axis=0, tiled=True)  187 us
    all_gather x4, waiting for transfers between devices, gather_ctx(): return lax.all_gather(rows, 'ctx', axis=0, tiled=True)  178 us
    reduce_scatter x4, waiting for transfers between devices, scatter_dp(): return lax.psum_scatter(partial, 'dp', scatter_dimension=0, tiled=True)  129 us
    reduce_scatter x4, waiting for transfers between devices, scatter_ctx(): lax.psum_scatter(partial, 'ctx', scatter_dimension=0, tiled=True)  124 us
    all_to_all x2, blocking collectives, exchange_ctx(): return lax.all_to_all(blocks, 'ctx', 0, 0, tiled=True)  101 us
    dot_general x7, matrix products, dot(): return jnp.dot(left, right, preferred_element_type=wide)  41.9 us
    dot_general x6, matrix products, dot_t(): lax.dot_general(left, right, (((1,), (1,)), ((), ())), preferred_element_...  35.9 us
    dot_general x6, matrix products, t_dot(): lax.dot_general(left, right, (((0,), (0,)), ((), ())), preferred_element_...  35.7 us
  transfers between devices with their start and end apart: 22, of which 16 were waited for; matrix products, arithmetic and copies ran while one was open for 14% of the time, Pallas kernels for 0%

profile of v1, /device:TPU:0, one launch (start us, length us, event | category | flops | bytes accessed | tf_op | source)
XLA Modules:
  0.0 956.1 jit_solution(12153881004574561478)
XLA Ops:
  11.1 21.6 %all_to_all.20 = bf16[8,64,512]{2,1,0:T(8,128)(2,1)} all-to-all(bf16[8,64,512]{2,1,0:T(8,128)(2,1)S(1)} %copy.54), channel_id=1, replica_groups=mesh['dp'=4,'ctx'=8] {'ctx'}, dimensions={0} | all-to-all | bytes 1048576 | tf_op jit(solution)/shard_map/all_to_all | solution.py:380
  36.0 37.5 %all-gather.12.cloned.1.call-done = bf16[2048,512]{1,0:T(8,128)(2,1)} async-done(((bf16[512,512]{1,0:T(8,128)(2,1)}), bf16[2048,512]{1,0:T(8,128)(2,1)}) %all-gather.12.cloned.1.call-update) | async-done | bytes 2097168 | tf_op jit(solution)/shard_map/all_gather | solution.py:372
  73.4 49.3 %all-gather.10.cloned.1.call-done = bf16[1024,2048]{1,0:T(8,128)(2,1)} async-done(((bf16[128,2048]{1,0:T(8,128)(2,1)}), bf16[1024,2048]{1,0:T(8,128)(2,1)}) %all-gather.10.cloned.1.call-update) | async-done | bytes 4194320 | tf_op jit(solution)/shard_map/all_gather | solution.py:364
  122.8 5.2 fusion.95
  128.0 2.3 fusion.62
  136.6 2.3 fusion.26
  138.9 18.0 %all-gather.14.cloned.1.call-done = bf16[256,2048]{1,0:T(8,128)(2,1)} async-done(((bf16[64,2048]{1,0:T(8,128)(2,1)}), bf16[256,2048]{1,0:T(8,128)(2,1)}) %all-gather.14.cloned.1.call-update) | async-done | bytes 1048592 | tf_op jit(solution)/shard_map/all_gather | solution.py:372
  157.0 4.6 convolution_convert_fusion.3
  161.6 2.9 convert_element_type.242
  165.4 2.9 fusion.15
  174.1 79.0 %all_to_all.21 = bf16[8,64,2048]{2,1,0:T(8,128)(2,1)} all-to-all(bf16[8,64,2048]{2,1,0:T(8,128)(2,1)S(1)} %pad_maximum_fusion.3), channel_id=1, replica_groups=mesh['dp'=4,'ctx'=8] {'ctx'}, dimensions={0} | all-to-all | bytes 4194304 | tf_op jit(solution)/shard_map/all_to_all | solution.py:380
  256.6 53.1 %all-gather.20.cloned.1.call-done = bf16[1024,2048]{1,0:T(8,128)(2,1)} async-done(((bf16[256,2048]{1,0:T(8,128)(2,1)}), bf16[1024,2048]{1,0:T(8,128)(2,1)}) %all-gather.20.cloned.1.call-update) | async-done | bytes 4194320 | tf_op jit(solution)/shard_map/all_gather | solution.py:372
  309.7 48.6 %all-gather.24.cloned.1.call-done = bf16[1,1024,2048]{2,1,0:T(8,128)(2,1)} async-done(((bf16[1,128,2048]{2,1,0:T(8,128)(2,1)}), bf16[1,1024,2048]{2,1,0:T(8,128)(2,1)}) %all-gather.24.cloned.1.call-update) | async-done | bytes 4194320 | tf_op jit(solution)/shard_map/all_gather | solution.py:364
  358.3 10.1 %fusion.6 = f32[1024,1024]{0,1:T(8,128)} fusion(bf16[1024,2048]{1,0:T(8,128)(2,1)} %all-gather.20.cloned.1.call-done, bf16[1,1024,2048]{2,1,0:T(8,128)(2,1)} %all-gather.24.cloned.1.call-done), kind=kOutput, calls=%fused_computation.8 | convolution fusion | flops 4294967296 | bytes 12582912 | tf_op jit(solution)/shard_map/dot_general | solution.py:419
  368.4 78.1 %all-gather.18.cloned.1.call-done = bf16[2048,2048]{1,0:T(8,128)(2,1)} async-done(((bf16[512,2048]{1,0:T(8,128)(2,1)}), bf16[2048,2048]{1,0:T(8,128)(2,1)}) %all-gather.18.cloned.1.call-update) | async-done | bytes 8388624 | tf_op jit(solution)/shard_map/all_gather | solution.py:372
  446.5 49.4 %all-gather.16.cloned.1.call-done = bf16[1024,2048]{1,0:T(8,128)(2,1)} async-done(((bf16[128,2048]{1,0:T(8,128)(2,1)}), bf16[1024,2048]{1,0:T(8,128)(2,1)}) %all-gather.16.cloned.1.call-update) | async-done | bytes 4194320 | tf_op jit(solution)/shard_map/all_gather | solution.py:364
  495.9 10.2 %fusion = f32[1024,1024]{0,1:T(8,128)} fusion(bf16[1024,2048]{1,0:T(8,128)(2,1)} %all-gather.16.cloned.1.call-done, bf16[2048,2048]{1,0:T(8,128)(2,1)} %all-gather.18.cloned.1.call-done), kind=kOutput, calls=%fused_computation.1 | convolution fusion | flops 4294967296 | bytes 12582912 | tf_op jit(solution)/shard_map/dot_general | solution.py:416
  506.1 10.2 %multiply_convert_fusion.2 = (bf16[1024,1024]{0,1:T(8,128)(2,1)}, bf16[1024,1024]{0,1:T(8,128)(2,1)}, bf16[1024,1024]{0,1:T(8,128)(2,1)}) fusion(f32[1024,1024]{0,1:T(8,128)S(1)} %copy-done.37, f32[1024,1024]{0,1:T(8,128)} %fusion, bf16[1024,2048]{1,0:T(8,128)(2,1)S(1)} %copy-done.31, bf16[2048,2048]{1,0:T(8,128)(2,1)S(1)} %copy-done.29), kind=kOutput, calls=%fused_computation.12 | convolution fusion | flops 4310695936 | bytes 23068672 | tf_op jit(solution)/shard_map/dot_general | solution.py:416
  516.4 12.0 %convolution_convert_fusion.2 = bf16[1024,2048]{1,0:T(8,128)(2,1)} fusion(bf16[2048,2048]{1,0:T(8,128)(2,1)S(1)} %copy-done.29, bf16[1024,1024]{0,1:T(8,128)(2,1)} %get-tuple-element.12, bf16[1024,1024]{0,1:T(8,128)(2,1)} %get-tuple-element.11), kind=kOutput, calls=%fused_computation.21 | convolution fusion | flops 8600420352 | bytes 16777216 | tf_op jit(solution)/shard_map/dot_general | solution.py:419
  528.5 48.8 %reduce-scatter.13.cloned.1.call-done = bf16[128,2048]{1,0:T(8,128)(2,1)} async-done(((bf16[1024,2048]{1,0:T(8,128)(2,1)}), bf16[128,2048]{1,0:T(8,128)(2,1)}) %reduce-scatter.13.cloned.1.call-update) | async-done | bytes 524304 | tf_op jit(solution)/shard_map/reduce_scatter | solution.py:368
  578.7 2.3 fusion.90
  581.0 14.2 %convolution_convert_fusion = bf16[2048,2048]{1,0:T(8,128)(2,1)} fusion(bf16[1024,2048]{1,0:T(8,128)(2,1)} %all-gather.16.cloned.1.call-done, bf16[1024,1024]{0,1:T(8,128)(2,1)} %get-tuple-element.12, bf16[1024,1024]{0,1:T(8,128)(2,1)} %get-tuple-element.11), kind=kOutput, calls=%fused_computation | convolution fusion | flops 8602517504 | bytes 16777216 | tf_op jit(solution)/shard_map/dot_general | solution.py:422
  595.3 31.1 %all-gather.22.cloned.1.call-done = bf16[1024,2048]{1,0:T(8,128)(2,1)} async-done(((bf16[128,2048]{1,0:T(8,128)(2,1)}), bf16[1024,2048]{1,0:T(8,128)(2,1)}) %all-gather.22.cloned.1.call-update) | async-done | bytes 4194320 | tf_op jit(solution)/shard_map/all_gather | solution.py:364
  626.4 3.9 multiply_reduce_fusion
  630.4 2.8 multiply_convert_fusion
  637.3 2.3 convolution_convert_fusion.6
  639.7 4.0 select_convert_fusion
  644.6 2.5 fusion.65
  647.4 2.3 fusion.68
  649.9 3.8 convolution_convert_fusion.5
  653.8 9.7 %fusion.11 = bf16[1024,2048]{1,0:T(8,128)(2,1)} fusion(bf16[1024,1024]{0,1:T(8,128)(2,1)} %get-tuple-element.13, bf16[1,1024,2048]{2,1,0:T(8,128)(2,1)} %all-gather.24.cloned.1.call-done), kind=kOutput, calls=%fused_computation.23 | convolution fusion | flops 4297064448 | bytes 10485760 | tf_op jit(solution)/shard_map/dot_general | solution.py:422
  663.5 6.1 convolution_convert_fusion.1
  671.3 8.6 convolution_convert_fusion.4
  679.9 34.8 %reduce-scatter.21.cloned.1.call-done = bf16[512,2048]{1,0:T(8,128)(2,1)} async-done(((bf16[2048,2048]{1,0:T(8,128)(2,1)}), bf16[512,2048]{1,0:T(8,128)(2,1)}) %reduce-scatter.21.cloned.1.call-update) | async-done | bytes 2097168 | tf_op jit(solution)/shard_map/reduce_scatter | solution.py:376
  714.6 4.6 all-to-all-start.3
  719.3 26.1 %reduce-scatter.19.cloned.1.call-done = bf16[64,2048]{1,0:T(8,128)(2,1)} async-done(((bf16[256,2048]{1,0:T(8,128)(2,1)}), bf16[64,2048]{1,0:T(8,128)(2,1)}) %reduce-scatter.19.cloned.1.call-update) | async-done | bytes 262160 | tf_op jit(solution)/shard_map/reduce_scatter | solution.py:376
  747.0 24.1 %all-to-all-done.3 = bf16[8,64,2048]{2,1,0:T(8,128)(2,1)S(1)} async-done(((bf16[8,64,2048]{2,1,0:T(8,128)(2,1)}), bf16[8,64,2048]{2,1,0:T(8,128)(2,1)S(1)}, u32[]{:S(2)}, u32[]{:S(2)}) %all-to-all-start.3) | async-done | bytes 2097184 | tf_op jit(solution)/shard_map/all_to_all | solution.py:380
  771.1 16.8 %reduce-scatter.17.cloned.1.call-done = bf16[512,512]{1,0:T(8,128)(2,1)} async-done(((bf16[2048,512]{1,0:T(8,128)(2,1)}), bf16[512,512]{1,0:T(8,128)(2,1)}) %reduce-scatter.17.cloned.1.call-update) | async-done | bytes 524304 | tf_op jit(solution)/shard_map/reduce_scatter | solution.py:376
  787.9 4.6 all-to-all-start.2
  792.5 51.2 %reduce-scatter.23.cloned.1.call-done = bf16[256,2048]{1,0:T(8,128)(2,1)} async-done(((bf16[1024,2048]{1,0:T(8,128)(2,1)}), bf16[256,2048]{1,0:T(8,128)(2,1)}) %reduce-scatter.23.cloned.1.call-update) | async-done | bytes 1048592 | tf_op jit(solution)/shard_map/reduce_scatter | solution.py:376
  843.7 2.8 convert_element_type.267
  847.3 2.5 fusion.92
  854.4 3.2 reshape.140
  857.6 3.0 copy.61
  861.8 2.8 fusion.16
  869.6 26.3 %reduce-scatter.15.cloned.1.call-done = bf16[128,2048]{1,0:T(8,128)(2,1)} async-done(((bf16[1024,2048]{1,0:T(8,128)(2,1)}), bf16[128,2048]{1,0:T(8,128)(2,1)}) %reduce-scatter.15.cloned.1.call-update) | async-done | bytes 524304 | tf_op jit(solution)/shard_map/reduce_scatter | solution.py:368
  897.3 48.9 %reduce-scatter.11.cloned.1.call-done = bf16[128,2048]{1,0:T(8,128)(2,1)} async-done(((bf16[1024,2048]{1,0:T(8,128)(2,1)}), bf16[128,2048]{1,0:T(8,128)(2,1)}) %reduce-scatter.11.cloned.1.call-update) | async-done | bytes 524304 | tf_op jit(solution)/shard_map/reduce_scatter | solution.py:368
  946.2 3.0 fusion.71
  (177 shorter events, 45.9 us)
Async XLA Ops:
  7.2 66.3 %all-gather.12.cloned.1.call-start = ((), (), s32[]{:S(2)}) async-start(), calls=%async_computation.13 | async-start | bytes 2621440 | tf_op jit(solution)/shard_map/all_gather | solution.py:372
  9.0 23.8 %copy-start = (bf16[1,128,2048]{2,1,0:T(8,128)(2,1)S(1)}, bf16[1,128,2048]{2,1,0:T(8,128)(2,1)}, u32[]{:S(2)}) copy-start(bf16[1,128,2048]{2,1,0:T(8,128)(2,1)} %param.12) | copy-start | bytes 1572868
  10.4 24.1 %copy-start.24 = (f32[64,2048]{1,0:T(8,128)S(1)}, f32[64,2048]{1,0:T(8,128)}, u32[]{:S(2)}) copy-start(f32[64,2048]{1,0:T(8,128)} %param.18) | copy-start | bytes 1572868
  32.7 90.1 %all-gather.10.cloned.1.call-start = ((), (), s32[]{:S(2)}) async-start(), calls=%async_computation.12 | async-start | bytes 4718592 | tf_op jit(solution)/shard_map/all_gather | solution.py:364
  34.5 122.5 %all-gather.14.cloned.1.call-start = ((), (), s32[]{:S(2)}) async-start(), calls=%async_computation.14 | async-start | bytes 1310720 | tf_op jit(solution)/shard_map/all_gather | solution.py:372
  34.6 96.9 %collective-permute-start.1 = (bf16[64,2048]{1,0:T(8,128)(2,1)S(1)}, bf16[64,2048]{1,0:T(8,128)(2,1)}, u32[]{:S(2)}, u32[]{:S(2)}) collective-permute-start(bf16[64,2048]{1,0:T(8,128)(2,1)S(1)} %convert_element_type.229), channel_id=1, source_target_pairs={{0,0},{1,8},{2,16},{3,24},{4,1},{5,9},{6,17},{7,25},{8,2},{9,10},{... | collective-permute-start | bytes 786440 | tf_op jit(solution)/shard_map/ppermute | solution.py:446
  130.5 3.2 collective-permute-start
  131.5 121.7 %reduce-scatter.9.cloned.1.call-start = ((), (), s32[]{:S(2)}) async-start(), calls=%async_computation.15 | async-start | bytes 4718592 | tf_op jit(solution)/shard_map/reduce_scatter | solution.py:368
  138.9 22.6 %copy-start.12 = (f32[1024,256]{0,1:T(8,128)}, f32[1024,256]{0,1:T(8,128)S(1)}, u32[]{:S(2)}) copy-start(f32[1024,256]{0,1:T(8,128)S(1)} %fusion.26) | copy-start | bytes 3145732
  161.5 3.8 copy-start.33
  161.5 3.8 copy-start.2
  161.6 148.1 %all-gather.20.cloned.1.call-start = ((), (), s32[]{:S(2)}) async-start(), calls=%async_computation.18 | async-start | bytes 5242880 | tf_op jit(solution)/shard_map/all_gather | solution.py:372
  164.5 193.8 %all-gather.24.cloned.1.call-start = ((), (), s32[]{:S(2)}) async-start(), calls=%async_computation.27 | async-start | bytes 4718592 | tf_op jit(solution)/shard_map/all_gather | solution.py:364
  165.1 281.5 %all-gather.18.cloned.1.call-start = ((), (), s32[]{:S(2)}) async-start(), calls=%async_computation.17 | async-start | bytes 10485760 | tf_op jit(solution)/shard_map/all_gather | solution.py:372
  253.1 242.8 %all-gather.16.cloned.1.call-start = ((), (), s32[]{:S(2)}) async-start(), calls=%async_computation.16 | async-start | bytes 4718592 | tf_op jit(solution)/shard_map/all_gather | solution.py:364
  256.5 320.7 %reduce-scatter.13.cloned.1.call-start = ((), (), s32[]{:S(2)}) async-start(), calls=%async_computation.20 | async-start | bytes 4718592 | tf_op jit(solution)/shard_map/reduce_scatter | solution.py:368
  495.9 10.2 %copy-start.29 = (bf16[2048,2048]{1,0:T(8,128)(2,1)S(1)}, bf16[2048,2048]{1,0:T(8,128)(2,1)}, u32[]{:S(2)}) copy-start(bf16[2048,2048]{1,0:T(8,128)(2,1)} %all-gather.18.cloned.1.call-done) | copy-start | bytes 25165828
  495.9 10.2 %copy-start.31 = (bf16[1024,2048]{1,0:T(8,128)(2,1)S(1)}, bf16[1024,2048]{1,0:T(8,128)(2,1)}, u32[]{:S(2)}) copy-start(bf16[1024,2048]{1,0:T(8,128)(2,1)} %all-gather.16.cloned.1.call-done) | copy-start | bytes 12582916
  495.9 10.2 %copy-start.37 = (f32[1024,1024]{0,1:T(8,128)S(1)}, f32[1024,1024]{0,1:T(8,128)}, u32[]{:S(2)}) copy-start(f32[1024,1024]{0,1:T(8,128)} %fusion.6) | copy-start | bytes 12582916
  528.4 48.9 %copy-start.1 = (bf16[128,2048]{1,0:T(8,128)(2,1)S(1)}, bf16[128,2048]{1,0:T(8,128)(2,1)}, u32[]{:S(2)}) copy-start(bf16[128,2048]{1,0:T(8,128)(2,1)} %reduce-scatter.9.cloned.1.call-done) | copy-start | bytes 1572868
  528.4 50.3 %copy-start.5 = (bf16[1,128,2048]{2,1,0:T(8,128)(2,1)S(1)}, bf16[1,128,2048]{2,1,0:T(8,128)(2,1)}, u32[]{:S(2)}) copy-start(bf16[1,128,2048]{2,1,0:T(8,128)(2,1)} %param.13) | copy-start | bytes 1572868
  528.4 98.0 %all-gather.22.cloned.1.call-start = ((), (), s32[]{:S(2)}) async-start(), calls=%async_computation.21 | async-start | bytes 4718592 | tf_op jit(solution)/shard_map/all_gather | solution.py:364
  581.0 133.7 %reduce-scatter.21.cloned.1.call-start = ((), (), s32[]{:S(2)}) async-start(), calls=%async_computation.25 | async-start | bytes 10485760 | tf_op jit(solution)/shard_map/reduce_scatter | solution.py:376
  595.2 31.2 %copy-start.13 = (f32[1024,256]{0,1:T(8,128)S(1)}, f32[1024,256]{0,1:T(8,128)}, u32[]{:S(2)}) copy-start(f32[1024,256]{0,1:T(8,128)} %copy-done.12) | copy-start | bytes 3145732
  595.2 150.2 %reduce-scatter.19.cloned.1.call-start = ((), (), s32[]{:S(2)}) async-start(), calls=%async_computation.24 | async-start | bytes 1310720 | tf_op jit(solution)/shard_map/reduce_scatter | solution.py:376
  626.4 4.0 copy-start.10
  630.4 2.9 copy-start.34
  630.4 4.2 copy-start.21
  630.4 4.2 copy-start.23
  634.6 2.7 copy-start.32
  639.6 148.3 %reduce-scatter.17.cloned.1.call-start = ((), (), s32[]{:S(2)}) async-start(), calls=%async_computation.23 | async-start | bytes 2621440 | tf_op jit(solution)/shard_map/reduce_scatter | solution.py:376
  639.7 4.1 copy-start.15
  643.7 3.4 copy-start.19
  643.7 3.4 collective-permute-start.2
  644.6 5.3 copy-start.30
  653.8 189.9 %reduce-scatter.23.cloned.1.call-start = ((), (), s32[]{:S(2)}) async-start(), calls=%async_computation.26 | async-start | bytes 5242880 | tf_op jit(solution)/shard_map/reduce_scatter | solution.py:376
  663.5 232.4 %reduce-scatter.15.cloned.1.call-start = ((), (), s32[]{:S(2)}) async-start(), calls=%async_computation.22 | async-start | bytes 4718592 | tf_op jit(solution)/shard_map/reduce_scatter | solution.py:368
  669.7 276.5 %reduce-scatter.11.cloned.1.call-start = ((), (), s32[]{:S(2)}) async-start(), calls=%async_computation.19 | async-start | bytes 4718592 | tf_op jit(solution)/shard_map/reduce_scatter | solution.py:368
  714.6 56.5 %all-to-all-start.3 = ((bf16[8,64,2048]{2,1,0:T(8,128)(2,1)}), bf16[8,64,2048]{2,1,0:T(8,128)(2,1)S(1)}, u32[]{:S(2)}, u32[]{:S(2)}) async-start(bf16[8,64,2048]{2,1,0:T(8,128)(2,1)} %bitcast.114), calls=%async_computation.10 | async-start | bytes 4194304 | tf_op jit(solution)/shard_map/all_to_all | solution.py:380
  745.4 101.1 %collective-permute-start.3 = (bf16[64,2048]{1,0:T(8,128)(2,1)}, bf16[64,2048]{1,0:T(8,128)(2,1)S(1)}, u32[]{:S(2)}, u32[]{:S(2)}) collective-permute-start(bf16[64,2048]{1,0:T(8,128)(2,1)} %reduce-scatter.19.cloned.1.call-done), channel_id=1, source_target_pairs={{0,0},{8,1},{16,2},{24,3},{1,4},{9,5},{17,6},{25,7},{2,8},{10,9},{... | collective-permute-start | bytes 786440 | tf_op jit(solution)/shard_map/ppermute | solution.py:518
  787.9 77.2 %all-to-all-start.2 = ((bf16[8,64,512]{2,1,0:T(8,128)(2,1)}), bf16[8,64,512]{2,1,0:T(8,128)(2,1)}, u32[]{:S(2)}, u32[]{:S(2)}) async-start(bf16[8,64,512]{2,1,0:T(8,128)(2,1)} %bitcast.126), calls=%async_computation.7 | async-start | bytes 1048576 | tf_op jit(solution)/shard_map/all_to_all | solution.py:380
  857.6 4.2 copy-start.3
  857.6 4.2 copy-start.4
  864.6 2.5 copy-start.16
  864.6 2.5 copy-start.26
  866.4 29.4 %copy-start.28 = (f32[128]{0:T(128)S(1)}, f32[128]{0:T(128)}, u32[]{:S(2)}) copy-start(f32[128]{0:T(128)} %copy-done.27) | copy-start | bytes 1540
  866.5 79.8 %copy-start.6 = (bf16[1,128,2048]{2,1,0:T(8,128)(2,1)S(1)}, bf16[1,128,2048]{2,1,0:T(8,128)(2,1)}, u32[]{:S(2)}) copy-start(bf16[1,128,2048]{2,1,0:T(8,128)(2,1)} %param.13) | copy-start | bytes 1572868
  866.5 79.7 %copy-start.7 = (bf16[128,2048]{1,0:T(8,128)(2,1)S(1)}, bf16[128,2048]{1,0:T(8,128)(2,1)}, u32[]{:S(2)}) copy-start(bf16[128,2048]{1,0:T(8,128)(2,1)} %reduce-scatter.13.cloned.1.call-done) | copy-start | bytes 1572868
  (12 other events, 20.1 us)
Sparse Core Ops, SparseCore 0:
  32.8 40.5 all-gather.11
  75.6 47.1 all-gather.9
  131.6 25.3 all-gather.13
  161.7 75.0 reduce-scatter.8
  239.1 70.5 all-gather.19
  311.1 47.1 all-gather.23
  360.2 86.3 all-gather.17
  448.7 47.1 all-gather.15
  528.5 48.7 reduce-scatter.12
  581.1 45.2 all-gather.21
  629.5 85.0 reduce-scatter.20
  717.6 27.7 reduce-scatter.18
  748.9 38.9 reduce-scatter.16
  791.0 52.6 reduce-scatter.22
  845.8 50.0 reduce-scatter.14
  898.0 48.1 reduce-scatter.10

commit v2 on v1

--- a/solution.py
+++ b/solution.py
@@ -355,9 +355,15 @@
         mlp_gain_sum,
     )
 
+N_Z = 4
+
+
+def after(value, *others):
+    return lax.optimization_barrier((value,) + others)[0]
+
+
 def swap_cores(values):
-    size = lax.axis_size("ctx")
-    return lax.ppermute(values, "ctx", [(i, i ^ 1) for i in range(size)])
+    return lax.ppermute(values, "ctx", [(i, i ^ 1) for i in range(2 * N_Z)])
 
 
 def gather_ctx(rows):
@@ -368,24 +374,112 @@
     return lax.psum_scatter(partial, "ctx", scatter_dimension=0, tiled=True).astype(jnp.float32)
 
 
-def gather_dp(rows):
-    return lax.all_gather(rows, "dp", axis=0, tiled=True)
-
-
-def scatter_dp(partial):
-    return lax.psum_scatter(partial, "dp", scatter_dimension=0, tiled=True)
-
-
-def exchange_ctx(blocks):
-    return lax.all_to_all(blocks, "ctx", 0, 0, tiled=True)
-
-
-def out_weight_moves(n_dp, n_ctx):
-    per_head = n_dp * n_ctx // QUERY_HEADS
+def hop(values, lowest, highest):
+    moves = [(2 * z, 2 * z + 2) for z in range(lowest, highest + 1)]
+    moves += [(2 * (N_Z - 1 - z) + 1, 2 * (N_Z - 1 - z) - 1) for z in range(lowest, highest + 1)]
+    return lax.ppermute(values, "ctx", moves)
+
+
+def pass_along(rows, *first):
+    other = swap_cores(rows)
+    even = is_even()
+    pair = jnp.concatenate([jnp.where(even, rows, other), jnp.where(even, other, rows)], axis=0)
+    held = [after(pair, *first)]
+    for step in range(1, N_Z):
+        held.append(hop(held[-1], step - 1, N_Z - 2))
+    return held
+
+
+def place_passed(held):
+    z, even = lax.axis_index("ctx") // 2, is_even()
+    size = held[0].shape[0]
+    whole = jnp.zeros(((N_Z + 1) * size,) + held[0].shape[1:], held[0].dtype)
+    whole = lax.dynamic_update_slice_in_dim(whole, held[0], z * size, 0)
+    for step in range(1, N_Z):
+        for block, up in ((held[step], even), (swap_cores(held[step]), ~even)):
+            place = jnp.where(up, z - step, z + step)
+            place = jnp.where((place >= 0) & (place < N_Z), place, N_Z)
+            whole = lax.dynamic_update_slice_in_dim(whole, block, place * size, 0)
+    return whole[: N_Z * size]
+
+
+def send_dp(values, first, second):
+    moves = [(d, c, d ^ (second if c % 2 else first)) for d in range(4) for c in range(2 * N_Z)]
+    moves = [(d * 2 * N_Z + c, to * 2 * N_Z + c) for d, c, to in moves]
+    return lax.ppermute(values, ("dp", "ctx"), moves)
+
+
+def rotate_z(values, step):
+    moves = [(2 * a + t, 2 * ((a + step) % N_Z) + t) for a in range(N_Z) for t in range(2)]
+    return lax.ppermute(values, "ctx", moves)
+
+
+def is_even():
+    return lax.axis_index("ctx") % 2 == 0
+
+
+def near_bit():
+    return jnp.where(is_even(), 1, 2)
+
+
+def place_dp(rows, first, second, third):
+    d = lax.axis_index("dp")
+    size = rows.shape[0]
+    whole = jnp.zeros((4 * size,) + rows.shape[1:], rows.dtype)
+    for block, place in (
+        (rows, d),
+        (first, d ^ near_bit()),
+        (second, d ^ (3 - near_bit())),
+        (third, d ^ 3),
+    ):
+        whole = lax.dynamic_update_slice_in_dim(whole, block, place * size, 0)
+    return whole
+
+
+def stack_dp(rows, first, second, third):
+    one = jnp.where(is_even(), first, second)
+    two = jnp.where(is_even(), second, first)
+    return jnp.concatenate([rows, one, two, third], axis=0)
+
+
+def pick(blocks, chip, core):
+    start = (chip, core) + (0,) * (blocks.ndim - 2)
+    return lax.dynamic_slice(blocks, start, (1, 1) + blocks.shape[2:])[0, 0]
+
+
+def exchange_pairs(blocks):
+    z, core = lax.axis_index("ctx") // 2, lax.axis_index("ctx") % 2
+    give = jnp.stack([pick(blocks, (z + s) % N_Z, 1 - core) for s in range(N_Z)])
+    got = swap_cores(give)
+    pairs = []
+    for s in range(N_Z):
+        keep = pick(blocks, (z + s) % N_Z, core)
+        pairs.append(
+            jnp.concatenate(
+                [jnp.where(is_even(), keep, got[s]), jnp.where(is_even(), got[s], keep)], axis=0
+            )
+        )
+    return pairs
+
+
+def place_z(pieces):
+    z = lax.axis_index("ctx") // 2
+    size = pieces[0].shape[0]
+    whole = jnp.zeros((N_Z * size,) + pieces[0].shape[1:], pieces[0].dtype)
+    for s, piece in enumerate(pieces):
+        whole = lax.dynamic_update_slice_in_dim(whole, piece, (z - s) % N_Z * size, 0)
+    return whole
+
+
+def rotate_pieces(pairs):
+    return [pairs[0]] + [rotate_z(pairs[s], s) for s in range(1, N_Z)]
+
+
+def out_weight_moves():
     moves = []
-    for block in range(n_dp * n_ctx):
-        head, part = divmod(block, per_head)
-        moves.append((block, part * n_ctx + head))
+    for block in range(8 * N_Z):
+        head, part = divmod(block, N_Z)
+        moves.append((block, part * 2 * N_Z + head))
     return moves
 
 
@@ -405,12 +499,13 @@
 ):
     low = jnp.bfloat16
     wide = jnp.float32
-    n_dp = lax.axis_size("dp")
-    n_ctx = lax.axis_size("ctx")
-    core = lax.axis_index("ctx") % 2
+    d = lax.axis_index("dp")
+    even = is_even()
     rows = w_query.shape[0]
-    seq_rows = layer_input.shape[1] * n_ctx
+    seq_rows = layer_input.shape[1] * 2 * N_Z
     ff_part = w_down.shape[0]
+    width = 4 * ff_part
+    cols = 2 * HEAD_SIZE
 
     def dot(left, right):
         return jnp.dot(left, right, preferred_element_type=wide)
@@ -423,6 +518,16 @@
 
     def lowered(weight):
         return weight.astype(low).astype(wide)
+
+    def turned(values):
+        size = values.shape[1] // 4
+        return jnp.concatenate(
+            [lax.dynamic_slice_in_dim(values, (d ^ e) * size, size, 1) for e in range(4)], axis=1
+        )
+
+    def block_columns(values, e):
+        size = values.shape[1] // 4
+        return lax.dynamic_slice_in_dim(values, e * size, size, 1)
 
     x_rows = layer_input[0].astype(wide)
     d_out = cotangent[0]
@@ -431,30 +536,40 @@
     low_q, low_k, low_v = lowered(w_query), lowered(key_weight), lowered(value_weight)
     low_g, low_u = lowered(w_gate), lowered(w_up)
 
+    moves = out_weight_moves()
+    out_own = lax.ppermute(w_out.astype(low), ("dp", "ctx"), moves)
+
     inverse1 = lax.rsqrt(jnp.mean(x_rows * x_rows, axis=-1, keepdims=True) + NORM_EPSILON)
     hat1 = x_rows * inverse1
-    all_hat1 = gather_ctx(hat1.astype(low))
-
-    q_cols = (low_q * gain_a).astype(low).reshape(rows, n_ctx, 1, HEAD_SIZE)
-    k_cols = (low_k * gain_a).astype(low).reshape(rows, n_ctx // 2, 1, 1, HEAD_SIZE)
-    v_cols = (low_v * gain_a).astype(low).reshape(rows, n_ctx // 2, 1, 1, HEAD_SIZE)
-    kv_cols = jnp.concatenate([k_cols, v_cols], axis=2).reshape(rows, n_ctx, 1, HEAD_SIZE)
-    proj = jnp.concatenate([q_cols, kv_cols], axis=2).reshape(rows, n_ctx, 2 * HEAD_SIZE)
-    proj = exchange_ctx(proj.transpose(1, 0, 2)).reshape(n_ctx * rows, 2 * HEAD_SIZE)
-    proj = gather_dp(proj)
-    moves = out_weight_moves(n_dp, n_ctx)
-    out_w = gather_dp(lax.ppermute(w_out.astype(low), ("dp", "ctx"), moves))
+    sent1 = turned(hat1).astype(low)
+
+    q_cols = (low_q * gain_a).astype(low).reshape(rows, N_Z, 2, HEAD_SIZE).transpose(1, 2, 0, 3)
+    k_cols = (low_k * gain_a).astype(low).reshape(rows, N_Z, 1, HEAD_SIZE).transpose(1, 2, 0, 3)
+    v_cols = (low_v * gain_a).astype(low).reshape(rows, N_Z, 1, HEAD_SIZE).transpose(1, 2, 0, 3)
+    proj_blocks = jnp.concatenate([q_cols, jnp.concatenate([k_cols, v_cols], axis=1)], axis=3)
+    proj_pairs = exchange_pairs(proj_blocks)
+    proj_moved = rotate_pieces(proj_pairs)
+    all_hat1 = gather_ctx(sent1)
+    proj_own = place_z(proj_moved)
+    proj_first, proj_second = send_dp(proj_own, 1, 2), send_dp(proj_own, 2, 1)
+    proj_third = send_dp(proj_first, 2, 1)
+    gain_late = after(gain_m, *proj_pairs)
 
     def ff_columns(weight):
-        blocks = (weight * gain_m).astype(low).reshape(rows, n_dp, n_ctx, ff_part)
-        return blocks.transpose(2, 0, 1, 3).reshape(n_ctx, rows, n_dp * ff_part)
-
-    gate_up = jnp.concatenate([ff_columns(low_g), ff_columns(low_u)], axis=2)
-    gate_up = exchange_ctx(gate_up).reshape(n_ctx * rows, 2 * n_dp * ff_part)
-    gate_up_w = gather_dp(gate_up)
-    down_w = gather_dp(w_down.astype(low))
-    all_cot = gather_ctx(d_out)
-
+        blocks = (weight * gain_late).astype(low).reshape(rows, 4, N_Z, 2, ff_part)
+        return blocks.transpose(2, 3, 0, 1, 4).reshape(N_Z, 2, rows, width)
+
+    gate_up_pairs = exchange_pairs(jnp.concatenate([ff_columns(low_g), ff_columns(low_u)], axis=3))
+    down_own = w_down.astype(low)
+    all_hat1, proj_third, out_own, down_own, *gate_up_pairs = lax.optimization_barrier(
+        (all_hat1, proj_third, out_own, down_own, *gate_up_pairs)
+    )
+    out_first, out_second = send_dp(out_own, 1, 2), send_dp(out_own, 2, 1)
+    out_w = place_dp(out_own, out_first, out_second, send_dp(out_first, 2, 1))
+    down_first, down_second = send_dp(down_own, 1, 2), send_dp(down_own, 2, 1)
+    all_cot = gather_ctx(after(d_out, all_hat1))
+    proj = stack_dp(proj_own, proj_first, proj_second, proj_third)
+    gate_up_moved = rotate_pieces(gate_up_pairs)
     positions = jnp.arange(seq_rows, dtype=jnp.int32)
     cosine, sine = rope_angles(positions, HEAD_SIZE)
     cosine, sine = cosine[:, 0], sine[:, 0]
@@ -468,10 +583,10 @@
     scale = HEAD_SIZE ** (-0.5)
     q_rot = (rotate(qkv[:, :HEAD_SIZE], 1.0) * scale).astype(low)
     own = qkv[:, HEAD_SIZE:]
-    own = jnp.where(core == 0, rotate(own, 1.0), own).astype(low)
+    own = jnp.where(even, rotate(own, 1.0), own).astype(low)
     other = swap_cores(own)
-    keys = jnp.where(core == 0, own, other)
-    values = jnp.where(core == 0, other, own)
+    keys = jnp.where(even, own, other)
+    values = jnp.where(even, other, own)
     allowed = (positions[None, :] <= positions[:, None]) | (positions[None, :] < prefix[0])
     scores = jnp.where(allowed, dot_t(q_rot, keys), -1e30)
     peak = jnp.max(scores, axis=-1, keepdims=True)
@@ -479,43 +594,83 @@
     total = jnp.sum(weights, axis=-1, keepdims=True)
     attended = dot(weights.astype(low), values) / total
     attn = attended.astype(low)
-    middle = x_rows + scatter_ctx(dot(attn, out_w).astype(low))
+    branch_part = dot(attn, out_w).astype(low)
+    branch_part, down_first, down_second, all_cot, *gate_up_moved = lax.optimization_barrier(
+        (branch_part, down_first, down_second, all_cot, *gate_up_moved)
+    )
+    gate_up_own = place_z(gate_up_moved)
+    branch = scatter_ctx(branch_part)
+    gu_first, gu_second = send_dp(gate_up_own, 1, 2), send_dp(gate_up_own, 2, 1)
+    middle = x_rows + branch
 
     inverse2 = lax.rsqrt(jnp.mean(middle * middle, axis=-1, keepdims=True) + NORM_EPSILON)
     hat2 = middle * inverse2
-    all_hat2 = gather_ctx(hat2.astype(low))
-    width = n_dp * ff_part
+    sent2, gu_first, gu_second = lax.optimization_barrier(
+        (turned(hat2).astype(low), gu_first, gu_second)
+    )
+    all_hat2 = gather_ctx(sent2)
+    gu_third = send_dp(gu_first, 2, 1)
+    down_third = send_dp(after(down_first, gu_first), 2, 1)
+    gate_up_w = stack_dp(gate_up_own, gu_first, gu_second, gu_third)
+    down_w = place_dp(down_own, down_first, down_second, down_third)
+    d_hidden = dot_t(all_cot, down_w)
+    all_hat2, gate_up_w, down_w, all_cot, d_hidden = lax.optimization_barrier(
+        (all_hat2, gate_up_w, down_w, all_cot, d_hidden)
+    )
     gate = dot(all_hat2, gate_up_w[:, :width])
     up = dot(all_hat2, gate_up_w[:, width:])
     sig = jax.nn.sigmoid(gate)
     silu = gate * sig
     hidden = (silu * up).astype(low)
-    output = (middle + scatter_ctx(dot(hidden, down_w).astype(low))).astype(low)[None]
-
-    d_hidden = dot_t(all_cot, down_w)
+
     d_gate = (d_hidden * up * sig * (1.0 + gate * (1.0 - sig))).astype(low)
     d_up = (d_hidden * silu).astype(low)
     d_gate_up = jnp.concatenate([d_gate, d_up], axis=1)
-    e2 = scatter_ctx(dot_t(d_gate_up, gate_up_w).astype(low))
-    down_sum = scatter_dp(t_dot(hidden, all_cot).astype(low)).astype(wide)
-    gate_up_sum = scatter_dp(t_dot(all_hat2, d_gate_up).astype(low))
-    gate_up_sum = exchange_ctx(gate_up_sum.reshape(n_ctx, rows, 2 * width)).astype(wide)
-
-    def ff_rows(part):
-        blocks = part.reshape(n_ctx, rows, n_dp, ff_part).transpose(1, 2, 0, 3)
-        return blocks.reshape(rows, n_dp * n_ctx * ff_part)
-
-    raw_gate = ff_rows(gate_up_sum[:, :, :width])
-    raw_up = ff_rows(gate_up_sum[:, :, width:])
-    gain_mlp = jnp.sum(raw_gate * low_g, axis=1) + jnp.sum(raw_up * low_u, axis=1)
-    gate_sum, up_sum = raw_gate * gain_m, raw_up * gain_m
+    e2_part = dot_t(d_gate_up, gate_up_w).astype(low)
+    e2 = scatter_ctx(e2_part)
+    d_gate_up, hidden = lax.optimization_barrier((d_gate_up, hidden, e2_part))[:2]
+
+    def gu_block(j):
+        return t_dot(block_columns(all_hat2, j), d_gate_up)
+
+    def down_block(j):
+        return t_dot(block_columns(hidden, d ^ j), all_cot)
+
+    gu_across = send_dp(gu_block(3).astype(low), 2, 1)
+    gu_far = send_dp(gu_block(3 - near_bit()).astype(low), 2, 1)
+    gu_near_term, gu_own_term = gu_block(near_bit()), gu_block(0)
+    out_part = dot(hidden, down_w).astype(low)
+    down_sent3 = down_block(3).astype(low)
+    down_sent_far = down_block(3 - near_bit()).astype(low)
+    e2, gu_across, gu_far, down_sent3, down_sent_far, out_part = lax.optimization_barrier(
+        (e2, gu_across, gu_far, down_sent3, down_sent_far, out_part)
+    )
+    gu_near = send_dp((gu_near_term + gu_across.astype(wide)).astype(low), 1, 2)
+    down_across, down_far = send_dp(down_sent3, 2, 1), send_dp(down_sent_far, 2, 1)
+    e2 = turned(e2)
     d_middle = d_out.astype(wide) + inverse2 * (
         e2 - hat2 * jnp.mean(e2 * hat2, axis=-1, keepdims=True)
     )
-
-    all_branch = gather_ctx(d_middle.astype(low))
-    out_sum = scatter_dp(t_dot(attn, all_branch).astype(low))
-    out_sum = lax.ppermute(out_sum, ("dp", "ctx"), [(b, a) for a, b in moves]).astype(wide)
+    branch_low = d_middle.astype(low)
+    out_branch = scatter_ctx(after(out_part, branch_low))
+    all_branch = place_passed(pass_along(branch_low))
+    gate_up_sum = (gu_own_term + gu_far.astype(wide) + gu_near.astype(wide)).astype(low)
+    sum_pairs = exchange_pairs(gate_up_sum.reshape(N_Z, 2, rows, 2 * width))
+
+    all_branch, down_across, down_far, out_branch, *sum_pairs = lax.optimization_barrier(
+        (all_branch, down_across, down_far, out_branch, *sum_pairs)
+    )
+    head_part = t_dot(attn, all_branch)
+
+    def out_block(j):
+        return lax.dynamic_slice_in_dim(head_part, (d ^ j) * rows, rows, 0)
+
+    out_across = send_dp(out_block(3).astype(low), 2, 1)
+    out_far = send_dp(out_block(3 - near_bit()).astype(low), 2, 1)
+    out_near = send_dp((out_block(near_bit()) + out_across.astype(wide)).astype(low), 1, 2)
+    down_near = send_dp((down_block(near_bit()) + down_across.astype(wide)).astype(low), 1, 2)
+    down_sum = down_block(0) + down_far.astype(wide) + down_near.astype(wide)
+    gate_up_sum = place_z(rotate_pieces(sum_pairs))
     d_attn = dot_t(all_branch, out_w).astype(low)
     delta = jnp.sum(d_attn.astype(wide) * attended, axis=-1, keepdims=True)
     probs = weights / total
@@ -523,18 +678,43 @@
     d_query = rotate(dot(d_scores, keys) * scale, -1.0)
     dk_part = t_dot(d_scores, q_rot)
     dv_part = t_dot(probs.astype(low), d_attn)
-    mine = jnp.where(core == 0, dk_part, dv_part)
-    mine = mine + swap_cores(jnp.where(core == 0, dv_part, dk_part).astype(low)).astype(wide)
-    mine = jnp.where(core == 0, rotate(mine, -1.0), mine)
+    mine = jnp.where(even, dk_part, dv_part)
+    mine = mine + swap_cores(jnp.where(even, dv_part, dk_part).astype(low)).astype(wide)
+    mine = jnp.where(even, rotate(mine, -1.0), mine)
     d_proj = jnp.concatenate([d_query, mine], axis=1).astype(low)
-    e1 = scatter_ctx(dot_t(d_proj, proj).astype(low))
-    proj_sum = scatter_dp(t_dot(all_hat1, d_proj).astype(low))
-    proj_sum = exchange_ctx(proj_sum.reshape(n_ctx, rows, 2 * HEAD_SIZE)).astype(wide)
-    proj_sum = proj_sum.transpose(1, 0, 2)
-    raw_q = proj_sum[:, :, :HEAD_SIZE].reshape(rows, n_ctx * HEAD_SIZE)
-    kv_sum = proj_sum[:, :, HEAD_SIZE:].reshape(rows, n_ctx // 2, 2, HEAD_SIZE)
-    raw_k = kv_sum[:, :, 0].reshape(rows, n_ctx // 2 * HEAD_SIZE)
-    raw_v = kv_sum[:, :, 1].reshape(rows, n_ctx // 2 * HEAD_SIZE)
+    e1_part = dot_t(d_proj, proj).astype(low)
+    e1 = turned(scatter_ctx(e1_part))
+    d_proj, out_near = lax.optimization_barrier((d_proj, out_near, e1_part))[:2]
+    output = (middle + out_branch).astype(low)[None]
+
+    def proj_block(j):
+        return t_dot(block_columns(all_hat1, j), d_proj)
+
+    proj_across = send_dp(proj_block(3).astype(low), 2, 1)
+    proj_far = send_dp(proj_block(3 - near_bit()).astype(low), 2, 1)
+    proj_near = send_dp((proj_block(near_bit()) + proj_across.astype(wide)).astype(low), 1, 2)
+    proj_sum = proj_block(0) + proj_far.astype(wide) + proj_near.astype(wide)
+    proj_sum = place_z(
+        rotate_pieces(exchange_pairs(proj_sum.astype(low).reshape(N_Z, 2, rows, cols)))
+    )
+    out_sum = out_block(0) + out_far.astype(wide) + out_near.astype(wide)
+    out_sum = lax.ppermute(
+        out_sum.astype(low), ("dp", "ctx"), [(to, start) for start, to in moves]
+    ).astype(wide)
+
+    def ff_rows(part):
+        blocks = part.astype(wide).reshape(2 * N_Z, rows, 4, ff_part).transpose(1, 2, 0, 3)
+        return blocks.reshape(rows, 8 * N_Z * ff_part)
+
+    raw_gate = ff_rows(gate_up_sum[:, :width])
+    raw_up = ff_rows(gate_up_sum[:, width:])
+    gain_mlp = jnp.sum(raw_gate * low_g, axis=1) + jnp.sum(raw_up * low_u, axis=1)
+    gate_sum, up_sum = raw_gate * gain_m, raw_up * gain_m
+    proj_sum = proj_sum.astype(wide).reshape(2 * N_Z, rows, cols).transpose(1, 0, 2)
+    raw_q = proj_sum[:, :, :HEAD_SIZE].reshape(rows, QUERY_HEADS * HEAD_SIZE)
+    kv_sum = proj_sum[:, :, HEAD_SIZE:].reshape(rows, KEY_VALUE_HEADS, 2, HEAD_SIZE)
+    raw_k = kv_sum[:, :, 0].reshape(rows, KEY_VALUE_HEADS * HEAD_SIZE)
+    raw_v = kv_sum[:, :, 1].reshape(rows, KEY_VALUE_HEADS * HEAD_SIZE)
     gain_attn = (
         jnp.sum(raw_q * low_q, axis=1)
         + jnp.sum(raw_k * low_k, axis=1)
@@ -557,7 +737,7 @@
 
 
 def solution(mesh):
-    local = head_local if mesh.shape["ctx"] == QUERY_HEADS else gathered_local
+    local = head_local if (mesh.shape["dp"], mesh.shape["ctx"]) == (4, 2 * N_Z) else gathered_local
     in_specs = (
         P("dp", "ctx", None),
         P("dp", "ctx", None),

time: 965 us -> 612 us (0.63)
  waiting for transfers between devices: 643 us -> 259 us
  blocking collectives: 101 us -> 0 us
  starting transfers between devices: 13.4 us -> 101 us
  other arithmetic: 44.1 us -> 69.5 us
  local copies, waits for them, and re-layouts: 25.6 us -> 50.7 us
    all_gather x4 -> x0, waiting for transfers between devices: 187 us -> none  [gather_dp(): return lax.all_gather(rows, 'dp', axis=0, tiled=True)]
    ppermute x4 -> x51, waiting for transfers between devices: 0.01 us -> 181 us  [the longest x24 81.7 us: send_dp(): return lax.ppermute(values, ('dp', 'ctx'), moves)]
    all_gather x4 -> x3, waiting for transfers between devices: 178 us -> 4.03 us  [gather_ctx(): return lax.all_gather(rows, 'ctx', axis=0, tiled=True)]
    reduce_scatter x4 -> x0, waiting for transfers between devices: 129 us -> none  [scatter_dp(): return lax.psum_scatter(partial, 'dp', scatter_dimension=0, tiled=True)]
    all_to_all x2 -> x0, blocking collectives: 101 us -> none  [exchange_ctx(): return lax.all_to_all(blocks, 'ctx', 0, 0, tiled=True)]
    ppermute x4 -> x51, starting transfers between devices: 3.34 us -> 101 us  [the longest x10 38.6 us: swap_cores(): return lax.ppermute(values, 'ctx', [(i, i ^ 1) for i in range(2 * N_Z)])]
    reduce_scatter x4, waiting for transfers between devices: 124 us -> 74.7 us  [scatter_ctx(): lax.psum_scatter(partial, 'ctx', scatter_dimension=0, tiled=True)]
    all_to_all x2 -> x0, waiting for transfers between devices: 24.1 us -> none  [exchange_ctx(): return lax.all_to_all(blocks, 'ctx', 0, 0, tiled=True)]
  transfers between devices with their start and end apart: 22 -> 58, of which waited for: 16 -> 22; matrix products, arithmetic and copies ran while one was open for 14% -> 30% of each run, Pallas kernels for 0% -> 0%
where the time goes in v2:
time: 612 us; the launch traced here: 605 us
  waiting for transfers between devices  259 us (42%)
  matrix products  107 us (17%)
  starting transfers between devices  101 us (17%)
  other arithmetic  69.5 us (11%)
  local copies, waits for them, and re-layouts  50.7 us (8%)
  between operations  17.3 us (3%)
    ppermute x24, waiting for transfers between devices, send_dp(): return lax.ppermute(values, ('dp', 'ctx'), moves)  81.7 us
    reduce_scatter x4, waiting for transfers between devices, scatter_ctx(): lax.psum_scatter(partial, 'ctx', scatter_dimension=0, tiled=True)  74.7 us
    ppermute x12, waiting for transfers between devices, rotate_z(): return lax.ppermute(values, 'ctx', moves)  67.2 us
    dot_general x15, matrix products, t_dot(): lax.dot_general(left, right, (((0,), (0,)), ((), ())), preferred_element_...  40.8 us
    ppermute x10, starting transfers between devices, swap_cores(): return lax.ppermute(values, 'ctx', [(i, i ^ 1) for i in range(2 * N_Z)])  38.6 us
    dot_general x7, matrix products, dot(): return jnp.dot(left, right, preferred_element_type=wide)  35.6 us
    ppermute x24, starting transfers between devices, send_dp(): return lax.ppermute(values, ('dp', 'ctx'), moves)  35 us
    dot_general x6, matrix products, dot_t(): lax.dot_general(left, right, (((1,), (1,)), ((), ())), preferred_element_...  30.2 us
  transfers between devices with their start and end apart: 58, of which 22 were waited for; matrix products, arithmetic and copies ran while one was open for 30% of the time, Pallas kernels for 0%

profile of v2, /device:TPU:0, one launch (start us, length us, event | category | flops | bytes accessed | tf_op | source)
XLA Modules:
  0.0 604.9 jit_solution(4589477712409949265)
XLA Ops:
  16.1 2.9 fusion.12
  33.5 6.3 %collective-permute-done.1 = bf16[128,512]{1,0:T(8,128)(2,1)} collective-permute-done((bf16[128,512]{1,0:T(8,128)(2,1)}, bf16[128,512]{1,0:T(8,128)(2,1)}, u32[]{:S(2)}, u32[]{:S(2)}) %collective-permute-start.1) | collective-permute-done | bytes 131104 | tf_op jit(solution)/shard_map/ppermute | solution.py:414
  40.8 18.8 %collective-permute-done.2 = bf16[128,512]{1,0:T(8,128)(2,1)S(1)} collective-permute-done((bf16[128,512]{1,0:T(8,128)(2,1)S(1)}, bf16[128,512]{1,0:T(8,128)(2,1)S(1)}, u32[]{:S(2)}, u32[]{:S(2)}) %collective-permute-start.2) | collective-permute-done | bytes 131104 | tf_op jit(solution)/shard_map/ppermute | solution.py:414
  65.8 7.3 %collective-permute-done.4 = bf16[512,512]{1,0:T(8,128)(2,1)S(1)} collective-permute-done((bf16[512,512]{1,0:T(8,128)(2,1)S(1)}, bf16[512,512]{1,0:T(8,128)(2,1)S(1)}, u32[]{:S(2)}, u32[]{:S(2)}) %collective-permute-start.4) | collective-permute-done | bytes 524320 | tf_op jit(solution)/shard_map/ppermute | solution.py:409
  77.2 5.2 collective-permute-done.5
  82.6 6.3 %collective-permute-start.8 = (bf16[512,512]{1,0:T(8,128)(2,1)S(1)}, bf16[512,512]{1,0:T(8,128)(2,1)S(1)}, u32[]{:S(2)}, u32[]{:S(2)}) collective-permute-start(bf16[512,512]{1,0:T(8,128)(2,1)S(1)} %copy-done.50), channel_id=1, source_target_pairs={{0,16},{1,9},{2,18},{3,11},{4,20},{5,13},{6,22},{7,15},{8,24},{9,1... | collective-permute-start | bytes 1572872 | tf_op jit(solution)/shard_map/ppermute | solution.py:409
  89.7 7.1 %collective-permute-done.8 = bf16[512,512]{1,0:T(8,128)(2,1)S(1)} collective-permute-done((bf16[512,512]{1,0:T(8,128)(2,1)S(1)}, bf16[512,512]{1,0:T(8,128)(2,1)S(1)}, u32[]{:S(2)}, u32[]{:S(2)}) %collective-permute-start.8) | collective-permute-done | bytes 524320 | tf_op jit(solution)/shard_map/ppermute | solution.py:409
  102.5 4.7 fusion.75
  119.0 8.6 %collective-permute-done.12 = bf16[64,2048]{1,0:T(8,128)(2,1)S(1)} collective-permute-done((bf16[64,2048]{1,0:T(8,128)(2,1)S(1)}, bf16[64,2048]{1,0:T(8,128)(2,1)S(1)}, u32[]{:S(2)}, u32[]{:S(2)}) %collective-permute-start.12) | collective-permute-done | bytes 262176 | tf_op jit(solution)/shard_map/ppermute | solution.py:409
  131.1 3.3 convolution_convert_fusion.2
  134.5 5.8 collective-permute-done.15
  140.2 25.1 %collective-permute-done.16 = bf16[128,2048]{1,0:T(8,128)(2,1)} collective-permute-done((bf16[128,2048]{1,0:T(8,128)(2,1)}, bf16[128,2048]{1,0:T(8,128)(2,1)}, u32[]{:S(2)}, u32[]{:S(2)}) %collective-permute-start.16) | collective-permute-done | bytes 524320 | tf_op jit(solution)/shard_map/ppermute | solution.py:414
  176.2 49.9 %reduce-scatter.5.cloned.1.call-done = bf16[128,2048]{1,0:T(8,128)(2,1)} async-done(((bf16[1024,2048]{1,0:T(8,128)(2,1)}), bf16[128,2048]{1,0:T(8,128)(2,1)}) %reduce-scatter.5.cloned.1.call-update) | async-done | bytes 524304 | tf_op jit(solution)/shard_map/reduce_scatter | solution.py:374
  237.8 8.6 %collective-permute-done.21 = bf16[256,2048]{1,0:T(8,128)(2,1)S(1)} collective-permute-done((bf16[256,2048]{1,0:T(8,128)(2,1)S(1)}, bf16[256,2048]{1,0:T(8,128)(2,1)S(1)}, u32[]{:S(2)}, u32[]{:S(2)}) %collective-permute-start.21) | collective-permute-done | bytes 1048608 | tf_op jit(solution)/shard_map/ppermute | solution.py:409
  246.6 6.3 %fusion.106 = f32[1024,1024]{1,0:T(8,128)} fusion(bf16[1024,2048]{1,0:T(8,128)(2,1)S(1)} %copy-done.4, bf16[1024,2048]{1,0:T(8,128)(2,1)S(1)} %constant_dynamic-update-slice_fusion.14), kind=kOutput, calls=%fused_computation.336 | convolution fusion | flops 4294967296 | bytes 12582912 | tf_op jit(solution)/shard_map/dot_general | solution.py:514
  252.9 16.0 %collective-permute-done.20 = bf16[512,2048]{1,0:T(8,128)(2,1)S(1)} collective-permute-done((bf16[512,2048]{1,0:T(8,128)(2,1)}, bf16[512,2048]{1,0:T(8,128)(2,1)S(1)}, u32[]{:S(2)}, u32[]{:S(2)}) %collective-permute-start.20) | collective-permute-done | bytes 2097184 | tf_op jit(solution)/shard_map/ppermute | solution.py:409
  268.9 5.7 pad_maximum_fusion
  274.6 4.0 all-gather.8.cloned.1.call-done
  278.6 10.0 %fusion.1 = f32[1024,1024]{1,0:T(8,128)} fusion(bf16[1024,2048]{1,0:T(8,128)(2,1)} %all-gather.8.cloned.1.call-done, bf16[2048,2048]{1,0:T(8,128)(2,1)} %pad_maximum_fusion), kind=kOutput, calls=%fused_computation.10 | convolution fusion | flops 4294967296 | bytes 12582912 | tf_op jit(solution)/shard_map/dot_general | solution.py:511
  288.6 9.5 %multiply_convert_fusion.1 = (bf16[1024,1024]{1,0:T(8,128)(2,1)}, bf16[1024,1024]{1,0:T(8,128)(2,1)S(1)}, bf16[1024,1024]{1,0:T(8,128)(2,1)}) fusion(f32[1024,1024]{1,0:T(8,128)} %fusion.1, f32[1024,1024]{1,0:T(8,128)S(1)} %copy-done.67, bf16[1024,2048]{1,0:T(8,128)(2,1)S(1)} %copy-done.30, bf16[2048,2048]{1,0:T(8,128)(2,1)S(1)} %copy-done.11), kind=kOutput, calls=%fused_computation.5 | convolution fusion | flops 4310695936 | bytes 23068672 | tf_op jit(solution)/shard_map/dot_general | solution.py:511
  299.4 11.6 %convolution_convert_fusion.1 = bf16[1024,2048]{1,0:T(8,128)(2,1)} fusion(bf16[2048,2048]{1,0:T(8,128)(2,1)S(1)} %copy-done.11, bf16[1024,1024]{1,0:T(8,128)(2,1)} %get-tuple-element.107, bf16[1024,1024]{1,0:T(8,128)(2,1)S(1)} %get-tuple-element.106), kind=kOutput, calls=%fused_computation.19 | convolution fusion | flops 8600420352 | bytes 16777216 | tf_op jit(solution)/shard_map/dot_general | solution.py:514
  311.5 2.9 pad_maximum_fusion.1
  315.0 3.7 convolution_convert_fusion.4
  318.7 3.7 convolution_convert_fusion.5
  329.0 6.1 %convolution_convert_fusion.3 = bf16[1024,2048]{1,0:T(8,128)(2,1)} fusion(bf16[1024,1024]{1,0:T(8,128)(2,1)S(1)} %copy-done.56, bf16[1024,2048]{1,0:T(8,128)(2,1)S(1)} %copy-done.21), kind=kOutput, calls=%fused_computation.21 | convolution fusion | flops 4297064448 | bytes 10485760 | tf_op jit(solution)/shard_map/dot_general | solution.py:511
  335.1 24.8 %reduce-scatter.7.cloned.1.call-done = bf16[128,2048]{1,0:T(8,128)(2,1)} async-done(((bf16[1024,2048]{1,0:T(8,128)(2,1)}), bf16[128,2048]{1,0:T(8,128)(2,1)}) %reduce-scatter.7.cloned.1.call-update) | async-done | bytes 524304 | tf_op jit(solution)/shard_map/reduce_scatter | solution.py:374
  361.1 10.1 %collective-permute-done.22 = bf16[512,2048]{1,0:T(8,128)(2,1)} collective-permute-done((bf16[512,2048]{1,0:T(8,128)(2,1)}, bf16[512,2048]{1,0:T(8,128)(2,1)}, u32[]{:S(2)}, u32[]{:S(2)}) %collective-permute-start.22) | collective-permute-done | bytes 2097184 | tf_op jit(solution)/shard_map/ppermute | solution.py:409
  374.0 5.6 add_convert_fusion.1
  381.3 3.0 collective-permute-start.25
  384.3 3.6 fusion.36
  387.9 29.7 %collective-permute-done.25 = bf16[256,2048]{1,0:T(8,128)(2,1)} collective-permute-done((bf16[256,2048]{1,0:T(8,128)(2,1)S(1)}, bf16[256,2048]{1,0:T(8,128)(2,1)}, u32[]{:S(2)}, u32[]{:S(2)}) %collective-permute-start.25) | collective-permute-done | bytes 1048608 | tf_op jit(solution)/shard_map/ppermute | solution.py:380
  429.9 13.2 %collective-permute-start.28 = (bf16[256,2048]{1,0:T(8,128)(2,1)}, bf16[256,2048]{1,0:T(8,128)(2,1)S(1)}, u32[]{:S(2)}, u32[]{:S(2)}) collective-permute-start(bf16[256,2048]{1,0:T(8,128)(2,1)} %collective-permute-done.27), channel_id=1, source_target_pairs={{0,1},{1,0},{2,3},{3,2},{4,5},{5,4},{6,7},{7,6},{8,9},{9,8},{10,11... | collective-permute-start | bytes 3145736 | tf_op jit(solution)/shard_map/ppermute | solution.py:366
  448.7 10.2 %collective-permute-start.30 = (bf16[256,2048]{1,0:T(8,128)(2,1)S(1)}, bf16[256,2048]{1,0:T(8,128)(2,1)S(1)}, u32[]{:S(2)}, u32[]{:S(2)}) collective-permute-start(bf16[256,2048]{1,0:T(8,128)(2,1)S(1)} %collective-permute-done.29), channel_id=1, source_target_pairs={{0,1},{1,0},{2,3},{3,2},{4,5},{5,4},{6,7},{7,6},{8,9},{9,8},{10,11... | collective-permute-start | bytes 3145736 | tf_op jit(solution)/shard_map/ppermute | solution.py:366
  465.8 3.9 collective-permute-start.48
  470.3 3.5 multiply_reduce_fusion.1
  484.8 5.5 convolution_convert_fusion
  490.3 3.6 fusion.80
  495.5 3.7 fusion.9
  502.4 14.6 %collective-permute-done.37 = bf16[64,2048]{1,0:T(8,128)(2,1)S(1)} collective-permute-done((bf16[64,2048]{1,0:T(8,128)(2,1)S(1)}, bf16[64,2048]{1,0:T(8,128)(2,1)S(1)}, u32[]{:S(2)}, u32[]{:S(2)}) %collective-permute-start.37) | collective-permute-done | bytes 262176 | tf_op jit(solution)/shard_map/ppermute | solution.py:409
  529.3 2.8 copy.51
  533.3 3.4 reshape.154
  536.7 3.0 copy.52
  552.3 4.1 collective-permute-done.40
  557.3 11.5 %collective-permute-start.41 = (bf16[4,64,512]{2,1,0:T(8,128)(2,1)S(1)}, bf16[4,64,512]{2,1,0:T(8,128)(2,1)S(1)}, u32[]{:S(2)}, u32[]{:S(2)}) collective-permute-start(bf16[4,64,512]{2,1,0:T(8,128)(2,1)S(1)} %pad_maximum_fusion.22), channel_id=1, source_target_pairs={{0,1},{1,0},{2,3},{3,2},{4,5},{5,4},{6,7},{7,6},{8,9},{9,8},{10,11... | collective-permute-start | bytes 786440 | tf_op jit(solution)/shard_map/ppermute | solution.py:366
  568.9 4.4 fusion.8
  573.3 5.9 collective-permute-start.44
  580.0 7.5 %collective-permute-done.42 = bf16[128,512]{1,0:T(8,128)(2,1)S(1)} collective-permute-done((bf16[128,512]{1,0:T(8,128)(2,1)S(1)}, bf16[128,512]{1,0:T(8,128)(2,1)S(1)}, u32[]{:S(2)}, u32[]{:S(2)}) %collective-permute-start.42) | collective-permute-done | bytes 131104 | tf_op jit(solution)/shard_map/ppermute | solution.py:414
  587.5 3.6 collective-permute-done.43
  (391 shorter events, 166.9 us)
Async XLA Ops:
  7.2 75.2 %all-gather.4.cloned.1.call-start = ((), (), s32[]{:S(2)}) async-start(), calls=%async_computation.4 | async-start | bytes 4718592 | tf_op jit(solution)/shard_map/all_gather | solution.py:370
  10.8 154.6 %all-gather.6.cloned.1.call-start = ((), (), s32[]{:S(2)}) async-start(), calls=%async_computation.5 | async-start | bytes 4718592 | tf_op jit(solution)/shard_map/all_gather | solution.py:370
  27.2 45.9 %collective-permute-start.7 = (bf16[4,64,2048]{2,1,0:T(8,128)(2,1)S(1)}, bf16[4,64,2048]{2,1,0:T(8,128)(2,1)}, u32[]{:S(2)}, u32[]{:S(2)}) collective-permute-start(bf16[4,64,2048]{2,1,0:T(8,128)(2,1)S(1)} %pad_maximum_fusion.3), channel_id=1, source_target_pairs={{0,1},{1,0},{2,3},{3,2},{4,5},{5,4},{6,7},{7,6},{8,9},{9,8},{10,11... | collective-permute-start | bytes 3145736 | tf_op jit(solution)/shard_map/ppermute | solution.py:366
  27.7 12.2 %collective-permute-start.1 = (bf16[128,512]{1,0:T(8,128)(2,1)}, bf16[128,512]{1,0:T(8,128)(2,1)}, u32[]{:S(2)}, u32[]{:S(2)}) collective-permute-start(bf16[128,512]{1,0:T(8,128)(2,1)} %pad_maximum_fusion.24), channel_id=1, source_target_pairs={{0,2},{1,3},{2,4},{3,5},{4,6},{5,7},{6,0},{7,1},{8,10},{9,11},{10,... | collective-permute-start | bytes 393224 | tf_op jit(solution)/shard_map/ppermute | solution.py:414
  30.4 29.2 %collective-permute-start.3 = (bf16[128,512]{1,0:T(8,128)(2,1)S(1)}, bf16[128,512]{1,0:T(8,128)(2,1)S(1)}, u32[]{:S(2)}, u32[]{:S(2)}) collective-permute-start(bf16[128,512]{1,0:T(8,128)(2,1)S(1)} %pad_maximum_fusion.26), channel_id=1, source_target_pairs={{0,6},{1,7},{2,0},{3,1},{4,2},{5,3},{6,4},{7,5},{8,14},{9,15},{10,... | collective-permute-start | bytes 393224 | tf_op jit(solution)/shard_map/ppermute | solution.py:414
  32.5 27.1 %collective-permute-start.2 = (bf16[128,512]{1,0:T(8,128)(2,1)S(1)}, bf16[128,512]{1,0:T(8,128)(2,1)S(1)}, u32[]{:S(2)}, u32[]{:S(2)}) collective-permute-start(bf16[128,512]{1,0:T(8,128)(2,1)S(1)} %pad_maximum_fusion.25), channel_id=1, source_target_pairs={{0,4},{1,5},{2,6},{3,7},{4,0},{5,1},{6,2},{7,3},{8,12},{9,13},{10,... | collective-permute-start | bytes 393224 | tf_op jit(solution)/shard_map/ppermute | solution.py:414
  59.7 13.4 %collective-permute-start.4 = (bf16[512,512]{1,0:T(8,128)(2,1)S(1)}, bf16[512,512]{1,0:T(8,128)(2,1)S(1)}, u32[]{:S(2)}, u32[]{:S(2)}) collective-permute-start(bf16[512,512]{1,0:T(8,128)(2,1)S(1)} %constant_dynamic-update-slice_fusion.26), channel_id=1, source_target_pairs={{0,8},{1,17},{2,10},{3,19},{4,12},{5,21},{6,14},{7,23},{8,0},{9,25... | collective-permute-start | bytes 1572872 | tf_op jit(solution)/shard_map/ppermute | solution.py:409
  62.3 14.9 %collective-permute-start.6 = (bf16[64,2048]{1,0:T(8,128)(2,1)S(1)}, bf16[64,2048]{1,0:T(8,128)(2,1)S(1)}, u32[]{:S(2)}, u32[]{:S(2)}) collective-permute-start(bf16[64,2048]{1,0:T(8,128)(2,1)S(1)} %convert_element_type.284), channel_id=1, source_target_pairs={{0,0},{1,8},{2,16},{3,24},{4,1},{5,9},{6,17},{7,25},{8,2},{9,10},{... | collective-permute-start | bytes 786440 | tf_op jit(solution)/shard_map/ppermute | solution.py:540
  82.4 143.7 %reduce-scatter.5.cloned.1.call-start = ((), (), s32[]{:S(2)}) async-start(), calls=%async_computation.6 | async-start | bytes 4718592 | tf_op jit(solution)/shard_map/reduce_scatter | solution.py:374
  82.6 14.1 %collective-permute-start.8 = (bf16[512,512]{1,0:T(8,128)(2,1)S(1)}, bf16[512,512]{1,0:T(8,128)(2,1)S(1)}, u32[]{:S(2)}, u32[]{:S(2)}) collective-permute-start(bf16[512,512]{1,0:T(8,128)(2,1)S(1)} %copy-done.50), channel_id=1, source_target_pairs={{0,16},{1,9},{2,18},{3,11},{4,20},{5,13},{6,22},{7,15},{8,24},{9,1... | collective-permute-start | bytes 1572872 | tf_op jit(solution)/shard_map/ppermute | solution.py:409
  97.9 14.1 %collective-permute-start.10 = (bf16[64,2048]{1,0:T(8,128)(2,1)S(1)}, bf16[64,2048]{1,0:T(8,128)(2,1)S(1)}, u32[]{:S(2)}, u32[]{:S(2)}) collective-permute-start(bf16[64,2048]{1,0:T(8,128)(2,1)S(1)} %collective-permute-done.6), channel_id=1, source_target_pairs={{0,8},{1,17},{2,10},{3,19},{4,12},{5,21},{6,14},{7,23},{8,0},{9,25... | collective-permute-start | bytes 786440 | tf_op jit(solution)/shard_map/ppermute | solution.py:409
  99.1 13.1 %collective-permute-start.11 = (bf16[64,2048]{1,0:T(8,128)(2,1)S(1)}, bf16[64,2048]{1,0:T(8,128)(2,1)S(1)}, u32[]{:S(2)}, u32[]{:S(2)}) collective-permute-start(bf16[64,2048]{1,0:T(8,128)(2,1)S(1)} %collective-permute-done.6), channel_id=1, source_target_pairs={{0,16},{1,9},{2,18},{3,11},{4,20},{5,13},{6,22},{7,15},{8,24},{9,1... | collective-permute-start | bytes 786440 | tf_op jit(solution)/shard_map/ppermute | solution.py:409
  101.5 63.8 %collective-permute-start.13 = (bf16[256,2048]{1,0:T(8,128)(2,1)}, bf16[256,2048]{1,0:T(8,128)(2,1)S(1)}, u32[]{:S(2)}, u32[]{:S(2)}) collective-permute-start(bf16[256,2048]{1,0:T(8,128)(2,1)} %convert_element_type.285), channel_id=1, source_target_pairs={{0,8},{1,17},{2,10},{3,19},{4,12},{5,21},{6,14},{7,23},{8,0},{9,25... | collective-permute-start | bytes 3145736 | tf_op jit(solution)/shard_map/ppermute | solution.py:409
  102.5 62.9 %collective-permute-start.14 = (bf16[256,2048]{1,0:T(8,128)(2,1)}, bf16[256,2048]{1,0:T(8,128)(2,1)}, u32[]{:S(2)}, u32[]{:S(2)}) collective-permute-start(bf16[256,2048]{1,0:T(8,128)(2,1)} %convert_element_type.285), channel_id=1, source_target_pairs={{0,16},{1,9},{2,18},{3,11},{4,20},{5,13},{6,22},{7,15},{8,24},{9,1... | collective-permute-start | bytes 3145736 | tf_op jit(solution)/shard_map/ppermute | solution.py:409
  112.1 28.2 %collective-permute-start.15 = (bf16[128,2048]{1,0:T(8,128)(2,1)}, bf16[128,2048]{1,0:T(8,128)(2,1)}, u32[]{:S(2)}, u32[]{:S(2)}) collective-permute-start(bf16[128,2048]{1,0:T(8,128)(2,1)} %pad_maximum_fusion.11), channel_id=1, source_target_pairs={{0,2},{1,3},{2,4},{3,5},{4,6},{5,7},{6,0},{7,1},{8,10},{9,11},{10,... | collective-permute-start | bytes 1572872 | tf_op jit(solution)/shard_map/ppermute | solution.py:414
  112.2 53.2 %collective-permute-start.16 = (bf16[128,2048]{1,0:T(8,128)(2,1)}, bf16[128,2048]{1,0:T(8,128)(2,1)}, u32[]{:S(2)}, u32[]{:S(2)}) collective-permute-start(bf16[128,2048]{1,0:T(8,128)(2,1)} %pad_maximum_fusion.12), channel_id=1, source_target_pairs={{0,4},{1,5},{2,6},{3,7},{4,0},{5,1},{6,2},{7,3},{8,12},{9,13},{10,... | collective-permute-start | bytes 1572872 | tf_op jit(solution)/shard_map/ppermute | solution.py:414
  113.8 13.8 %collective-permute-start.12 = (bf16[64,2048]{1,0:T(8,128)(2,1)S(1)}, bf16[64,2048]{1,0:T(8,128)(2,1)S(1)}, u32[]{:S(2)}, u32[]{:S(2)}) collective-permute-start(bf16[64,2048]{1,0:T(8,128)(2,1)S(1)} %collective-permute-done.10), channel_id=1, source_target_pairs={{0,16},{1,9},{2,18},{3,11},{4,20},{5,13},{6,22},{7,15},{8,24},{9,1... | collective-permute-start | bytes 786440 | tf_op jit(solution)/shard_map/ppermute | solution.py:409
  127.6 37.8 %collective-permute-start.17 = (bf16[128,2048]{1,0:T(8,128)(2,1)}, bf16[128,2048]{1,0:T(8,128)(2,1)S(1)}, u32[]{:S(2)}, u32[]{:S(2)}) collective-permute-start(bf16[128,2048]{1,0:T(8,128)(2,1)} %pad_maximum_fusion.13), channel_id=1, source_target_pairs={{0,6},{1,7},{2,0},{3,1},{4,2},{5,3},{6,4},{7,5},{8,14},{9,15},{10,... | collective-permute-start | bytes 1572872 | tf_op jit(solution)/shard_map/ppermute | solution.py:414
  166.2 112.4 %all-gather.8.cloned.1.call-start = ((), (), s32[]{:S(2)}) async-start(), calls=%async_computation.7 | async-start | bytes 4718592 | tf_op jit(solution)/shard_map/all_gather | solution.py:370
  173.2 56.4 %collective-permute-start.18 = (bf16[512,2048]{1,0:T(8,128)(2,1)}, bf16[512,2048]{1,0:T(8,128)(2,1)}, u32[]{:S(2)}, u32[]{:S(2)}) collective-permute-start(bf16[512,2048]{1,0:T(8,128)(2,1)} %constant_dynamic-update-slice_fusion.18), channel_id=1, source_target_pairs={{0,8},{1,17},{2,10},{3,19},{4,12},{5,21},{6,14},{7,23},{8,0},{9,25... | collective-permute-start | bytes 6291464 | tf_op jit(solution)/shard_map/ppermute | solution.py:409
  174.6 55.0 %collective-permute-start.19 = (bf16[512,2048]{1,0:T(8,128)(2,1)}, bf16[512,2048]{1,0:T(8,128)(2,1)}, u32[]{:S(2)}, u32[]{:S(2)}) collective-permute-start(bf16[512,2048]{1,0:T(8,128)(2,1)} %constant_dynamic-update-slice_fusion.18), channel_id=1, source_target_pairs={{0,16},{1,9},{2,18},{3,11},{4,20},{5,13},{6,22},{7,15},{8,24},{9,1... | collective-permute-start | bytes 6291464 | tf_op jit(solution)/shard_map/ppermute | solution.py:409
  229.6 130.3 %reduce-scatter.7.cloned.1.call-start = ((), (), s32[]{:S(2)}) async-start(), calls=%async_computation.8 | async-start | bytes 4718592 | tf_op jit(solution)/shard_map/reduce_scatter | solution.py:374
  231.6 14.9 %collective-permute-start.21 = (bf16[256,2048]{1,0:T(8,128)(2,1)S(1)}, bf16[256,2048]{1,0:T(8,128)(2,1)S(1)}, u32[]{:S(2)}, u32[]{:S(2)}) collective-permute-start(bf16[256,2048]{1,0:T(8,128)(2,1)S(1)} %copy-done.33), channel_id=1, source_target_pairs={{0,16},{1,9},{2,18},{3,11},{4,20},{5,13},{6,22},{7,15},{8,24},{9,1... | collective-permute-start | bytes 3145736 | tf_op jit(solution)/shard_map/ppermute | solution.py:409
  233.2 35.7 %collective-permute-start.20 = (bf16[512,2048]{1,0:T(8,128)(2,1)}, bf16[512,2048]{1,0:T(8,128)(2,1)S(1)}, u32[]{:S(2)}, u32[]{:S(2)}) collective-permute-start(bf16[512,2048]{1,0:T(8,128)(2,1)} %collective-permute-done.18), channel_id=1, source_target_pairs={{0,16},{1,9},{2,18},{3,11},{4,20},{5,13},{6,22},{7,15},{8,24},{9,1... | collective-permute-start | bytes 6291464 | tf_op jit(solution)/shard_map/ppermute | solution.py:409
  311.0 152.6 %reduce-scatter.9.cloned.1.call-start = ((), (), s32[]{:S(2)}) async-start(), calls=%async_computation.9 | async-start | bytes 4718592 | tf_op jit(solution)/shard_map/reduce_scatter | solution.py:374
  322.4 38.7 %collective-permute-start.23 = (bf16[512,2048]{1,0:T(8,128)(2,1)}, bf16[512,2048]{1,0:T(8,128)(2,1)}, u32[]{:S(2)}, u32[]{:S(2)}) collective-permute-start(bf16[512,2048]{1,0:T(8,128)(2,1)} %convolution_convert_fusion.4), channel_id=1, source_target_pairs={{0,16},{1,9},{2,18},{3,11},{4,20},{5,13},{6,22},{7,15},{8,24},{9,1... | collective-permute-start | bytes 6291464 | tf_op jit(solution)/shard_map/ppermute | solution.py:409
  323.9 47.3 %collective-permute-start.22 = (bf16[512,2048]{1,0:T(8,128)(2,1)}, bf16[512,2048]{1,0:T(8,128)(2,1)}, u32[]{:S(2)}, u32[]{:S(2)}) collective-permute-start(bf16[512,2048]{1,0:T(8,128)(2,1)} %convolution_convert_fusion.5), channel_id=1, source_target_pairs={{0,16},{1,9},{2,18},{3,11},{4,20},{5,13},{6,22},{7,15},{8,24},{9,1... | collective-permute-start | bytes 6291464 | tf_op jit(solution)/shard_map/ppermute | solution.py:409
  373.9 220.7 %reduce-scatter.11.cloned.1.call-start = ((), (), s32[]{:S(2)}) async-start(), calls=%async_computation.10 | async-start | bytes 4718592 | tf_op jit(solution)/shard_map/reduce_scatter | solution.py:374
  379.6 42.2 %collective-permute-start.33 = (bf16[512,2048]{1,0:T(8,128)(2,1)S(1)}, bf16[512,2048]{1,0:T(8,128)(2,1)S(1)}, u32[]{:S(2)}, u32[]{:S(2)}) collective-permute-start(bf16[512,2048]{1,0:T(8,128)(2,1)S(1)} %add_convert_fusion.1), channel_id=1, source_target_pairs={{0,8},{1,17},{2,10},{3,19},{4,12},{5,21},{6,14},{7,23},{8,0},{9,25... | collective-permute-start | bytes 6291464 | tf_op jit(solution)/shard_map/ppermute | solution.py:409
  381.3 36.3 %collective-permute-start.25 = (bf16[256,2048]{1,0:T(8,128)(2,1)S(1)}, bf16[256,2048]{1,0:T(8,128)(2,1)}, u32[]{:S(2)}, u32[]{:S(2)}) collective-permute-start(bf16[256,2048]{1,0:T(8,128)(2,1)S(1)} %pad_maximum_fusion.5), channel_id=1, source_target_pairs={{0,2},{2,4},{4,6},{7,5},{5,3},{3,1},{8,10},{10,12},{12,14},{15,13}... | collective-permute-start | bytes 3145736 | tf_op jit(solution)/shard_map/ppermute | solution.py:380
  417.6 25.5 %collective-permute-start.26 = (bf16[256,2048]{1,0:T(8,128)(2,1)}, bf16[256,2048]{1,0:T(8,128)(2,1)}, u32[]{:S(2)}, u32[]{:S(2)}) collective-permute-start(bf16[256,2048]{1,0:T(8,128)(2,1)} %collective-permute-done.25), channel_id=1, source_target_pairs={{0,1},{1,0},{2,3},{3,2},{4,5},{5,4},{6,7},{7,6},{8,9},{9,8},{10,11... | collective-permute-start | bytes 3145736 | tf_op jit(solution)/shard_map/ppermute | solution.py:366
  425.8 20.7 %collective-permute-start.34 = (bf16[4,64,2048]{2,1,0:T(8,128)(2,1)}, bf16[4,64,2048]{2,1,0:T(8,128)(2,1)}, u32[]{:S(2)}, u32[]{:S(2)}) collective-permute-start(bf16[4,64,2048]{2,1,0:T(8,128)(2,1)} %pad_maximum_fusion.6), channel_id=1, source_target_pairs={{0,1},{1,0},{2,3},{3,2},{4,5},{5,4},{6,7},{7,6},{8,9},{9,8},{10,11... | collective-permute-start | bytes 3145736 | tf_op jit(solution)/shard_map/ppermute | solution.py:366
  425.8 40.0 %collective-permute-start.31 = (bf16[256,2048]{1,0:T(8,128)(2,1)}, bf16[256,2048]{1,0:T(8,128)(2,1)}, u32[]{:S(2)}, u32[]{:S(2)}) collective-permute-start(bf16[256,2048]{1,0:T(8,128)(2,1)} %convolution_convert_fusion.7), channel_id=1, source_target_pairs={{0,16},{1,9},{2,18},{3,11},{4,20},{5,13},{6,22},{7,15},{8,24},{9,1... | collective-permute-start | bytes 3145736 | tf_op jit(solution)/shard_map/ppermute | solution.py:409
  426.4 39.3 %collective-permute-start.32 = (bf16[256,2048]{1,0:T(8,128)(2,1)}, bf16[256,2048]{1,0:T(8,128)(2,1)}, u32[]{:S(2)}, u32[]{:S(2)}) collective-permute-start(bf16[256,2048]{1,0:T(8,128)(2,1)} %convolution_convert_fusion.6), channel_id=1, source_target_pairs={{0,16},{1,9},{2,18},{3,11},{4,20},{5,13},{6,22},{7,15},{8,24},{9,1... | collective-permute-start | bytes 3145736 | tf_op jit(solution)/shard_map/ppermute | solution.py:409
  429.9 30.7 %collective-permute-start.28 = (bf16[256,2048]{1,0:T(8,128)(2,1)}, bf16[256,2048]{1,0:T(8,128)(2,1)S(1)}, u32[]{:S(2)}, u32[]{:S(2)}) collective-permute-start(bf16[256,2048]{1,0:T(8,128)(2,1)} %collective-permute-done.27), channel_id=1, source_target_pairs={{0,1},{1,0},{2,3},{3,2},{4,5},{5,4},{6,7},{7,6},{8,9},{9,8},{10,11... | collective-permute-start | bytes 3145736 | tf_op jit(solution)/shard_map/ppermute | solution.py:366
  448.7 12.5 %collective-permute-start.30 = (bf16[256,2048]{1,0:T(8,128)(2,1)S(1)}, bf16[256,2048]{1,0:T(8,128)(2,1)S(1)}, u32[]{:S(2)}, u32[]{:S(2)}) collective-permute-start(bf16[256,2048]{1,0:T(8,128)(2,1)S(1)} %collective-permute-done.29), channel_id=1, source_target_pairs={{0,1},{1,0},{2,3},{3,2},{4,5},{5,4},{6,7},{7,6},{8,9},{9,8},{10,11... | collective-permute-start | bytes 3145736 | tf_op jit(solution)/shard_map/ppermute | solution.py:366
  465.8 53.4 %collective-permute-start.47 = (bf16[128,2048]{1,0:T(8,128)(2,1)}, bf16[128,2048]{1,0:T(8,128)(2,1)}, u32[]{:S(2)}, u32[]{:S(2)}) collective-permute-start(bf16[128,2048]{1,0:T(8,128)(2,1)} %pad_maximum_fusion.16), channel_id=1, source_target_pairs={{0,2},{1,3},{2,4},{3,5},{4,6},{5,7},{6,0},{7,1},{8,10},{9,11},{10,... | collective-permute-start | bytes 1572872 | tf_op jit(solution)/shard_map/ppermute | solution.py:414
  465.8 55.9 %collective-permute-start.48 = (bf16[128,2048]{1,0:T(8,128)(2,1)}, bf16[128,2048]{1,0:T(8,128)(2,1)}, u32[]{:S(2)}, u32[]{:S(2)}) collective-permute-start(bf16[128,2048]{1,0:T(8,128)(2,1)} %pad_maximum_fusion.17), channel_id=1, source_target_pairs={{0,4},{1,5},{2,6},{3,7},{4,0},{5,1},{6,2},{7,3},{8,12},{9,13},{10,... | collective-permute-start | bytes 1572872 | tf_op jit(solution)/shard_map/ppermute | solution.py:414
  469.8 53.1 %collective-permute-start.49 = (bf16[128,2048]{1,0:T(8,128)(2,1)}, bf16[128,2048]{1,0:T(8,128)(2,1)}, u32[]{:S(2)}, u32[]{:S(2)}) collective-permute-start(bf16[128,2048]{1,0:T(8,128)(2,1)} %pad_maximum_fusion.18), channel_id=1, source_target_pairs={{0,6},{1,7},{2,0},{3,1},{4,2},{5,3},{6,4},{7,5},{8,14},{9,15},{10,... | collective-permute-start | bytes 1572872 | tf_op jit(solution)/shard_map/ppermute | solution.py:414
  499.2 69.6 %collective-permute-start.50 = (bf16[256,2048]{1,0:T(8,128)(2,1)}, bf16[256,2048]{1,0:T(8,128)(2,1)}, u32[]{:S(2)}, u32[]{:S(2)}) collective-permute-start(bf16[256,2048]{1,0:T(8,128)(2,1)} %fusion.9), channel_id=1, source_target_pairs={{0,8},{1,17},{2,10},{3,19},{4,12},{5,21},{6,14},{7,23},{8,0},{9,25... | collective-permute-start | bytes 3145736 | tf_op jit(solution)/shard_map/ppermute | solution.py:409
  500.8 16.2 %collective-permute-start.37 = (bf16[64,2048]{1,0:T(8,128)(2,1)S(1)}, bf16[64,2048]{1,0:T(8,128)(2,1)S(1)}, u32[]{:S(2)}, u32[]{:S(2)}) collective-permute-start(bf16[64,2048]{1,0:T(8,128)(2,1)S(1)} %add_convert_fusion.5), channel_id=1, source_target_pairs={{0,8},{1,17},{2,10},{3,19},{4,12},{5,21},{6,14},{7,23},{8,0},{9,25... | collective-permute-start | bytes 786440 | tf_op jit(solution)/shard_map/ppermute | solution.py:409
  517.0 24.6 %collective-permute-start.45 = (bf16[64,2048]{1,0:T(8,128)(2,1)S(1)}, bf16[64,2048]{1,0:T(8,128)(2,1)}, u32[]{:S(2)}, u32[]{:S(2)}) collective-permute-start(bf16[64,2048]{1,0:T(8,128)(2,1)S(1)} %get-tuple-element.136), channel_id=1, source_target_pairs={{0,16},{1,9},{2,18},{3,11},{4,20},{5,13},{6,22},{7,15},{8,24},{9,1... | collective-permute-start | bytes 786440 | tf_op jit(solution)/shard_map/ppermute | solution.py:409
  519.2 24.3 %collective-permute-start.39 = (bf16[512,512]{1,0:T(8,128)(2,1)}, bf16[512,512]{1,0:T(8,128)(2,1)}, u32[]{:S(2)}, u32[]{:S(2)}) collective-permute-start(bf16[512,512]{1,0:T(8,128)(2,1)} %convolution_convert_fusion.8), channel_id=1, source_target_pairs={{0,16},{1,9},{2,18},{3,11},{4,20},{5,13},{6,22},{7,15},{8,24},{9,1... | collective-permute-start | bytes 1572872 | tf_op jit(solution)/shard_map/ppermute | solution.py:409
  541.0 11.4 %collective-permute-start.38 = (bf16[512,512]{1,0:T(8,128)(2,1)S(1)}, bf16[512,512]{1,0:T(8,128)(2,1)S(1)}, u32[]{:S(2)}, u32[]{:S(2)}) collective-permute-start(bf16[512,512]{1,0:T(8,128)(2,1)S(1)} %copy-done.64), channel_id=1, source_target_pairs={{0,16},{1,9},{2,18},{3,11},{4,20},{5,13},{6,22},{7,15},{8,24},{9,1... | collective-permute-start | bytes 1572872 | tf_op jit(solution)/shard_map/ppermute | solution.py:409
  545.4 11.1 %collective-permute-start.40 = (bf16[512,512]{1,0:T(8,128)(2,1)S(1)}, bf16[512,512]{1,0:T(8,128)(2,1)S(1)}, u32[]{:S(2)}, u32[]{:S(2)}) collective-permute-start(bf16[512,512]{1,0:T(8,128)(2,1)S(1)} %fusion.22), channel_id=1, source_target_pairs={{0,8},{1,17},{2,10},{3,19},{4,12},{5,21},{6,14},{7,23},{8,0},{9,25... | collective-permute-start | bytes 1572872 | tf_op jit(solution)/shard_map/ppermute | solution.py:409
  557.3 15.9 %collective-permute-start.41 = (bf16[4,64,512]{2,1,0:T(8,128)(2,1)S(1)}, bf16[4,64,512]{2,1,0:T(8,128)(2,1)S(1)}, u32[]{:S(2)}, u32[]{:S(2)}) collective-permute-start(bf16[4,64,512]{2,1,0:T(8,128)(2,1)S(1)} %pad_maximum_fusion.22), channel_id=1, source_target_pairs={{0,1},{1,0},{2,3},{3,2},{4,5},{5,4},{6,7},{7,6},{8,9},{9,8},{10,11... | collective-permute-start | bytes 786440 | tf_op jit(solution)/shard_map/ppermute | solution.py:366
  573.3 17.8 %collective-permute-start.44 = (bf16[128,512]{1,0:T(8,128)(2,1)S(1)}, bf16[128,512]{1,0:T(8,128)(2,1)S(1)}, u32[]{:S(2)}, u32[]{:S(2)}) collective-permute-start(bf16[128,512]{1,0:T(8,128)(2,1)S(1)} %pad_maximum_fusion.29), channel_id=1, source_target_pairs={{0,6},{1,7},{2,0},{3,1},{4,2},{5,3},{6,4},{7,5},{8,14},{9,15},{10,... | collective-permute-start | bytes 393224 | tf_op jit(solution)/shard_map/ppermute | solution.py:414
  579.3 11.8 %collective-permute-start.43 = (bf16[128,512]{1,0:T(8,128)(2,1)S(1)}, bf16[128,512]{1,0:T(8,128)(2,1)S(1)}, u32[]{:S(2)}, u32[]{:S(2)}) collective-permute-start(bf16[128,512]{1,0:T(8,128)(2,1)S(1)} %pad_maximum_fusion.28), channel_id=1, source_target_pairs={{0,4},{1,5},{2,6},{3,7},{4,0},{5,1},{6,2},{7,3},{8,12},{9,13},{10,... | collective-permute-start | bytes 393224 | tf_op jit(solution)/shard_map/ppermute | solution.py:414
  (78 other events, 500.5 us)
Sparse Core Ops, SparseCore 0:
  10.9 69.2 all-gather.3
  82.5 80.8 all-gather.5
  166.3 59.7 reduce-scatter.4
  229.7 48.7 all-gather.7
  311.2 48.7 reduce-scatter.6
  374.0 59.9 reduce-scatter.8
  490.4 63.2 reduce-scatter.10

commit v3 on v2

--- a/solution.py
+++ b/solution.py
@@ -1,6 +1,8 @@
 import jax
 import jax.numpy as jnp
 from jax import lax
+from jax.experimental import pallas as pl
+from jax.experimental.pallas import tpu as pltpu
 from jax.sharding import PartitionSpec as P
 
 FF = 8192
@@ -380,38 +382,28 @@
     return lax.ppermute(values, "ctx", moves)
 
 
-def pass_along(rows, *first):
-    other = swap_cores(rows)
-    even = is_even()
-    pair = jnp.concatenate([jnp.where(even, rows, other), jnp.where(even, other, rows)], axis=0)
-    held = [after(pair, *first)]
-    for step in range(1, N_Z):
-        held.append(hop(held[-1], step - 1, N_Z - 2))
-    return held
-
-
-def place_passed(held):
-    z, even = lax.axis_index("ctx") // 2, is_even()
-    size = held[0].shape[0]
-    whole = jnp.zeros(((N_Z + 1) * size,) + held[0].shape[1:], held[0].dtype)
-    whole = lax.dynamic_update_slice_in_dim(whole, held[0], z * size, 0)
-    for step in range(1, N_Z):
-        for block, up in ((held[step], even), (swap_cores(held[step]), ~even)):
-            place = jnp.where(up, z - step, z + step)
-            place = jnp.where((place >= 0) & (place < N_Z), place, N_Z)
-            whole = lax.dynamic_update_slice_in_dim(whole, block, place * size, 0)
-    return whole[: N_Z * size]
+def sum_step(slots, carried, step):
+    low, wide = jnp.bfloat16, jnp.float32
+    keep = jnp.where(is_even(), slots[step], slots[N_Z - step])
+    give = jnp.where(is_even(), slots[N_Z - step], slots[step])
+    total = keep.astype(wide) + swap_cores(give).astype(wide)
+    if carried is not None:
+        total = total + carried.astype(wide)
+    return hop(total.astype(low), 0, N_Z - 1 - step)
+
+
+def sum_end(slots, carried):
+    low, wide = jnp.bfloat16, jnp.float32
+    total = slots[0].astype(wide) + carried.astype(wide)
+    half = total.shape[0] // 2
+    give = jnp.where(is_even(), total[half:], total[:half]).astype(low)
+    return jnp.where(is_even(), total[:half], total[half:]) + swap_cores(give).astype(wide)
 
 
 def send_dp(values, first, second):
     moves = [(d, c, d ^ (second if c % 2 else first)) for d in range(4) for c in range(2 * N_Z)]
     moves = [(d * 2 * N_Z + c, to * 2 * N_Z + c) for d, c, to in moves]
     return lax.ppermute(values, ("dp", "ctx"), moves)
-
-
-def rotate_z(values, step):
-    moves = [(2 * a + t, 2 * ((a + step) % N_Z) + t) for a in range(N_Z) for t in range(2)]
-    return lax.ppermute(values, "ctx", moves)
 
 
 def is_even():
@@ -442,37 +434,86 @@
     return jnp.concatenate([rows, one, two, third], axis=0)
 
 
-def pick(blocks, chip, core):
-    start = (chip, core) + (0,) * (blocks.ndim - 2)
-    return lax.dynamic_slice(blocks, start, (1, 1) + blocks.shape[2:])[0, 0]
-
-
-def exchange_pairs(blocks):
-    z, core = lax.axis_index("ctx") // 2, lax.axis_index("ctx") % 2
-    give = jnp.stack([pick(blocks, (z + s) % N_Z, 1 - core) for s in range(N_Z)])
-    got = swap_cores(give)
-    pairs = []
-    for s in range(N_Z):
-        keep = pick(blocks, (z + s) % N_Z, core)
-        pairs.append(
-            jnp.concatenate(
-                [jnp.where(is_even(), keep, got[s]), jnp.where(is_even(), got[s], keep)], axis=0
-            )
-        )
-    return pairs
-
-
-def place_z(pieces):
-    z = lax.axis_index("ctx") // 2
-    size = pieces[0].shape[0]
-    whole = jnp.zeros((N_Z * size,) + pieces[0].shape[1:], pieces[0].dtype)
-    for s, piece in enumerate(pieces):
-        whole = lax.dynamic_update_slice_in_dim(whole, piece, (z - s) % N_Z * size, 0)
-    return whole
-
-
-def rotate_pieces(pairs):
-    return [pairs[0]] + [rotate_z(pairs[s], s) for s in range(1, N_Z)]
+def exchange_ctx(blocks):
+    return lax.all_to_all(blocks, "ctx", 0, 0, tiled=True)
+
+
+def finish_feedforward(sums, w_gate, w_up, gain):
+    n_ctx, rows, both = sums.shape
+    part = both // 8
+
+    def kernel(sums_ref, gate_ref, up_ref, gain_ref, gate_out, up_out, gain_out):
+        scale = gain_ref[...]
+        total = jnp.zeros((rows, part), jnp.float32)
+        for d in range(4):
+            for c in range(n_ctx):
+                place = pl.ds((d * n_ctx + c) * part, part)
+                for half, weight_ref, out_ref in ((0, gate_ref, gate_out), (1, up_ref, up_out)):
+                    raw = sums_ref[c, :, pl.ds((half * 4 + d) * part, part)].astype(jnp.float32)
+                    weight = weight_ref[:, place].astype(jnp.bfloat16).astype(jnp.float32)
+                    total = total + raw * weight
+                    out_ref[:, place] = raw * scale
+        gain_out[...] = jnp.sum(total, axis=1, keepdims=True)
+
+    return pl.pallas_call(
+        kernel,
+        out_shape=(
+            jax.ShapeDtypeStruct(w_gate.shape, jnp.float32),
+            jax.ShapeDtypeStruct(w_up.shape, jnp.float32),
+            jax.ShapeDtypeStruct((rows, 1), jnp.float32),
+        ),
+        compiler_params=pltpu.CompilerParams(vmem_limit_bytes=32 * 1024 * 1024),
+        cost_estimate=pl.CostEstimate(
+            flops=4 * w_gate.size, bytes_accessed=20 * w_gate.size, transcendentals=0
+        ),
+    )(sums, w_gate, w_up, gain)
+
+
+def feedforward(hat, weight, d_hidden):
+    rows, depth = hat.shape
+    width = weight.shape[1] // 2
+    tile, chunk = 256, 256
+    tiles = width // tile
+
+    def kernel(hat_ref, gate_ref, up_ref, grad_ref, hidden_ref, out_ref):
+        place = pl.multiple_of(pl.program_id(0) * tile, tile)
+        for start in range(0, rows, chunk):
+            part = pl.ds(start, chunk)
+            left = hat_ref[part, :]
+            gate = jnp.dot(left, gate_ref[...], preferred_element_type=jnp.float32)
+            up = jnp.dot(left, up_ref[...], preferred_element_type=jnp.float32)
+            sig = jax.nn.sigmoid(gate)
+            silu = gate * sig
+            grad = grad_ref[part, :]
+            hidden_ref[part, :] = (silu * up).astype(jnp.bfloat16)
+            d_gate = grad * up * sig * (1.0 + gate * (1.0 - sig))
+            out_ref[part, pl.ds(place, tile)] = d_gate.astype(jnp.bfloat16)
+            out_ref[part, pl.ds(width + place, tile)] = (grad * silu).astype(jnp.bfloat16)
+
+    return pl.pallas_call(
+        kernel,
+        grid=(tiles,),
+        in_specs=[
+            pl.BlockSpec((rows, depth), lambda j: (0, 0)),
+            pl.BlockSpec((depth, tile), lambda j: (0, j)),
+            pl.BlockSpec((depth, tile), lambda j: (0, tiles + j)),
+            pl.BlockSpec((rows, tile), lambda j: (0, j)),
+        ],
+        out_specs=(
+            pl.BlockSpec((rows, tile), lambda j: (0, j)),
+            pl.BlockSpec((rows, 2 * width), lambda j: (0, 0)),
+        ),
+        out_shape=(
+            jax.ShapeDtypeStruct((rows, width), jnp.bfloat16),
+            jax.ShapeDtypeStruct((rows, 2 * width), jnp.bfloat16),
+        ),
+        compiler_params=pltpu.CompilerParams(vmem_limit_bytes=44 * 1024 * 1024),
+        cost_estimate=pl.CostEstimate(
+            flops=4 * rows * depth * width,
+            bytes_accessed=2 * rows * depth + 4 * depth * width + 10 * rows * width,
+            transcendentals=rows * width,
+        ),
+    )(hat, weight, weight, d_hidden)
 
 
 def out_weight_moves():
@@ -541,35 +582,38 @@
 
     inverse1 = lax.rsqrt(jnp.mean(x_rows * x_rows, axis=-1, keepdims=True) + NORM_EPSILON)
     hat1 = x_rows * inverse1
-    sent1 = turned(hat1).astype(low)
+    sent1 = turned(layer_input[0])
 
     q_cols = (low_q * gain_a).astype(low).reshape(rows, N_Z, 2, HEAD_SIZE).transpose(1, 2, 0, 3)
     k_cols = (low_k * gain_a).astype(low).reshape(rows, N_Z, 1, HEAD_SIZE).transpose(1, 2, 0, 3)
     v_cols = (low_v * gain_a).astype(low).reshape(rows, N_Z, 1, HEAD_SIZE).transpose(1, 2, 0, 3)
     proj_blocks = jnp.concatenate([q_cols, jnp.concatenate([k_cols, v_cols], axis=1)], axis=3)
-    proj_pairs = exchange_pairs(proj_blocks)
-    proj_moved = rotate_pieces(proj_pairs)
-    all_hat1 = gather_ctx(sent1)
-    proj_own = place_z(proj_moved)
+    proj_own = exchange_ctx(proj_blocks.reshape(2 * N_Z, rows, cols))
+    all_rows = gather_ctx(sent1)
+    proj_own = proj_own.reshape(2 * N_Z * rows, cols)
     proj_first, proj_second = send_dp(proj_own, 1, 2), send_dp(proj_own, 2, 1)
-    proj_third = send_dp(proj_first, 2, 1)
-    gain_late = after(gain_m, *proj_pairs)
+    gain_late = after(gain_m, proj_own)
 
     def ff_columns(weight):
         blocks = (weight * gain_late).astype(low).reshape(rows, 4, N_Z, 2, ff_part)
         return blocks.transpose(2, 3, 0, 1, 4).reshape(N_Z, 2, rows, width)
 
-    gate_up_pairs = exchange_pairs(jnp.concatenate([ff_columns(low_g), ff_columns(low_u)], axis=3))
+    gate_up_blocks = jnp.concatenate([ff_columns(low_g), ff_columns(low_u)], axis=3)
     down_own = w_down.astype(low)
-    all_hat1, proj_third, out_own, down_own, *gate_up_pairs = lax.optimization_barrier(
-        (all_hat1, proj_third, out_own, down_own, *gate_up_pairs)
-    )
-    out_first, out_second = send_dp(out_own, 1, 2), send_dp(out_own, 2, 1)
-    out_w = place_dp(out_own, out_first, out_second, send_dp(out_first, 2, 1))
-    down_first, down_second = send_dp(down_own, 1, 2), send_dp(down_own, 2, 1)
-    all_cot = gather_ctx(after(d_out, all_hat1))
+    all_rows, out_own, down_own, gate_up_blocks, proj_first, proj_second = (
+        lax.optimization_barrier(
+            (all_rows, out_own, down_own, gate_up_blocks, proj_first, proj_second)
+        )
+    )
+    proj_third = send_dp(proj_first, 2, 1)
+    all_cot = gather_ctx(after(d_out, all_rows))
+    all_rows = all_rows.astype(wide)
+    all_hat1 = all_rows * lax.rsqrt(
+        jnp.mean(all_rows * all_rows, axis=-1, keepdims=True) + NORM_EPSILON
+    )
+    all_hat1 = all_hat1.astype(low)
     proj = stack_dp(proj_own, proj_first, proj_second, proj_third)
-    gate_up_moved = rotate_pieces(gate_up_pairs)
+    gate_up_own = exchange_ctx(gate_up_blocks.reshape(2 * N_Z, rows, 2 * width))
     positions = jnp.arange(seq_rows, dtype=jnp.int32)
     cosine, sine = rope_angles(positions, HEAD_SIZE)
     cosine, sine = cosine[:, 0], sine[:, 0]
@@ -584,6 +628,10 @@
     q_rot = (rotate(qkv[:, :HEAD_SIZE], 1.0) * scale).astype(low)
     own = qkv[:, HEAD_SIZE:]
     own = jnp.where(even, rotate(own, 1.0), own).astype(low)
+    own, q_rot, out_own, down_own = lax.optimization_barrier((own, q_rot, out_own, down_own))
+    out_first, out_second = send_dp(out_own, 1, 2), send_dp(out_own, 2, 1)
+    out_w = place_dp(out_own, out_first, out_second, send_dp(out_first, 2, 1))
+    down_first, down_second = send_dp(down_own, 1, 2), send_dp(down_own, 2, 1)
     other = swap_cores(own)
     keys = jnp.where(even, own, other)
     values = jnp.where(even, other, own)
@@ -595,10 +643,11 @@
     attended = dot(weights.astype(low), values) / total
     attn = attended.astype(low)
     branch_part = dot(attn, out_w).astype(low)
-    branch_part, down_first, down_second, all_cot, *gate_up_moved = lax.optimization_barrier(
-        (branch_part, down_first, down_second, all_cot, *gate_up_moved)
-    )
-    gate_up_own = place_z(gate_up_moved)
+    down_third = send_dp(down_first, 2, 1)
+    branch_part, all_cot, down_second, down_third, gate_up_own = lax.optimization_barrier(
+        (branch_part, all_cot, down_second, down_third, gate_up_own)
+    )
+    gate_up_own = gate_up_own.reshape(2 * N_Z * rows, 2 * width)
     branch = scatter_ctx(branch_part)
     gu_first, gu_second = send_dp(gate_up_own, 1, 2), send_dp(gate_up_own, 2, 1)
     middle = x_rows + branch
@@ -610,22 +659,13 @@
     )
     all_hat2 = gather_ctx(sent2)
     gu_third = send_dp(gu_first, 2, 1)
-    down_third = send_dp(after(down_first, gu_first), 2, 1)
     gate_up_w = stack_dp(gate_up_own, gu_first, gu_second, gu_third)
     down_w = place_dp(down_own, down_first, down_second, down_third)
     d_hidden = dot_t(all_cot, down_w)
     all_hat2, gate_up_w, down_w, all_cot, d_hidden = lax.optimization_barrier(
         (all_hat2, gate_up_w, down_w, all_cot, d_hidden)
     )
-    gate = dot(all_hat2, gate_up_w[:, :width])
-    up = dot(all_hat2, gate_up_w[:, width:])
-    sig = jax.nn.sigmoid(gate)
-    silu = gate * sig
-    hidden = (silu * up).astype(low)
-
-    d_gate = (d_hidden * up * sig * (1.0 + gate * (1.0 - sig))).astype(low)
-    d_up = (d_hidden * silu).astype(low)
-    d_gate_up = jnp.concatenate([d_gate, d_up], axis=1)
+    hidden, d_gate_up = feedforward(all_hat2, gate_up_w, d_hidden)
     e2_part = dot_t(d_gate_up, gate_up_w).astype(low)
     e2 = scatter_ctx(e2_part)
     d_gate_up, hidden = lax.optimization_barrier((d_gate_up, hidden, e2_part))[:2]
@@ -639,42 +679,51 @@
     gu_across = send_dp(gu_block(3).astype(low), 2, 1)
     gu_far = send_dp(gu_block(3 - near_bit()).astype(low), 2, 1)
     gu_near_term, gu_own_term = gu_block(near_bit()), gu_block(0)
-    out_part = dot(hidden, down_w).astype(low)
+    z = lax.axis_index("ctx") // 2
+    size = seq_rows // N_Z
+    out_slots = [
+        dot(lax.dynamic_slice_in_dim(hidden, (z + j) % N_Z * size, size, 0), down_w).astype(low)
+        for j in range(N_Z)
+    ]
+    carried = sum_step(out_slots, None, 3)
     down_sent3 = down_block(3).astype(low)
     down_sent_far = down_block(3 - near_bit()).astype(low)
-    e2, gu_across, gu_far, down_sent3, down_sent_far, out_part = lax.optimization_barrier(
-        (e2, gu_across, gu_far, down_sent3, down_sent_far, out_part)
-    )
-    gu_near = send_dp((gu_near_term + gu_across.astype(wide)).astype(low), 1, 2)
+    gu_relay = (gu_near_term + gu_across.astype(wide)).astype(low)
+    e2, gu_relay, gu_far, down_sent3, down_sent_far, carried = lax.optimization_barrier(
+        (e2, gu_relay, gu_far, down_sent3, down_sent_far, carried)
+    )
+    gu_near = send_dp(gu_relay, 1, 2)
+    gu_own_sum = gu_own_term + gu_far.astype(wide)
     down_across, down_far = send_dp(down_sent3, 2, 1), send_dp(down_sent_far, 2, 1)
     e2 = turned(e2)
     d_middle = d_out.astype(wide) + inverse2 * (
         e2 - hat2 * jnp.mean(e2 * hat2, axis=-1, keepdims=True)
     )
     branch_low = d_middle.astype(low)
-    out_branch = scatter_ctx(after(out_part, branch_low))
-    all_branch = place_passed(pass_along(branch_low))
-    gate_up_sum = (gu_own_term + gu_far.astype(wide) + gu_near.astype(wide)).astype(low)
-    sum_pairs = exchange_pairs(gate_up_sum.reshape(N_Z, 2, rows, 2 * width))
-
-    all_branch, down_across, down_far, out_branch, *sum_pairs = lax.optimization_barrier(
-        (all_branch, down_across, down_far, out_branch, *sum_pairs)
-    )
-    head_part = t_dot(attn, all_branch)
+    all_branch = gather_ctx(branch_low)
+    carried = sum_step(out_slots, carried, 2)
+    gate_up_sum = (gu_own_sum + gu_near.astype(wide)).astype(low)
+
+    gate_up_source = gate_up_sum.reshape(2 * N_Z, rows, 2 * width)
+    gate_up_sum = exchange_ctx(gate_up_source)
+    all_branch, down_across = lax.optimization_barrier((all_branch, down_across, gate_up_source))[:2]
 
     def out_block(j):
         return lax.dynamic_slice_in_dim(head_part, (d ^ j) * rows, rows, 0)
 
+    down_near = send_dp((down_block(near_bit()) + down_across.astype(wide)).astype(low), 1, 2)
+    d_attn = dot_t(all_branch, out_w).astype(low)
+    head_part = t_dot(attn, after(all_branch, d_attn))
     out_across = send_dp(out_block(3).astype(low), 2, 1)
     out_far = send_dp(out_block(3 - near_bit()).astype(low), 2, 1)
-    out_near = send_dp((out_block(near_bit()) + out_across.astype(wide)).astype(low), 1, 2)
-    down_near = send_dp((down_block(near_bit()) + down_across.astype(wide)).astype(low), 1, 2)
-    down_sum = down_block(0) + down_far.astype(wide) + down_near.astype(wide)
-    gate_up_sum = place_z(rotate_pieces(sum_pairs))
-    d_attn = dot_t(all_branch, out_w).astype(low)
     delta = jnp.sum(d_attn.astype(wide) * attended, axis=-1, keepdims=True)
     probs = weights / total
     d_scores = (probs * (dot_t(d_attn, values) - delta)).astype(low)
+    d_scores, out_across, carried, gate_up_sum = lax.optimization_barrier(
+        (d_scores, out_across, carried, gate_up_sum)
+    )
+    carried = sum_step(out_slots, carried, 1)
+    out_near = send_dp((out_block(near_bit()) + out_across.astype(wide)).astype(low), 1, 2)
     d_query = rotate(dot(d_scores, keys) * scale, -1.0)
     dk_part = t_dot(d_scores, q_rot)
     dv_part = t_dot(probs.astype(low), d_attn)
@@ -683,34 +732,36 @@
     mine = jnp.where(even, rotate(mine, -1.0), mine)
     d_proj = jnp.concatenate([d_query, mine], axis=1).astype(low)
     e1_part = dot_t(d_proj, proj).astype(low)
+    e1_part, out_near, down_near, carried = lax.optimization_barrier(
+        (e1_part, out_near, down_near, carried)
+    )
     e1 = turned(scatter_ctx(e1_part))
-    d_proj, out_near = lax.optimization_barrier((d_proj, out_near, e1_part))[:2]
-    output = (middle + out_branch).astype(low)[None]
+    d_proj = after(d_proj, e1_part)
 
     def proj_block(j):
         return t_dot(block_columns(all_hat1, j), d_proj)
 
     proj_across = send_dp(proj_block(3).astype(low), 2, 1)
     proj_far = send_dp(proj_block(3 - near_bit()).astype(low), 2, 1)
-    proj_near = send_dp((proj_block(near_bit()) + proj_across.astype(wide)).astype(low), 1, 2)
-    proj_sum = proj_block(0) + proj_far.astype(wide) + proj_near.astype(wide)
-    proj_sum = place_z(
-        rotate_pieces(exchange_pairs(proj_sum.astype(low).reshape(N_Z, 2, rows, cols)))
-    )
+    relayed = (proj_block(near_bit()) + proj_across.astype(wide)).astype(low)
+    proj_near = send_dp(relayed, 1, 2)
+    out_near = after(out_near, proj_across)
     out_sum = out_block(0) + out_far.astype(wide) + out_near.astype(wide)
     out_sum = lax.ppermute(
         out_sum.astype(low), ("dp", "ctx"), [(to, start) for start, to in moves]
-    ).astype(wide)
-
-    def ff_rows(part):
-        blocks = part.astype(wide).reshape(2 * N_Z, rows, 4, ff_part).transpose(1, 2, 0, 3)
-        return blocks.reshape(rows, 8 * N_Z * ff_part)
-
-    raw_gate = ff_rows(gate_up_sum[:, :width])
-    raw_up = ff_rows(gate_up_sum[:, width:])
-    gain_mlp = jnp.sum(raw_gate * low_g, axis=1) + jnp.sum(raw_up * low_u, axis=1)
-    gate_sum, up_sum = raw_gate * gain_m, raw_up * gain_m
-    proj_sum = proj_sum.astype(wide).reshape(2 * N_Z, rows, cols).transpose(1, 0, 2)
+    )
+    proj_sum = proj_block(0) + proj_far.astype(wide) + proj_near.astype(wide)
+    proj_sum = proj_sum.astype(low)
+    out_branch = sum_end(out_slots, after(carried, proj_sum))
+    output = (middle + out_branch).astype(low)[None]
+    proj_sum = exchange_ctx(proj_sum.reshape(2 * N_Z, rows, cols))
+    down_sum = down_block(0) + down_far.astype(wide) + down_near.astype(wide)
+    out_sum, proj_sum = lax.optimization_barrier((out_sum, proj_sum))
+    out_sum = out_sum.astype(wide)
+
+    gate_sum, up_sum, gain_mlp = finish_feedforward(gate_up_sum, w_gate, w_up, gain_m)
+    gain_mlp = gain_mlp[:, 0]
+    proj_sum = proj_sum.astype(wide).transpose(1, 0, 2)
     raw_q = proj_sum[:, :, :HEAD_SIZE].reshape(rows, QUERY_HEADS * HEAD_SIZE)
     kv_sum = proj_sum[:, :, HEAD_SIZE:].reshape(rows, KEY_VALUE_HEADS, 2, HEAD_SIZE)
     raw_k = kv_sum[:, :, 0].reshape(rows, KEY_VALUE_HEADS * HEAD_SIZE)

time: 612 us -> 573 us (0.936)
  starting transfers between devices: 101 us -> 78.7 us
  waiting for transfers between devices: 259 us -> 238 us
  Pallas kernels: 0 us -> 19.1 us
  local copies, waits for them, and re-layouts: 50.7 us -> 32.5 us
  other arithmetic: 69.5 us -> 77.4 us
    all_to_all x0 -> x4, waiting for transfers between devices: none -> 70.8 us  [exchange_ctx(): return lax.all_to_all(blocks, 'ctx', 0, 0, tiled=True)]
    ppermute x12 -> x0, waiting for transfers between devices: 67.2 us -> none  [rotate_z(): return lax.ppermute(values, 'ctx', moves)]
    ppermute x10 -> x6, starting transfers between devices: 38.6 us -> 0.53 us  [swap_cores(): return lax.ppermute(values, 'ctx', [(i, i ^ 1) for i in range(2 * N_Z)])]
    all_to_all x0 -> x4, starting transfers between devices: none -> 22.1 us  [exchange_ctx(): return lax.all_to_all(blocks, 'ctx', 0, 0, tiled=True)]
    ppermute x12 -> x0, starting transfers between devices: 20.2 us -> none  [rotate_z(): return lax.ppermute(values, 'ctx', moves)]
    pallas_call x0 -> x2, Pallas kernels: none -> 19.1 us  [the longest x1 14.5 us: feedforward(): pl.pallas_call(kernel, grid=(tiles,), in_specs=[pl.BlockSpec((rows, depth...]
    ppermute x3, starting transfers between devices: 5.33 us -> 22.5 us  [hop(): return lax.ppermute(values, 'ctx', moves)]
    all_gather x3 -> x4, waiting for transfers between devices: 4.03 us -> 20.7 us  [gather_ctx(): return lax.all_gather(rows, 'ctx', axis=0, tiled=True)]
  transfers between devices with their start and end apart: 58 -> 46, of which waited for: 22 -> 20; matrix products, arithmetic and copies ran while one was open for 30% -> 33% of each run, Pallas kernels for 0% -> 1%
where the time goes in v3:
time: 573 us; the launch traced here: 567 us
  waiting for transfers between devices  238 us (42%)
  matrix products  105 us (18%)
  starting transfers between devices  78.7 us (14%)
  other arithmetic  77.4 us (14%)
  local copies, waits for them, and re-layouts  32.5 us (6%)
  Pallas kernels  19.1 us (3%)
  between operations  16.6 us (3%)
    all_to_all x4, waiting for transfers between devices, exchange_ctx(): return lax.all_to_all(blocks, 'ctx', 0, 0, tiled=True)  70.8 us
    ppermute x24, waiting for transfers between devices, send_dp(): return lax.ppermute(values, ('dp', 'ctx'), moves)  67.3 us
    reduce_scatter x3, waiting for transfers between devices, scatter_ctx(): lax.psum_scatter(partial, 'ctx', scatter_dimension=0, tiled=True)  61.5 us
    dot_general x15, matrix products, t_dot(): lax.dot_general(left, right, (((0,), (0,)), ((), ())), preferred_element_...  55.9 us
    ppermute x24, starting transfers between devices, send_dp(): return lax.ppermute(values, ('dp', 'ctx'), moves)  29.4 us
    dot_general x6, matrix products, dot_t(): lax.dot_general(left, right, (((1,), (1,)), ((), ())), preferred_element_...  27.6 us
    ppermute x3, starting transfers between devices, hop(): return lax.ppermute(values, 'ctx', moves)  22.5 us
    all_to_all x4, starting transfers between devices, exchange_ctx(): return lax.all_to_all(blocks, 'ctx', 0, 0, tiled=True)  22.1 us
  transfers between devices with their start and end apart: 46, of which 20 were waited for; matrix products, arithmetic and copies ran while one was open for 33% of the time, Pallas kernels for 1%

profile of v3, /device:TPU:0, one launch (start us, length us, event | category | flops | bytes accessed | tf_op | source)
XLA Modules:
  0.0 567.3 jit_solution(910516529134019908)
XLA Ops:
  13.4 6.3 %all-to-all-start = ((bf16[8,64,512]{2,1,0:T(8,128)(2,1)}), bf16[8,64,512]{2,1,0:T(8,128)(2,1)}, u32[]{:S(2)}, u32[]{:S(2)}) async-start(bf16[8,64,512]{2,1,0:T(8,128)(2,1)} %bitcast.10), calls=%async_computation | async-start | bytes 1048576 | tf_op jit(solution)/shard_map/all_to_all | solution.py:438
  25.0 30.3 %all-to-all-done = bf16[8,64,512]{2,1,0:T(8,128)(2,1)} async-done(((bf16[8,64,512]{2,1,0:T(8,128)(2,1)}), bf16[8,64,512]{2,1,0:T(8,128)(2,1)}, u32[]{:S(2)}, u32[]{:S(2)}) %all-to-all-start) | async-done | bytes 524320 | tf_op jit(solution)/shard_map/all_to_all | solution.py:438
  75.2 8.4 %all-gather.5.cloned.1.call-done = bf16[1024,2048]{1,0:T(8,128)(2,1)} async-done(((bf16[128,2048]{1,0:T(8,128)(2,1)}), bf16[1024,2048]{1,0:T(8,128)(2,1)}) %all-gather.5.cloned.1.call-update) | async-done | bytes 4194320 | tf_op jit(solution)/shard_map/all_gather | solution.py:372
  84.4 4.4 all-to-all-start.1
  94.6 3.9 fusion.97
  108.8 3.8 collective-permute-done.5
  116.8 18.3 %collective-permute-done.9 = bf16[256,2048]{1,0:T(8,128)(2,1)} collective-permute-done((bf16[256,2048]{1,0:T(8,128)(2,1)}, bf16[256,2048]{1,0:T(8,128)(2,1)}, u32[]{:S(2)}, u32[]{:S(2)}) %collective-permute-start.9) | collective-permute-done | bytes 1048608 | tf_op jit(solution)/shard_map/ppermute | solution.py:406
  139.9 3.3 convolution_convert_fusion.2
  143.2 7.0 %collective-permute-done.10 = bf16[256,2048]{1,0:T(8,128)(2,1)} collective-permute-done((bf16[256,2048]{1,0:T(8,128)(2,1)}, bf16[256,2048]{1,0:T(8,128)(2,1)}, u32[]{:S(2)}, u32[]{:S(2)}) %collective-permute-start.10) | collective-permute-done | bytes 1048608 | tf_op jit(solution)/shard_map/ppermute | solution.py:406
  150.1 21.4 %all-to-all-done.1 = bf16[8,64,2048]{2,1,0:T(8,128)(2,1)} async-done(((bf16[8,64,2048]{2,1,0:T(8,128)(2,1)}), bf16[8,64,2048]{2,1,0:T(8,128)(2,1)}, u32[]{:S(2)}, u32[]{:S(2)}) %all-to-all-start.1) | async-done | bytes 2097184 | tf_op jit(solution)/shard_map/all_to_all | solution.py:438
  174.1 46.5 %reduce-scatter.4.cloned.1.call-done = bf16[128,2048]{1,0:T(8,128)(2,1)} async-done(((bf16[1024,2048]{1,0:T(8,128)(2,1)}), bf16[128,2048]{1,0:T(8,128)(2,1)}) %reduce-scatter.4.cloned.1.call-update) | async-done | bytes 524304 | tf_op jit(solution)/shard_map/reduce_scatter | solution.py:376
  233.2 6.1 %fusion.124.grad_ref = f32[1024,1024]{1,0:T(8,128)} fusion(bf16[1024,2048]{1,0:T(8,128)(2,1)S(1)} %copy-done.52, bf16[1024,2048]{1,0:T(8,128)(2,1)S(1)} %constant_dynamic-update-slice_fusion), kind=kOutput, calls=%fused_computation.225 | convolution fusion | flops 4294967296 | bytes 12582912 | tf_op jit(solution)/shard_map/dot_general | solution.py:555
  241.8 13.3 %collective-permute-done.13 = bf16[512,2048]{1,0:T(8,128)(2,1)S(1)} collective-permute-done((bf16[512,2048]{1,0:T(8,128)(2,1)}, bf16[512,2048]{1,0:T(8,128)(2,1)S(1)}, u32[]{:S(2)}, u32[]{:S(2)}) %collective-permute-start.13) | collective-permute-done | bytes 2097184 | tf_op jit(solution)/shard_map/ppermute | solution.py:406
  255.1 5.7 pad_maximum_fusion.gate_ref.up_ref
  260.8 9.7 %all-gather.9.cloned.1.call-done.hat_ref = bf16[1024,2048]{1,0:T(8,128)(2,1)} async-done(((bf16[128,2048]{1,0:T(8,128)(2,1)}), bf16[1024,2048]{1,0:T(8,128)(2,1)}) %all-gather.9.cloned.1.call-update) | async-done | bytes 4194320 | tf_op jit(solution)/shard_map/all_gather | solution.py:372
  270.5 14.5 %shard_map.203 = (bf16[1024,1024]{1,0:T(8,128)(2,1)S(1)}, bf16[1024,2048]{1,0:T(8,128)(2,1)S(1)}) custom-call(bf16[1024,2048]{1,0:T(8,128)(2,1)} %all-gather.9.cloned.1.call-done.hat_ref, bf16[2048,2048]{1,0:T(8,128)(2,1)} %pad_maximum_fusion.gate_ref.up_ref, bf16[2048,2048]{1,0:T(8,128)(2,1)} %pad_maximum_fusion.gate_ref.up_ref, f32[1024,1024]{1,0:T(8,128)} %fusion.124.grad_ref), custom_call_target="tpu_custom_call" | custom-call | flops 8589934592 | bytes 23068672 | tf_op jit(solution)/shard_map/pallas_call | solution.py:493
  288.3 10.5 %convolution_convert_fusion.1 = bf16[1024,2048]{1,0:T(8,128)(2,1)} fusion(bf16[1024,2048]{1,0:T(8,128)(2,1)S(1)} %get-tuple-element.92, bf16[2048,2048]{1,0:T(8,128)(2,1)S(1)} %copy-done.14), kind=kOutput, calls=%fused_computation.13 | convolution fusion | flops 8592031744 | bytes 16777216 | tf_op jit(solution)/shard_map/dot_general | solution.py:555
  299.4 6.4 %convolution_convert_fusion.4 = bf16[512,2048]{1,0:T(8,128)(2,1)} fusion(bf16[1024,2048]{1,0:T(8,128)(2,1)} %copy-done, bf16[1024,2048]{1,0:T(8,128)(2,1)} %all-gather.9.cloned.1.call-done.hat_ref), kind=kOutput, calls=%fused_computation.17 | convolution fusion | flops 2148532224 | bytes 7340032 | tf_op jit(solution)/shard_map/dot_general | solution.py:558
  311.3 6.3 %convolution_convert_fusion.3 = bf16[512,2048]{1,0:T(8,128)(2,1)} fusion(bf16[1024,2048]{1,0:T(8,128)(2,1)} %copy-done, bf16[1024,2048]{1,0:T(8,128)(2,1)} %all-gather.9.cloned.1.call-done.hat_ref, s32[]{:T(128)S(6)} %select_n.286), kind=kOutput, calls=%fused_computation.16 | convolution fusion | flops 2148532224 | bytes 7340036 | tf_op jit(solution)/shard_map/dot_general | solution.py:558
  318.9 4.8 convolution_convert_fusion.9
  323.8 3.4 add_convert_fusion.5
  327.2 3.3 collective-permute-start.17
  330.5 3.3 convolution_convert_fusion.8
  333.8 5.7 %add_convert_fusion.1 = bf16[512,2048]{1,0:T(8,128)(2,1)} fusion(bf16[512,2048]{1,0:T(8,128)(2,1)} %collective-permute-done.14, bf16[1024,2048]{1,0:T(8,128)(2,1)S(1)} %copy-done.1, bf16[1024,2048]{1,0:T(8,128)(2,1)} %all-gather.9.cloned.1.call-done.hat_ref, s32[]{:T(128)S(6)} %select_n.285), kind=kOutput, calls=%fused_computation.7 | convolution fusion | flops 2150629376 | bytes 9437188 | tf_op jit(solution)/shard_map/dot_general | solution.py:558
  339.5 15.0 %reduce-scatter.6.cloned.1.call-done = bf16[128,2048]{1,0:T(8,128)(2,1)} async-done(((bf16[1024,2048]{1,0:T(8,128)(2,1)}), bf16[128,2048]{1,0:T(8,128)(2,1)}) %reduce-scatter.6.cloned.1.call-update) | async-done | bytes 524304 | tf_op jit(solution)/shard_map/reduce_scatter | solution.py:376
  359.6 4.7 convolution_convert_fusion.5
  364.3 3.7 fusion.46
  368.0 16.0 %collective-permute-done.19 = bf16[512,2048]{1,0:T(8,128)(2,1)} collective-permute-done((bf16[512,2048]{1,0:T(8,128)(2,1)}, bf16[512,2048]{1,0:T(8,128)(2,1)}, u32[]{:S(2)}, u32[]{:S(2)}) %collective-permute-start.19) | collective-permute-done | bytes 2097184 | tf_op jit(solution)/shard_map/ppermute | solution.py:406
  384.0 4.8 add_convert_fusion
  388.8 4.4 all-to-all-start.2
  395.2 3.5 add_convert_fusion.4
  398.7 4.8 collective-permute-start.22
  403.5 5.0 collective-permute-done.18
  411.0 3.9 fusion.102
  419.6 3.9 add_convert_fusion.3
  424.5 3.4 multiply_convert_fusion
  427.8 17.3 %collective-permute-done.22 = bf16[256,2048]{1,0:T(8,128)(2,1)} collective-permute-done((bf16[256,2048]{1,0:T(8,128)(2,1)}, bf16[256,2048]{1,0:T(8,128)(2,1)}, u32[]{:S(2)}, u32[]{:S(2)}) %collective-permute-start.22) | collective-permute-done | bytes 1048608 | tf_op jit(solution)/shard_map/ppermute | solution.py:382
  445.1 3.4 all-to-all-done.2.sums_ref
  456.5 3.4 add_convert_fusion.2
  459.9 14.4 %collective-permute-start.27 = (bf16[256,2048]{1,0:T(8,128)(2,1)}, bf16[256,2048]{1,0:T(8,128)(2,1)}, u32[]{:S(2)}, u32[]{:S(2)}) collective-permute-start(bf16[256,2048]{1,0:T(8,128)(2,1)} %add_convert_fusion.2), channel_id=1, source_target_pairs={{0,2},{2,4},{4,6},{7,5},{5,3},{3,1},{8,10},{10,12},{12,14},{15,13}... | collective-permute-start | bytes 3145736 | tf_op jit(solution)/shard_map/ppermute | solution.py:382
  480.3 5.4 convolution_convert_fusion
  493.1 3.6 fusion.84
  497.9 4.6 shard_map.204
  509.8 3.4 convert_add_fusion
  522.3 7.1 %all-to-all-start.3 = ((bf16[8,64,512]{2,1,0:T(8,128)(2,1)}), bf16[8,64,512]{2,1,0:T(8,128)(2,1)S(1)}, u32[]{:S(2)}, u32[]{:S(2)}) async-start(bf16[8,64,512]{2,1,0:T(8,128)(2,1)} %bitcast.22), calls=%async_computation.6 | async-start | bytes 1048576 | tf_op jit(solution)/shard_map/all_to_all | solution.py:438
  529.4 4.0 fusion.6
  534.8 15.7 %all-to-all-done.3 = bf16[8,64,512]{2,1,0:T(8,128)(2,1)S(1)} async-done(((bf16[8,64,512]{2,1,0:T(8,128)(2,1)}), bf16[8,64,512]{2,1,0:T(8,128)(2,1)S(1)}, u32[]{:S(2)}, u32[]{:S(2)}) %all-to-all-start.3) | async-done | bytes 524320 | tf_op jit(solution)/shard_map/all_to_all | solution.py:438
  556.4 3.6 fusion.96
  (293 shorter events, 145.6 us)
Async XLA Ops:
  7.2 76.4 %all-gather.5.cloned.1.call-start = ((), (), s32[]{:S(2)}) async-start(), calls=%async_computation.7 | async-start | bytes 4718592 | tf_op jit(solution)/shard_map/all_gather | solution.py:372
  11.4 45.3 %copy-start.3 = (f32[64,8192]{1,0:T(8,128)S(1)}, f32[64,8192]{1,0:T(8,128)}, u32[]{:S(2)}) copy-start(f32[64,8192]{1,0:T(8,128)} %gate_ref.1) | copy-start | bytes 6291460
  13.4 41.8 %all-to-all-start = ((bf16[8,64,512]{2,1,0:T(8,128)(2,1)}), bf16[8,64,512]{2,1,0:T(8,128)(2,1)}, u32[]{:S(2)}, u32[]{:S(2)}) async-start(bf16[8,64,512]{2,1,0:T(8,128)(2,1)} %bitcast.10), calls=%async_computation | async-start | bytes 1048576 | tf_op jit(solution)/shard_map/all_to_all | solution.py:438
  19.7 151.8 %all-gather.7.cloned.1.call-start = ((), (), s32[]{:S(2)}) async-start(), calls=%async_computation.8 | async-start | bytes 4718592 | tf_op jit(solution)/shard_map/all_gather | solution.py:372
  20.9 54.3 %collective-permute-start = (bf16[64,2048]{1,0:T(8,128)(2,1)S(1)}, bf16[64,2048]{1,0:T(8,128)(2,1)}, u32[]{:S(2)}, u32[]{:S(2)}) collective-permute-start(bf16[64,2048]{1,0:T(8,128)(2,1)S(1)} %convert_element_type.316), channel_id=1, source_target_pairs={{0,0},{1,8},{2,16},{3,24},{4,1},{5,9},{6,17},{7,25},{8,2},{9,10},{... | collective-permute-start | bytes 786440 | tf_op jit(solution)/shard_map/ppermute | solution.py:581
  55.2 19.9 %collective-permute-start.1 = (bf16[512,512]{1,0:T(8,128)(2,1)}, bf16[512,512]{1,0:T(8,128)(2,1)}, u32[]{:S(2)}, u32[]{:S(2)}) collective-permute-start(bf16[512,512]{1,0:T(8,128)(2,1)} %bitcast.11), channel_id=1, source_target_pairs={{0,8},{1,17},{2,10},{3,19},{4,12},{5,21},{6,14},{7,23},{8,0},{9,25... | collective-permute-start | bytes 1572872 | tf_op jit(solution)/shard_map/ppermute | solution.py:406
  56.6 18.5 %collective-permute-start.2 = (bf16[512,512]{1,0:T(8,128)(2,1)}, bf16[512,512]{1,0:T(8,128)(2,1)}, u32[]{:S(2)}, u32[]{:S(2)}) collective-permute-start(bf16[512,512]{1,0:T(8,128)(2,1)} %bitcast.11), channel_id=1, source_target_pairs={{0,16},{1,9},{2,18},{3,11},{4,20},{5,13},{6,22},{7,15},{8,24},{9,1... | collective-permute-start | bytes 1572872 | tf_op jit(solution)/shard_map/ppermute | solution.py:406
  84.3 10.1 %collective-permute-start.3 = (bf16[512,512]{1,0:T(8,128)(2,1)}, bf16[512,512]{1,0:T(8,128)(2,1)S(1)}, u32[]{:S(2)}, u32[]{:S(2)}) collective-permute-start(bf16[512,512]{1,0:T(8,128)(2,1)} %collective-permute-done.1), channel_id=1, source_target_pairs={{0,16},{1,9},{2,18},{3,11},{4,20},{5,13},{6,22},{7,15},{8,24},{9,1... | collective-permute-start | bytes 1572872 | tf_op jit(solution)/shard_map/ppermute | solution.py:406
  84.4 87.1 %all-to-all-start.1 = ((bf16[8,64,2048]{2,1,0:T(8,128)(2,1)}), bf16[8,64,2048]{2,1,0:T(8,128)(2,1)}, u32[]{:S(2)}, u32[]{:S(2)}) async-start(bf16[8,64,2048]{2,1,0:T(8,128)(2,1)} %bitcast.92), calls=%async_computation.1 | async-start | bytes 4194304 | tf_op jit(solution)/shard_map/all_to_all | solution.py:438
  88.7 131.8 %reduce-scatter.4.cloned.1.call-start = ((), (), s32[]{:S(2)}) async-start(), calls=%async_computation.9 | async-start | bytes 4718592 | tf_op jit(solution)/shard_map/reduce_scatter | solution.py:376
  103.2 9.4 %collective-permute-start.5 = (bf16[64,2048]{1,0:T(8,128)(2,1)}, bf16[64,2048]{1,0:T(8,128)(2,1)S(1)}, u32[]{:S(2)}, u32[]{:S(2)}) collective-permute-start(bf16[64,2048]{1,0:T(8,128)(2,1)} %collective-permute-done), channel_id=1, source_target_pairs={{0,8},{1,17},{2,10},{3,19},{4,12},{5,21},{6,14},{7,23},{8,0},{9,25... | collective-permute-start | bytes 786440 | tf_op jit(solution)/shard_map/ppermute | solution.py:406
  105.5 9.4 %collective-permute-start.6 = (bf16[64,2048]{1,0:T(8,128)(2,1)}, bf16[64,2048]{1,0:T(8,128)(2,1)S(1)}, u32[]{:S(2)}, u32[]{:S(2)}) collective-permute-start(bf16[64,2048]{1,0:T(8,128)(2,1)} %collective-permute-done), channel_id=1, source_target_pairs={{0,16},{1,9},{2,18},{3,11},{4,20},{5,13},{6,22},{7,15},{8,24},{9,1... | collective-permute-start | bytes 786440 | tf_op jit(solution)/shard_map/ppermute | solution.py:406
  105.5 37.6 %collective-permute-start.8 = (bf16[256,2048]{1,0:T(8,128)(2,1)}, bf16[256,2048]{1,0:T(8,128)(2,1)}, u32[]{:S(2)}, u32[]{:S(2)}) collective-permute-start(bf16[256,2048]{1,0:T(8,128)(2,1)} %convert_element_type.317), channel_id=1, source_target_pairs={{0,16},{1,9},{2,18},{3,11},{4,20},{5,13},{6,22},{7,15},{8,24},{9,1... | collective-permute-start | bytes 3145736 | tf_op jit(solution)/shard_map/ppermute | solution.py:406
  107.6 27.5 %collective-permute-start.9 = (bf16[256,2048]{1,0:T(8,128)(2,1)}, bf16[256,2048]{1,0:T(8,128)(2,1)}, u32[]{:S(2)}, u32[]{:S(2)}) collective-permute-start(bf16[256,2048]{1,0:T(8,128)(2,1)} %convert_element_type.317), channel_id=1, source_target_pairs={{0,8},{1,17},{2,10},{3,19},{4,12},{5,21},{6,14},{7,23},{8,0},{9,25... | collective-permute-start | bytes 3145736 | tf_op jit(solution)/shard_map/ppermute | solution.py:406
  107.7 7.3 %collective-permute-start.4 = (bf16[1024,256]{0,1:T(8,128)(2,1)S(1)}, bf16[1024,256]{0,1:T(8,128)(2,1)S(1)}, u32[]{:S(2)}, u32[]{:S(2)}) collective-permute-start(bf16[1024,256]{0,1:T(8,128)(2,1)S(1)} %fusion.38), channel_id=1, source_target_pairs={{0,1},{1,0},{2,3},{3,2},{4,5},{5,4},{6,7},{7,6},{8,9},{9,8},{10,11... | collective-permute-start | bytes 1572872 | tf_op jit(solution)/shard_map/ppermute | solution.py:368
  112.6 25.0 %collective-permute-start.7 = (bf16[64,2048]{1,0:T(8,128)(2,1)S(1)}, bf16[64,2048]{1,0:T(8,128)(2,1)S(1)}, u32[]{:S(2)}, u32[]{:S(2)}) collective-permute-start(bf16[64,2048]{1,0:T(8,128)(2,1)S(1)} %collective-permute-done.5), channel_id=1, source_target_pairs={{0,16},{1,9},{2,18},{3,11},{4,20},{5,13},{6,22},{7,15},{8,24},{9,1... | collective-permute-start | bytes 786440 | tf_op jit(solution)/shard_map/ppermute | solution.py:406
  135.0 15.1 %collective-permute-start.10 = (bf16[256,2048]{1,0:T(8,128)(2,1)}, bf16[256,2048]{1,0:T(8,128)(2,1)}, u32[]{:S(2)}, u32[]{:S(2)}) collective-permute-start(bf16[256,2048]{1,0:T(8,128)(2,1)} %collective-permute-done.9), channel_id=1, source_target_pairs={{0,16},{1,9},{2,18},{3,11},{4,20},{5,13},{6,22},{7,15},{8,24},{9,1... | collective-permute-start | bytes 3145736 | tf_op jit(solution)/shard_map/ppermute | solution.py:406
  143.2 77.4 %copy-start.11 = (bf16[1,128,2048]{2,1,0:T(8,128)(2,1)S(1)}, bf16[1,128,2048]{2,1,0:T(8,128)(2,1)}, u32[]{:S(2)}) copy-start(bf16[1,128,2048]{2,1,0:T(8,128)(2,1)} %param.12) | copy-start | bytes 1572868
  171.5 99.0 %all-gather.9.cloned.1.call-start = ((), (), s32[]{:S(2)}) async-start(), calls=%async_computation.10 | async-start | bytes 4718592 | tf_op jit(solution)/shard_map/all_gather | solution.py:372
  171.6 53.4 %collective-permute-start.11 = (bf16[512,2048]{1,0:T(8,128)(2,1)}, bf16[512,2048]{1,0:T(8,128)(2,1)}, u32[]{:S(2)}, u32[]{:S(2)}) collective-permute-start(bf16[512,2048]{1,0:T(8,128)(2,1)} %bitcast.17), channel_id=1, source_target_pairs={{0,8},{1,17},{2,10},{3,19},{4,12},{5,21},{6,14},{7,23},{8,0},{9,25... | collective-permute-start | bytes 6291464 | tf_op jit(solution)/shard_map/ppermute | solution.py:406
  174.0 51.0 %collective-permute-start.12 = (bf16[512,2048]{1,0:T(8,128)(2,1)}, bf16[512,2048]{1,0:T(8,128)(2,1)}, u32[]{:S(2)}, u32[]{:S(2)}) collective-permute-start(bf16[512,2048]{1,0:T(8,128)(2,1)} %bitcast.17), channel_id=1, source_target_pairs={{0,16},{1,9},{2,18},{3,11},{4,20},{5,13},{6,22},{7,15},{8,24},{9,1... | collective-permute-start | bytes 6291464 | tf_op jit(solution)/shard_map/ppermute | solution.py:406
  225.0 129.4 %reduce-scatter.6.cloned.1.call-start = ((), (), s32[]{:S(2)}) async-start(), calls=%async_computation.11 | async-start | bytes 4718592 | tf_op jit(solution)/shard_map/reduce_scatter | solution.py:376
  228.8 26.3 %collective-permute-start.13 = (bf16[512,2048]{1,0:T(8,128)(2,1)}, bf16[512,2048]{1,0:T(8,128)(2,1)S(1)}, u32[]{:S(2)}, u32[]{:S(2)}) collective-permute-start(bf16[512,2048]{1,0:T(8,128)(2,1)} %collective-permute-done.11), channel_id=1, source_target_pairs={{0,16},{1,9},{2,18},{3,11},{4,20},{5,13},{6,22},{7,15},{8,24},{9,1... | collective-permute-start | bytes 6291464 | tf_op jit(solution)/shard_map/ppermute | solution.py:406
  298.8 112.2 %all-gather.11.cloned.1.call-start = ((), (), s32[]{:S(2)}) async-start(), calls=%async_computation.12 | async-start | bytes 4718592 | tf_op jit(solution)/shard_map/all_gather | solution.py:372
  305.8 28.0 %collective-permute-start.14 = (bf16[512,2048]{1,0:T(8,128)(2,1)}, bf16[512,2048]{1,0:T(8,128)(2,1)}, u32[]{:S(2)}, u32[]{:S(2)}) collective-permute-start(bf16[512,2048]{1,0:T(8,128)(2,1)} %convolution_convert_fusion.4), channel_id=1, source_target_pairs={{0,16},{1,9},{2,18},{3,11},{4,20},{5,13},{6,22},{7,15},{8,24},{9,1... | collective-permute-start | bytes 6291464 | tf_op jit(solution)/shard_map/ppermute | solution.py:406
  311.3 12.5 %collective-permute-start.16 = (bf16[256,2048]{1,0:T(8,128)(2,1)}, bf16[256,2048]{1,0:T(8,128)(2,1)}, u32[]{:S(2)}, u32[]{:S(2)}) collective-permute-start(bf16[256,2048]{1,0:T(8,128)(2,1)} %get-tuple-element.173), channel_id=1, source_target_pairs={{0,1},{1,0},{2,3},{3,2},{4,5},{5,4},{6,7},{7,6},{8,9},{9,8},{10,11... | collective-permute-start | bytes 3145736 | tf_op jit(solution)/shard_map/ppermute | solution.py:368
  317.5 38.2 %collective-permute-start.15 = (bf16[512,2048]{1,0:T(8,128)(2,1)}, bf16[512,2048]{1,0:T(8,128)(2,1)}, u32[]{:S(2)}, u32[]{:S(2)}) collective-permute-start(bf16[512,2048]{1,0:T(8,128)(2,1)} %convolution_convert_fusion.3), channel_id=1, source_target_pairs={{0,16},{1,9},{2,18},{3,11},{4,20},{5,13},{6,22},{7,15},{8,24},{9,1... | collective-permute-start | bytes 6291464 | tf_op jit(solution)/shard_map/ppermute | solution.py:406
  327.2 28.6 %collective-permute-start.17 = (bf16[256,2048]{1,0:T(8,128)(2,1)}, bf16[256,2048]{1,0:T(8,128)(2,1)}, u32[]{:S(2)}, u32[]{:S(2)}) collective-permute-start(bf16[256,2048]{1,0:T(8,128)(2,1)} %get-tuple-element.123), channel_id=1, source_target_pairs={{0,2},{7,5},{8,10},{15,13},{16,18},{23,21},{24,26},{31,29}} | collective-permute-start | bytes 3145736 | tf_op jit(solution)/shard_map/ppermute | solution.py:382
  357.6 26.4 %collective-permute-start.19 = (bf16[512,2048]{1,0:T(8,128)(2,1)}, bf16[512,2048]{1,0:T(8,128)(2,1)}, u32[]{:S(2)}, u32[]{:S(2)}) collective-permute-start(bf16[512,2048]{1,0:T(8,128)(2,1)} %add_convert_fusion.1), channel_id=1, source_target_pairs={{0,8},{1,17},{2,10},{3,19},{4,12},{5,21},{6,14},{7,23},{8,0},{9,25... | collective-permute-start | bytes 6291464 | tf_op jit(solution)/shard_map/ppermute | solution.py:406
  364.3 30.9 %collective-permute-start.21 = (bf16[256,2048]{1,0:T(8,128)(2,1)}, bf16[256,2048]{1,0:T(8,128)(2,1)}, u32[]{:S(2)}, u32[]{:S(2)}) collective-permute-start(bf16[256,2048]{1,0:T(8,128)(2,1)} %convolution_convert_fusion.5), channel_id=1, source_target_pairs={{0,1},{1,0},{2,3},{3,2},{4,5},{5,4},{6,7},{7,6},{8,9},{9,8},{10,11... | collective-permute-start | bytes 3145736 | tf_op jit(solution)/shard_map/ppermute | solution.py:368
  388.8 59.7 %all-to-all-start.2 = ((bf16[8,64,2048]{2,1,0:T(8,128)(2,1)}), bf16[8,64,2048]{2,1,0:T(8,128)(2,1)}, u32[]{:S(2)}, u32[]{:S(2)}) async-start(bf16[8,64,2048]{2,1,0:T(8,128)(2,1)} %bitcast.91), calls=%async_computation.4 | async-start | bytes 4194304 | tf_op jit(solution)/shard_map/all_to_all | solution.py:438
  393.2 161.6 %reduce-scatter.8.cloned.1.call-start = ((), (), s32[]{:S(2)}) async-start(), calls=%async_computation.13 | async-start | bytes 4718592 | tf_op jit(solution)/shard_map/reduce_scatter | solution.py:376
  393.2 15.2 %collective-permute-start.18 = (bf16[256,2048]{1,0:T(8,128)(2,1)}, bf16[256,2048]{1,0:T(8,128)(2,1)}, u32[]{:S(2)}, u32[]{:S(2)}) collective-permute-start(bf16[256,2048]{1,0:T(8,128)(2,1)} %convolution_convert_fusion.9), channel_id=1, source_target_pairs={{0,16},{1,9},{2,18},{3,11},{4,20},{5,13},{6,22},{7,15},{8,24},{9,1... | collective-permute-start | bytes 3145736 | tf_op jit(solution)/shard_map/ppermute | solution.py:406
  395.2 61.3 %collective-permute-start.26 = (bf16[256,2048]{1,0:T(8,128)(2,1)}, bf16[256,2048]{1,0:T(8,128)(2,1)}, u32[]{:S(2)}, u32[]{:S(2)}) collective-permute-start(bf16[256,2048]{1,0:T(8,128)(2,1)} %get-tuple-element.124), channel_id=1, source_target_pairs={{0,1},{1,0},{2,3},{3,2},{4,5},{5,4},{6,7},{7,6},{8,9},{9,8},{10,11... | collective-permute-start | bytes 3145736 | tf_op jit(solution)/shard_map/ppermute | solution.py:368
  398.7 46.5 %collective-permute-start.22 = (bf16[256,2048]{1,0:T(8,128)(2,1)}, bf16[256,2048]{1,0:T(8,128)(2,1)}, u32[]{:S(2)}, u32[]{:S(2)}) collective-permute-start(bf16[256,2048]{1,0:T(8,128)(2,1)} %add_convert_fusion.4), channel_id=1, source_target_pairs={{0,2},{2,4},{7,5},{5,3},{8,10},{10,12},{15,13},{13,11},{16,18},{18... | collective-permute-start | bytes 3145736 | tf_op jit(solution)/shard_map/ppermute | solution.py:382
  417.1 31.4 %collective-permute-start.20 = (bf16[64,2048]{1,0:T(8,128)(2,1)S(1)}, bf16[64,2048]{1,0:T(8,128)(2,1)}, u32[]{:S(2)}, u32[]{:S(2)}) collective-permute-start(bf16[64,2048]{1,0:T(8,128)(2,1)S(1)} %get-tuple-element.132), channel_id=1, source_target_pairs={{0,16},{1,9},{2,18},{3,11},{4,20},{5,13},{6,22},{7,15},{8,24},{9,1... | collective-permute-start | bytes 786440 | tf_op jit(solution)/shard_map/ppermute | solution.py:406
  423.5 62.3 %collective-permute-start.25 = (bf16[256,2048]{1,0:T(8,128)(2,1)}, bf16[256,2048]{1,0:T(8,128)(2,1)}, u32[]{:S(2)}, u32[]{:S(2)}) collective-permute-start(bf16[256,2048]{1,0:T(8,128)(2,1)} %add_convert_fusion.3), channel_id=1, source_target_pairs={{0,8},{1,17},{2,10},{3,19},{4,12},{5,21},{6,14},{7,23},{8,0},{9,25... | collective-permute-start | bytes 3145736 | tf_op jit(solution)/shard_map/ppermute | solution.py:406
  452.9 24.6 %collective-permute-start.23 = (bf16[1024,256]{0,1:T(8,128)(2,1)S(1)}, bf16[1024,256]{0,1:T(8,128)(2,1)S(1)}, u32[]{:S(2)}, u32[]{:S(2)}) collective-permute-start(bf16[1024,256]{0,1:T(8,128)(2,1)S(1)} %get-tuple-element.177), channel_id=1, source_target_pairs={{0,1},{1,0},{2,3},{3,2},{4,5},{5,4},{6,7},{7,6},{8,9},{9,8},{10,11... | collective-permute-start | bytes 1572872 | tf_op jit(solution)/shard_map/ppermute | solution.py:368
  455.0 30.7 %collective-permute-start.24 = (bf16[64,2048]{1,0:T(8,128)(2,1)}, bf16[64,2048]{1,0:T(8,128)(2,1)}, u32[]{:S(2)}, u32[]{:S(2)}) collective-permute-start(bf16[64,2048]{1,0:T(8,128)(2,1)} %add_convert_fusion.9), channel_id=1, source_target_pairs={{0,8},{1,17},{2,10},{3,19},{4,12},{5,21},{6,14},{7,23},{8,0},{9,25... | collective-permute-start | bytes 786440 | tf_op jit(solution)/shard_map/ppermute | solution.py:406
  459.9 25.9 %collective-permute-start.27 = (bf16[256,2048]{1,0:T(8,128)(2,1)}, bf16[256,2048]{1,0:T(8,128)(2,1)}, u32[]{:S(2)}, u32[]{:S(2)}) collective-permute-start(bf16[256,2048]{1,0:T(8,128)(2,1)} %add_convert_fusion.2), channel_id=1, source_target_pairs={{0,2},{2,4},{4,6},{7,5},{5,3},{3,1},{8,10},{10,12},{12,14},{15,13}... | collective-permute-start | bytes 3145736 | tf_op jit(solution)/shard_map/ppermute | solution.py:382
  485.9 23.9 %collective-permute-start.34 = (bf16[256,2048]{1,0:T(8,128)(2,1)}, bf16[256,2048]{1,0:T(8,128)(2,1)}, u32[]{:S(2)}, u32[]{:S(2)}) collective-permute-start(bf16[256,2048]{1,0:T(8,128)(2,1)} %convolution_convert_fusion.8), channel_id=1, source_target_pairs={{0,16},{1,9},{2,18},{3,11},{4,20},{5,13},{6,22},{7,15},{8,24},{9,1... | collective-permute-start | bytes 3145736 | tf_op jit(solution)/shard_map/ppermute | solution.py:406
  492.3 14.5 %collective-permute-start.29 = (bf16[512,512]{1,0:T(8,128)(2,1)}, bf16[512,512]{1,0:T(8,128)(2,1)}, u32[]{:S(2)}, u32[]{:S(2)}) collective-permute-start(bf16[512,512]{1,0:T(8,128)(2,1)} %convolution_convert_fusion.11), channel_id=1, source_target_pairs={{0,16},{1,9},{2,18},{3,11},{4,20},{5,13},{6,22},{7,15},{8,24},{9,1... | collective-permute-start | bytes 1572872 | tf_op jit(solution)/shard_map/ppermute | solution.py:406
  496.8 16.4 %collective-permute-start.32 = (bf16[64,2048]{1,0:T(8,128)(2,1)S(1)}, bf16[64,2048]{1,0:T(8,128)(2,1)S(1)}, u32[]{:S(2)}, u32[]{:S(2)}) collective-permute-start(bf16[64,2048]{1,0:T(8,128)(2,1)S(1)} %copy-done.49), channel_id=1, source_target_pairs={{0,16},{1,9},{2,18},{3,11},{4,20},{5,13},{6,22},{7,15},{8,24},{9,1... | collective-permute-start | bytes 786440 | tf_op jit(solution)/shard_map/ppermute | solution.py:406
  505.5 14.0 %collective-permute-start.28 = (bf16[512,512]{1,0:T(8,128)(2,1)S(1)}, bf16[512,512]{1,0:T(8,128)(2,1)S(1)}, u32[]{:S(2)}, u32[]{:S(2)}) collective-permute-start(bf16[512,512]{1,0:T(8,128)(2,1)S(1)} %convolution_convert_fusion.12), channel_id=1, source_target_pairs={{0,16},{1,9},{2,18},{3,11},{4,20},{5,13},{6,22},{7,15},{8,24},{9,1... | collective-permute-start | bytes 1572872 | tf_op jit(solution)/shard_map/ppermute | solution.py:406
  509.2 10.3 %collective-permute-start.30 = (bf16[512,512]{1,0:T(8,128)(2,1)S(1)}, bf16[512,512]{1,0:T(8,128)(2,1)S(1)}, u32[]{:S(2)}, u32[]{:S(2)}) collective-permute-start(bf16[512,512]{1,0:T(8,128)(2,1)S(1)} %add_convert_fusion.7), channel_id=1, source_target_pairs={{0,8},{1,17},{2,10},{3,19},{4,12},{5,21},{6,14},{7,23},{8,0},{9,25... | collective-permute-start | bytes 1572872 | tf_op jit(solution)/shard_map/ppermute | solution.py:406
  515.1 19.8 %collective-permute-start.33 = (bf16[64,2048]{1,0:T(8,128)(2,1)}, bf16[64,2048]{1,0:T(8,128)(2,1)S(1)}, u32[]{:S(2)}, u32[]{:S(2)}) collective-permute-start(bf16[64,2048]{1,0:T(8,128)(2,1)} %add_convert_fusion.8), channel_id=1, source_target_pairs={{0,0},{8,1},{16,2},{24,3},{1,4},{9,5},{17,6},{25,7},{2,8},{10,9},{... | collective-permute-start | bytes 786440 | tf_op jit(solution)/shard_map/ppermute | solution.py:750
  522.3 28.2 %all-to-all-start.3 = ((bf16[8,64,512]{2,1,0:T(8,128)(2,1)}), bf16[8,64,512]{2,1,0:T(8,128)(2,1)S(1)}, u32[]{:S(2)}, u32[]{:S(2)}) async-start(bf16[8,64,512]{2,1,0:T(8,128)(2,1)} %bitcast.22), calls=%async_computation.6 | async-start | bytes 1048576 | tf_op jit(solution)/shard_map/all_to_all | solution.py:438
  534.4 22.0 %collective-permute-start.31 = (bf16[128,2048]{1,0:T(8,128)(2,1)}, bf16[128,2048]{1,0:T(8,128)(2,1)}, u32[]{:S(2)}, u32[]{:S(2)}) collective-permute-start(bf16[128,2048]{1,0:T(8,128)(2,1)} %select_convert_fusion), channel_id=1, source_target_pairs={{0,1},{1,0},{2,3},{3,2},{4,5},{5,4},{6,7},{7,6},{8,9},{9,8},{10,11... | collective-permute-start | bytes 1572872 | tf_op jit(solution)/shard_map/ppermute | solution.py:368
  (59 other events, 434.4 us)
Sparse Core Ops, SparseCore 0:
  10.2 73.3 all-gather.4
  85.2 84.4 all-gather.6
  172.0 48.4 reduce-scatter.3
  225.2 45.2 all-gather.8
  299.0 55.4 reduce-scatter.5
  357.7 53.2 all-gather.10
  485.9 58.9 reduce-scatter.7

commit v4 on v3

--- a/solution.py
+++ b/solution.py
@@ -719,10 +719,7 @@
     delta = jnp.sum(d_attn.astype(wide) * attended, axis=-1, keepdims=True)
     probs = weights / total
     d_scores = (probs * (dot_t(d_attn, values) - delta)).astype(low)
-    d_scores, out_across, carried, gate_up_sum = lax.optimization_barrier(
-        (d_scores, out_across, carried, gate_up_sum)
-    )
-    carried = sum_step(out_slots, carried, 1)
+    d_scores, out_across, carried = lax.optimization_barrier((d_scores, out_across, carried))
     out_near = send_dp((out_block(near_bit()) + out_across.astype(wide)).astype(low), 1, 2)
     d_query = rotate(dot(d_scores, keys) * scale, -1.0)
     dk_part = t_dot(d_scores, q_rot)
@@ -736,7 +733,7 @@
         (e1_part, out_near, down_near, carried)
     )
     e1 = turned(scatter_ctx(e1_part))
-    d_proj = after(d_proj, e1_part)
+    d_proj, gate_up_sum = lax.optimization_barrier((d_proj, gate_up_sum, e1_part))[:2]
 
     def proj_block(j):
         return t_dot(block_columns(all_hat1, j), d_proj)
@@ -745,16 +742,19 @@
     proj_far = send_dp(proj_block(3 - near_bit()).astype(low), 2, 1)
     relayed = (proj_block(near_bit()) + proj_across.astype(wide)).astype(low)
     proj_near = send_dp(relayed, 1, 2)
-    out_near = after(out_near, proj_across)
+    proj_sum = proj_block(0) + proj_far.astype(wide) + proj_near.astype(wide)
+    proj_source = proj_sum.astype(low).reshape(2 * N_Z, rows, cols)
+    proj_sum = exchange_ctx(proj_source)
+    gate_up_sum, down_near, out_near, carried = lax.optimization_barrier(
+        (gate_up_sum, down_near, out_near, carried, proj_source)
+    )[:4]
+    carried = sum_step(out_slots, carried, 1)
     out_sum = out_block(0) + out_far.astype(wide) + out_near.astype(wide)
     out_sum = lax.ppermute(
         out_sum.astype(low), ("dp", "ctx"), [(to, start) for start, to in moves]
     )
-    proj_sum = proj_block(0) + proj_far.astype(wide) + proj_near.astype(wide)
-    proj_sum = proj_sum.astype(low)
-    out_branch = sum_end(out_slots, after(carried, proj_sum))
+    out_branch = sum_end(out_slots, carried)
     output = (middle + out_branch).astype(low)[None]
-    proj_sum = exchange_ctx(proj_sum.reshape(2 * N_Z, rows, cols))
     down_sum = down_block(0) + down_far.astype(wide) + down_near.astype(wide)
     out_sum, proj_sum = lax.optimization_barrier((out_sum, proj_sum))
     out_sum = out_sum.astype(wide)

time: 573 us -> 552 us (0.963)
  waiting for transfers between devices: 238 us -> 219 us
    ppermute x3, waiting for transfers between devices: 17.3 us -> 0.01 us  [hop(): return lax.ppermute(values, 'ctx', moves)]
    ppermute x3, starting transfers between devices: 22.5 us -> 11.4 us  [hop(): return lax.ppermute(values, 'ctx', moves)]
    all_to_all x4, waiting for transfers between devices: 70.8 us -> 59.8 us  [exchange_ctx(): return lax.all_to_all(blocks, 'ctx', 0, 0, tiled=True)]
    ppermute x6, starting transfers between devices: 0.53 us -> 9.65 us  [swap_cores(): return lax.ppermute(values, 'ctx', [(i, i ^ 1) for i in range(2 * N_Z)])]
    all_gather x4, waiting for transfers between devices: 20.7 us -> 28 us  [gather_ctx(): return lax.all_gather(rows, 'ctx', axis=0, tiled=True)]
  transfers between devices with their start and end apart: 46 -> 46, of which waited for: 20 -> 17; matrix products, arithmetic and copies ran while one was open for 33% -> 34% of each run, Pallas kernels for 1% -> 1%
where the time goes in v4:
time: 552 us; the launch traced here: 543 us
  waiting for transfers between devices  219 us (40%)
  matrix products  101 us (18%)
  starting transfers between devices  81.4 us (15%)
  other arithmetic  75.9 us (14%)
  local copies, waits for them, and re-layouts  31.2 us (6%)
  Pallas kernels  19 us (3%)
  between operations  16.5 us (3%)
    ppermute x24, waiting for transfers between devices, send_dp(): return lax.ppermute(values, ('dp', 'ctx'), moves)  69 us
    reduce_scatter x3, waiting for transfers between devices, scatter_ctx(): lax.psum_scatter(partial, 'ctx', scatter_dimension=0, tiled=True)  61.6 us
    all_to_all x4, waiting for transfers between devices, exchange_ctx(): return lax.all_to_all(blocks, 'ctx', 0, 0, tiled=True)  59.8 us
    dot_general x15, matrix products, t_dot(): lax.dot_general(left, right, (((0,), (0,)), ((), ())), preferred_element_...  51.6 us
    ppermute x24, starting transfers between devices, send_dp(): return lax.ppermute(values, ('dp', 'ctx'), moves)  32.6 us
    dot_general x6, matrix products, dot_t(): lax.dot_general(left, right, (((1,), (1,)), ((), ())), preferred_element_...  29.6 us
    all_gather x4, waiting for transfers between devices, gather_ctx(): return lax.all_gather(rows, 'ctx', axis=0, tiled=True)  28 us
    all_to_all x4, starting transfers between devices, exchange_ctx(): return lax.all_to_all(blocks, 'ctx', 0, 0, tiled=True)  23 us
  transfers between devices with their start and end apart: 46, of which 17 were waited for; matrix products, arithmetic and copies ran while one was open for 34% of the time, Pallas kernels for 1%

profile of v4, /device:TPU:0, one launch (start us, length us, event | category | flops | bytes accessed | tf_op | source)
XLA Modules:
  0.0 543.4 jit_solution(4438376159027156674)
XLA Ops:
  13.4 6.3 %all-to-all-start = ((bf16[8,64,512]{2,1,0:T(8,128)(2,1)}), bf16[8,64,512]{2,1,0:T(8,128)(2,1)}, u32[]{:S(2)}, u32[]{:S(2)}) async-start(bf16[8,64,512]{2,1,0:T(8,128)(2,1)} %bitcast.10), calls=%async_computation | async-start | bytes 1048576 | tf_op jit(solution)/shard_map/all_to_all | solution.py:438
  25.0 30.2 %all-to-all-done = bf16[8,64,512]{2,1,0:T(8,128)(2,1)} async-done(((bf16[8,64,512]{2,1,0:T(8,128)(2,1)}), bf16[8,64,512]{2,1,0:T(8,128)(2,1)}, u32[]{:S(2)}, u32[]{:S(2)}) %all-to-all-start) | async-done | bytes 524320 | tf_op jit(solution)/shard_map/all_to_all | solution.py:438
  56.7 2.9 multiply_convert_fusion.2
  72.1 3.1 pad_maximum_fusion.1
  75.2 8.4 %all-gather.5.cloned.1.call-done = bf16[1024,2048]{1,0:T(8,128)(2,1)} async-done(((bf16[128,2048]{1,0:T(8,128)(2,1)}), bf16[1024,2048]{1,0:T(8,128)(2,1)}) %all-gather.5.cloned.1.call-update) | async-done | bytes 4194320 | tf_op jit(solution)/shard_map/all_gather | solution.py:372
  84.4 4.3 all-to-all-start.1
  89.0 3.2 fusion
  94.6 3.9 fusion.97
  108.8 3.8 collective-permute-done.5
  116.8 18.3 %collective-permute-done.9 = bf16[256,2048]{1,0:T(8,128)(2,1)} collective-permute-done((bf16[256,2048]{1,0:T(8,128)(2,1)}, bf16[256,2048]{1,0:T(8,128)(2,1)}, u32[]{:S(2)}, u32[]{:S(2)}) %collective-permute-start.9) | collective-permute-done | bytes 1048608 | tf_op jit(solution)/shard_map/ppermute | solution.py:406
  139.9 3.3 convolution_convert_fusion.2
  143.2 7.0 %collective-permute-done.10 = bf16[256,2048]{1,0:T(8,128)(2,1)} collective-permute-done((bf16[256,2048]{1,0:T(8,128)(2,1)}, bf16[256,2048]{1,0:T(8,128)(2,1)}, u32[]{:S(2)}, u32[]{:S(2)}) %collective-permute-start.10) | collective-permute-done | bytes 1048608 | tf_op jit(solution)/shard_map/ppermute | solution.py:406
  150.1 21.4 %all-to-all-done.1 = bf16[8,64,2048]{2,1,0:T(8,128)(2,1)} async-done(((bf16[8,64,2048]{2,1,0:T(8,128)(2,1)}), bf16[8,64,2048]{2,1,0:T(8,128)(2,1)}, u32[]{:S(2)}, u32[]{:S(2)}) %all-to-all-start.1) | async-done | bytes 2097184 | tf_op jit(solution)/shard_map/all_to_all | solution.py:438
  174.1 46.5 %reduce-scatter.4.cloned.1.call-done = bf16[128,2048]{1,0:T(8,128)(2,1)} async-done(((bf16[1024,2048]{1,0:T(8,128)(2,1)}), bf16[128,2048]{1,0:T(8,128)(2,1)}) %reduce-scatter.4.cloned.1.call-update) | async-done | bytes 524304 | tf_op jit(solution)/shard_map/reduce_scatter | solution.py:376
  233.2 6.1 %fusion.124.grad_ref = f32[1024,1024]{1,0:T(8,128)} fusion(bf16[1024,2048]{1,0:T(8,128)(2,1)S(1)} %copy-done.48, bf16[1024,2048]{1,0:T(8,128)(2,1)S(1)} %constant_dynamic-update-slice_fusion), kind=kOutput, calls=%fused_computation.225 | convolution fusion | flops 4294967296 | bytes 12582912 | tf_op jit(solution)/shard_map/dot_general | solution.py:555
  241.8 13.3 %collective-permute-done.13 = bf16[512,2048]{1,0:T(8,128)(2,1)S(1)} collective-permute-done((bf16[512,2048]{1,0:T(8,128)(2,1)}, bf16[512,2048]{1,0:T(8,128)(2,1)S(1)}, u32[]{:S(2)}, u32[]{:S(2)}) %collective-permute-start.13) | collective-permute-done | bytes 2097184 | tf_op jit(solution)/shard_map/ppermute | solution.py:406
  255.1 5.7 %pad_maximum_fusion.gate_ref.up_ref = bf16[2048,2048]{1,0:T(8,128)(2,1)} fusion(bf16[512,2048]{1,0:T(8,128)(2,1)S(1)} %collective-permute-done.13, bf16[512,2048]{1,0:T(8,128)(2,1)S(1)} %get-tuple-element.130, bf16[512,2048]{1,0:T(8,128)(2,1)S(1)} %get-tuple-element.129, bf16[512,2048]{1,0:T(8,128)(2,1)} %bitcast.17), kind=kLoop, calls=%fused_computation.4 | loop fusion | flops 33554432 | bytes 16777216 | tf_op jit(solution)/shard_map/concatenate | solution.py:434
  260.8 9.7 %all-gather.9.cloned.1.call-done.hat_ref = bf16[1024,2048]{1,0:T(8,128)(2,1)} async-done(((bf16[128,2048]{1,0:T(8,128)(2,1)}), bf16[1024,2048]{1,0:T(8,128)(2,1)}) %all-gather.9.cloned.1.call-update) | async-done | bytes 4194320 | tf_op jit(solution)/shard_map/all_gather | solution.py:372
  270.5 14.5 %shard_map.203 = (bf16[1024,1024]{1,0:T(8,128)(2,1)S(1)}, bf16[1024,2048]{1,0:T(8,128)(2,1)S(1)}) custom-call(bf16[1024,2048]{1,0:T(8,128)(2,1)} %all-gather.9.cloned.1.call-done.hat_ref, bf16[2048,2048]{1,0:T(8,128)(2,1)} %pad_maximum_fusion.gate_ref.up_ref, bf16[2048,2048]{1,0:T(8,128)(2,1)} %pad_maximum_fusion.gate_ref.up_ref, f32[1024,1024]{1,0:T(8,128)} %fusion.124.grad_ref), custom_call_target="tpu_custom_call" | custom-call | flops 8589934592 | bytes 23068672 | tf_op jit(solution)/shard_map/pallas_call | solution.py:493
  288.3 10.5 %convolution_convert_fusion.1 = bf16[1024,2048]{1,0:T(8,128)(2,1)} fusion(bf16[1024,2048]{1,0:T(8,128)(2,1)S(1)} %get-tuple-element.94, bf16[2048,2048]{1,0:T(8,128)(2,1)S(1)} %copy-done.14), kind=kOutput, calls=%fused_computation.13 | convolution fusion | flops 8592031744 | bytes 16777216 | tf_op jit(solution)/shard_map/dot_general | solution.py:555
  299.4 6.4 %convolution_convert_fusion.4 = bf16[512,2048]{1,0:T(8,128)(2,1)} fusion(bf16[1024,2048]{1,0:T(8,128)(2,1)} %copy-done, bf16[1024,2048]{1,0:T(8,128)(2,1)} %all-gather.9.cloned.1.call-done.hat_ref), kind=kOutput, calls=%fused_computation.17 | convolution fusion | flops 2148532224 | bytes 7340032 | tf_op jit(solution)/shard_map/dot_general | solution.py:558
  311.1 6.3 %convolution_convert_fusion.3 = bf16[512,2048]{1,0:T(8,128)(2,1)} fusion(bf16[1024,2048]{1,0:T(8,128)(2,1)} %copy-done, bf16[1024,2048]{1,0:T(8,128)(2,1)} %all-gather.9.cloned.1.call-done.hat_ref, s32[]{:T(128)S(6)} %select_n.293), kind=kOutput, calls=%fused_computation.16 | convolution fusion | flops 2148532224 | bytes 7340036 | tf_op jit(solution)/shard_map/dot_general | solution.py:558
  318.8 4.8 convolution_convert_fusion.7
  323.7 3.3 add_convert_fusion.5
  327.0 3.2 collective-permute-start.18
  330.3 3.4 convolution_convert_fusion.6
  333.6 5.7 %add_convert_fusion.1 = bf16[512,2048]{1,0:T(8,128)(2,1)} fusion(bf16[512,2048]{1,0:T(8,128)(2,1)} %collective-permute-done.15, bf16[1024,2048]{1,0:T(8,128)(2,1)S(1)} %copy-done.1, bf16[1024,2048]{1,0:T(8,128)(2,1)} %all-gather.9.cloned.1.call-done.hat_ref, s32[]{:T(128)S(6)} %select_n.292), kind=kOutput, calls=%fused_computation.7 | convolution fusion | flops 2150629376 | bytes 9437188 | tf_op jit(solution)/shard_map/dot_general | solution.py:558
  339.4 15.1 %reduce-scatter.6.cloned.1.call-done = bf16[128,2048]{1,0:T(8,128)(2,1)} async-done(((bf16[1024,2048]{1,0:T(8,128)(2,1)}), bf16[128,2048]{1,0:T(8,128)(2,1)}) %reduce-scatter.6.cloned.1.call-update) | async-done | bytes 524304 | tf_op jit(solution)/shard_map/reduce_scatter | solution.py:376
  359.6 3.7 convolution_convert_fusion.5
  363.4 3.7 fusion.46
  371.6 3.1 collective-permute-start.23
  374.8 20.5 %collective-permute-done.20 = bf16[512,2048]{1,0:T(8,128)(2,1)} collective-permute-done((bf16[512,2048]{1,0:T(8,128)(2,1)}, bf16[512,2048]{1,0:T(8,128)(2,1)}, u32[]{:S(2)}, u32[]{:S(2)}) %collective-permute-start.20) | collective-permute-done | bytes 2097184 | tf_op jit(solution)/shard_map/ppermute | solution.py:406
  395.2 4.7 add_convert_fusion
  400.0 4.3 all-to-all-start.2
  404.6 9.9 %all-gather.11.cloned.1.call-done = bf16[1024,2048]{1,0:T(8,128)(2,1)} async-done(((bf16[128,2048]{1,0:T(8,128)(2,1)}), bf16[1024,2048]{1,0:T(8,128)(2,1)}) %all-gather.11.cloned.1.call-update) | async-done | bytes 4194320 | tf_op jit(solution)/shard_map/all_gather | solution.py:372
  414.5 4.2 fusion.24
  423.5 3.7 add_convert_fusion.3
  440.9 5.5 %convolution_convert_fusion = bf16[1024,2048]{1,0:T(8,128)(2,1)} fusion(bf16[512,512]{1,0:T(8,128)(2,1)S(1)} %copy-done.53, bf16[512,512]{1,0:T(8,128)(2,1)S(1)} %copy-done.42, bf16[512,512]{1,0:T(8,128)(2,1)S(1)} %copy-done.40, bf16[512,512]{1,0:T(8,128)(2,1)} %bitcast.11, bf16[1024,256]{0,1:T(8,128)(2,1)S(1)} %fusion.40, ...), kind=kOutput, calls=%fused_computation.12 | convolution fusion | flops 2161115136 | bytes 7340032 | tf_op jit(solution)/shard_map/dot_general | solution.py:555
  448.4 8.2 %all-to-all-done.2.sums_ref = bf16[8,64,2048]{2,1,0:T(8,128)(2,1)} async-done(((bf16[8,64,2048]{2,1,0:T(8,128)(2,1)}), bf16[8,64,2048]{2,1,0:T(8,128)(2,1)}, u32[]{:S(2)}, u32[]{:S(2)}) %all-to-all-start.2) | async-done | bytes 2097184 | tf_op jit(solution)/shard_map/all_to_all | solution.py:438
  456.6 3.1 convolution_convert_fusion.11
  473.4 3.7 fusion.84
  479.1 3.8 collective-permute-done.29
  485.8 8.0 %all-to-all-start.3 = ((bf16[8,64,512]{2,1,0:T(8,128)(2,1)}), bf16[8,64,512]{2,1,0:T(8,128)(2,1)S(1)}, u32[]{:S(2)}, u32[]{:S(2)}) async-start(bf16[8,64,512]{2,1,0:T(8,128)(2,1)} %bitcast.105), calls=%async_computation.6 | async-start | bytes 1048576 | tf_op jit(solution)/shard_map/all_to_all | solution.py:438
  493.8 3.6 add_convert_fusion.2
  497.4 5.1 collective-permute-start.30
  506.3 3.3 convert_add_fusion
  509.6 4.5 shard_map.204
  523.9 7.6 %collective-permute-start.31 = (bf16[128,2048]{1,0:T(8,128)(2,1)}, bf16[128,2048]{1,0:T(8,128)(2,1)S(1)}, u32[]{:S(2)}, u32[]{:S(2)}) collective-permute-start(bf16[128,2048]{1,0:T(8,128)(2,1)} %select_convert_fusion), channel_id=1, source_target_pairs={{0,1},{1,0},{2,3},{3,2},{4,5},{5,4},{6,7},{7,6},{8,9},{9,8},{10,11... | collective-permute-start | bytes 1572872 | tf_op jit(solution)/shard_map/ppermute | solution.py:368
  (281 shorter events, 142.2 us)
Async XLA Ops:
  7.2 76.4 %all-gather.5.cloned.1.call-start = ((), (), s32[]{:S(2)}) async-start(), calls=%async_computation.7 | async-start | bytes 4718592 | tf_op jit(solution)/shard_map/all_gather | solution.py:372
  11.4 45.3 %copy-start.3 = (f32[64,8192]{1,0:T(8,128)S(1)}, f32[64,8192]{1,0:T(8,128)}, u32[]{:S(2)}) copy-start(f32[64,8192]{1,0:T(8,128)} %gate_ref.1) | copy-start | bytes 6291460
  13.4 41.8 %all-to-all-start = ((bf16[8,64,512]{2,1,0:T(8,128)(2,1)}), bf16[8,64,512]{2,1,0:T(8,128)(2,1)}, u32[]{:S(2)}, u32[]{:S(2)}) async-start(bf16[8,64,512]{2,1,0:T(8,128)(2,1)} %bitcast.10), calls=%async_computation | async-start | bytes 1048576 | tf_op jit(solution)/shard_map/all_to_all | solution.py:438
  19.7 151.8 %all-gather.7.cloned.1.call-start = ((), (), s32[]{:S(2)}) async-start(), calls=%async_computation.8 | async-start | bytes 4718592 | tf_op jit(solution)/shard_map/all_gather | solution.py:372
  20.9 54.3 %collective-permute-start = (bf16[64,2048]{1,0:T(8,128)(2,1)S(1)}, bf16[64,2048]{1,0:T(8,128)(2,1)}, u32[]{:S(2)}, u32[]{:S(2)}) collective-permute-start(bf16[64,2048]{1,0:T(8,128)(2,1)S(1)} %convert_element_type.316), channel_id=1, source_target_pairs={{0,0},{1,8},{2,16},{3,24},{4,1},{5,9},{6,17},{7,25},{8,2},{9,10},{... | collective-permute-start | bytes 786440 | tf_op jit(solution)/shard_map/ppermute | solution.py:581
  55.2 19.9 %collective-permute-start.1 = (bf16[512,512]{1,0:T(8,128)(2,1)}, bf16[512,512]{1,0:T(8,128)(2,1)}, u32[]{:S(2)}, u32[]{:S(2)}) collective-permute-start(bf16[512,512]{1,0:T(8,128)(2,1)} %bitcast.11), channel_id=1, source_target_pairs={{0,8},{1,17},{2,10},{3,19},{4,12},{5,21},{6,14},{7,23},{8,0},{9,25... | collective-permute-start | bytes 1572872 | tf_op jit(solution)/shard_map/ppermute | solution.py:406
  56.6 18.5 %collective-permute-start.2 = (bf16[512,512]{1,0:T(8,128)(2,1)}, bf16[512,512]{1,0:T(8,128)(2,1)}, u32[]{:S(2)}, u32[]{:S(2)}) collective-permute-start(bf16[512,512]{1,0:T(8,128)(2,1)} %bitcast.11), channel_id=1, source_target_pairs={{0,16},{1,9},{2,18},{3,11},{4,20},{5,13},{6,22},{7,15},{8,24},{9,1... | collective-permute-start | bytes 1572872 | tf_op jit(solution)/shard_map/ppermute | solution.py:406
  84.3 10.1 %collective-permute-start.3 = (bf16[512,512]{1,0:T(8,128)(2,1)}, bf16[512,512]{1,0:T(8,128)(2,1)S(1)}, u32[]{:S(2)}, u32[]{:S(2)}) collective-permute-start(bf16[512,512]{1,0:T(8,128)(2,1)} %collective-permute-done.1), channel_id=1, source_target_pairs={{0,16},{1,9},{2,18},{3,11},{4,20},{5,13},{6,22},{7,15},{8,24},{9,1... | collective-permute-start | bytes 1572872 | tf_op jit(solution)/shard_map/ppermute | solution.py:406
  84.4 87.1 %all-to-all-start.1 = ((bf16[8,64,2048]{2,1,0:T(8,128)(2,1)}), bf16[8,64,2048]{2,1,0:T(8,128)(2,1)}, u32[]{:S(2)}, u32[]{:S(2)}) async-start(bf16[8,64,2048]{2,1,0:T(8,128)(2,1)} %bitcast.92), calls=%async_computation.1 | async-start | bytes 4194304 | tf_op jit(solution)/shard_map/all_to_all | solution.py:438
  88.7 131.8 %reduce-scatter.4.cloned.1.call-start = ((), (), s32[]{:S(2)}) async-start(), calls=%async_computation.9 | async-start | bytes 4718592 | tf_op jit(solution)/shard_map/reduce_scatter | solution.py:376
  103.2 9.4 %collective-permute-start.5 = (bf16[64,2048]{1,0:T(8,128)(2,1)}, bf16[64,2048]{1,0:T(8,128)(2,1)S(1)}, u32[]{:S(2)}, u32[]{:S(2)}) collective-permute-start(bf16[64,2048]{1,0:T(8,128)(2,1)} %collective-permute-done), channel_id=1, source_target_pairs={{0,8},{1,17},{2,10},{3,19},{4,12},{5,21},{6,14},{7,23},{8,0},{9,25... | collective-permute-start | bytes 786440 | tf_op jit(solution)/shard_map/ppermute | solution.py:406
  105.5 9.4 %collective-permute-start.6 = (bf16[64,2048]{1,0:T(8,128)(2,1)}, bf16[64,2048]{1,0:T(8,128)(2,1)S(1)}, u32[]{:S(2)}, u32[]{:S(2)}) collective-permute-start(bf16[64,2048]{1,0:T(8,128)(2,1)} %collective-permute-done), channel_id=1, source_target_pairs={{0,16},{1,9},{2,18},{3,11},{4,20},{5,13},{6,22},{7,15},{8,24},{9,1... | collective-permute-start | bytes 786440 | tf_op jit(solution)/shard_map/ppermute | solution.py:406
  105.5 37.6 %collective-permute-start.8 = (bf16[256,2048]{1,0:T(8,128)(2,1)}, bf16[256,2048]{1,0:T(8,128)(2,1)}, u32[]{:S(2)}, u32[]{:S(2)}) collective-permute-start(bf16[256,2048]{1,0:T(8,128)(2,1)} %convert_element_type.317), channel_id=1, source_target_pairs={{0,16},{1,9},{2,18},{3,11},{4,20},{5,13},{6,22},{7,15},{8,24},{9,1... | collective-permute-start | bytes 3145736 | tf_op jit(solution)/shard_map/ppermute | solution.py:406
  107.6 27.5 %collective-permute-start.9 = (bf16[256,2048]{1,0:T(8,128)(2,1)}, bf16[256,2048]{1,0:T(8,128)(2,1)}, u32[]{:S(2)}, u32[]{:S(2)}) collective-permute-start(bf16[256,2048]{1,0:T(8,128)(2,1)} %convert_element_type.317), channel_id=1, source_target_pairs={{0,8},{1,17},{2,10},{3,19},{4,12},{5,21},{6,14},{7,23},{8,0},{9,25... | collective-permute-start | bytes 3145736 | tf_op jit(solution)/shard_map/ppermute | solution.py:406
  107.7 7.2 %collective-permute-start.4 = (bf16[1024,256]{0,1:T(8,128)(2,1)S(1)}, bf16[1024,256]{0,1:T(8,128)(2,1)S(1)}, u32[]{:S(2)}, u32[]{:S(2)}) collective-permute-start(bf16[1024,256]{0,1:T(8,128)(2,1)S(1)} %fusion.38), channel_id=1, source_target_pairs={{0,1},{1,0},{2,3},{3,2},{4,5},{5,4},{6,7},{7,6},{8,9},{9,8},{10,11... | collective-permute-start | bytes 1572872 | tf_op jit(solution)/shard_map/ppermute | solution.py:368
  112.6 25.0 %collective-permute-start.7 = (bf16[64,2048]{1,0:T(8,128)(2,1)S(1)}, bf16[64,2048]{1,0:T(8,128)(2,1)S(1)}, u32[]{:S(2)}, u32[]{:S(2)}) collective-permute-start(bf16[64,2048]{1,0:T(8,128)(2,1)S(1)} %collective-permute-done.5), channel_id=1, source_target_pairs={{0,16},{1,9},{2,18},{3,11},{4,20},{5,13},{6,22},{7,15},{8,24},{9,1... | collective-permute-start | bytes 786440 | tf_op jit(solution)/shard_map/ppermute | solution.py:406
  135.0 15.1 %collective-permute-start.10 = (bf16[256,2048]{1,0:T(8,128)(2,1)}, bf16[256,2048]{1,0:T(8,128)(2,1)}, u32[]{:S(2)}, u32[]{:S(2)}) collective-permute-start(bf16[256,2048]{1,0:T(8,128)(2,1)} %collective-permute-done.9), channel_id=1, source_target_pairs={{0,16},{1,9},{2,18},{3,11},{4,20},{5,13},{6,22},{7,15},{8,24},{9,1... | collective-permute-start | bytes 3145736 | tf_op jit(solution)/shard_map/ppermute | solution.py:406
  143.2 77.4 %copy-start.11 = (bf16[1,128,2048]{2,1,0:T(8,128)(2,1)S(1)}, bf16[1,128,2048]{2,1,0:T(8,128)(2,1)}, u32[]{:S(2)}) copy-start(bf16[1,128,2048]{2,1,0:T(8,128)(2,1)} %param.12) | copy-start | bytes 1572868
  171.5 99.0 %all-gather.9.cloned.1.call-start = ((), (), s32[]{:S(2)}) async-start(), calls=%async_computation.10 | async-start | bytes 4718592 | tf_op jit(solution)/shard_map/all_gather | solution.py:372
  171.6 53.4 %collective-permute-start.11 = (bf16[512,2048]{1,0:T(8,128)(2,1)}, bf16[512,2048]{1,0:T(8,128)(2,1)}, u32[]{:S(2)}, u32[]{:S(2)}) collective-permute-start(bf16[512,2048]{1,0:T(8,128)(2,1)} %bitcast.17), channel_id=1, source_target_pairs={{0,8},{1,17},{2,10},{3,19},{4,12},{5,21},{6,14},{7,23},{8,0},{9,25... | collective-permute-start | bytes 6291464 | tf_op jit(solution)/shard_map/ppermute | solution.py:406
  174.0 51.0 %collective-permute-start.12 = (bf16[512,2048]{1,0:T(8,128)(2,1)}, bf16[512,2048]{1,0:T(8,128)(2,1)}, u32[]{:S(2)}, u32[]{:S(2)}) collective-permute-start(bf16[512,2048]{1,0:T(8,128)(2,1)} %bitcast.17), channel_id=1, source_target_pairs={{0,16},{1,9},{2,18},{3,11},{4,20},{5,13},{6,22},{7,15},{8,24},{9,1... | collective-permute-start | bytes 6291464 | tf_op jit(solution)/shard_map/ppermute | solution.py:406
  225.0 129.5 %reduce-scatter.6.cloned.1.call-start = ((), (), s32[]{:S(2)}) async-start(), calls=%async_computation.11 | async-start | bytes 4718592 | tf_op jit(solution)/shard_map/reduce_scatter | solution.py:376
  228.8 26.3 %collective-permute-start.13 = (bf16[512,2048]{1,0:T(8,128)(2,1)}, bf16[512,2048]{1,0:T(8,128)(2,1)S(1)}, u32[]{:S(2)}, u32[]{:S(2)}) collective-permute-start(bf16[512,2048]{1,0:T(8,128)(2,1)} %collective-permute-done.11), channel_id=1, source_target_pairs={{0,16},{1,9},{2,18},{3,11},{4,20},{5,13},{6,22},{7,15},{8,24},{9,1... | collective-permute-start | bytes 6291464 | tf_op jit(solution)/shard_map/ppermute | solution.py:406
  298.8 115.7 %all-gather.11.cloned.1.call-start = ((), (), s32[]{:S(2)}) async-start(), calls=%async_computation.12 | async-start | bytes 4718592 | tf_op jit(solution)/shard_map/all_gather | solution.py:372
  305.7 27.9 %collective-permute-start.15 = (bf16[512,2048]{1,0:T(8,128)(2,1)}, bf16[512,2048]{1,0:T(8,128)(2,1)}, u32[]{:S(2)}, u32[]{:S(2)}) collective-permute-start(bf16[512,2048]{1,0:T(8,128)(2,1)} %convolution_convert_fusion.4), channel_id=1, source_target_pairs={{0,16},{1,9},{2,18},{3,11},{4,20},{5,13},{6,22},{7,15},{8,24},{9,1... | collective-permute-start | bytes 6291464 | tf_op jit(solution)/shard_map/ppermute | solution.py:406
  311.1 12.6 %collective-permute-start.17 = (bf16[256,2048]{1,0:T(8,128)(2,1)}, bf16[256,2048]{1,0:T(8,128)(2,1)}, u32[]{:S(2)}, u32[]{:S(2)}) collective-permute-start(bf16[256,2048]{1,0:T(8,128)(2,1)} %get-tuple-element.177), channel_id=1, source_target_pairs={{0,1},{1,0},{2,3},{3,2},{4,5},{5,4},{6,7},{7,6},{8,9},{9,8},{10,11... | collective-permute-start | bytes 3145736 | tf_op jit(solution)/shard_map/ppermute | solution.py:368
  317.4 38.4 %collective-permute-start.16 = (bf16[512,2048]{1,0:T(8,128)(2,1)}, bf16[512,2048]{1,0:T(8,128)(2,1)}, u32[]{:S(2)}, u32[]{:S(2)}) collective-permute-start(bf16[512,2048]{1,0:T(8,128)(2,1)} %convolution_convert_fusion.3), channel_id=1, source_target_pairs={{0,16},{1,9},{2,18},{3,11},{4,20},{5,13},{6,22},{7,15},{8,24},{9,1... | collective-permute-start | bytes 6291464 | tf_op jit(solution)/shard_map/ppermute | solution.py:406
  327.0 28.8 %collective-permute-start.18 = (bf16[256,2048]{1,0:T(8,128)(2,1)}, bf16[256,2048]{1,0:T(8,128)(2,1)}, u32[]{:S(2)}, u32[]{:S(2)}) collective-permute-start(bf16[256,2048]{1,0:T(8,128)(2,1)} %get-tuple-element.127), channel_id=1, source_target_pairs={{0,2},{7,5},{8,10},{15,13},{16,18},{23,21},{24,26},{31,29}} | collective-permute-start | bytes 3145736 | tf_op jit(solution)/shard_map/ppermute | solution.py:382
  357.6 37.7 %collective-permute-start.20 = (bf16[512,2048]{1,0:T(8,128)(2,1)}, bf16[512,2048]{1,0:T(8,128)(2,1)}, u32[]{:S(2)}, u32[]{:S(2)}) collective-permute-start(bf16[512,2048]{1,0:T(8,128)(2,1)} %add_convert_fusion.1), channel_id=1, source_target_pairs={{0,8},{1,17},{2,10},{3,19},{4,12},{5,21},{6,14},{7,23},{8,0},{9,25... | collective-permute-start | bytes 6291464 | tf_op jit(solution)/shard_map/ppermute | solution.py:406
  363.3 5.6 %collective-permute-start.22 = (bf16[256,2048]{1,0:T(8,128)(2,1)S(1)}, bf16[256,2048]{1,0:T(8,128)(2,1)S(1)}, u32[]{:S(2)}, u32[]{:S(2)}) collective-permute-start(bf16[256,2048]{1,0:T(8,128)(2,1)S(1)} %convolution_convert_fusion.5), channel_id=1, source_target_pairs={{0,1},{1,0},{2,3},{3,2},{4,5},{5,4},{6,7},{7,6},{8,9},{9,8},{10,11... | collective-permute-start | bytes 3145736 | tf_op jit(solution)/shard_map/ppermute | solution.py:368
  367.1 37.5 %collective-permute-start.19 = (bf16[256,2048]{1,0:T(8,128)(2,1)}, bf16[256,2048]{1,0:T(8,128)(2,1)}, u32[]{:S(2)}, u32[]{:S(2)}) collective-permute-start(bf16[256,2048]{1,0:T(8,128)(2,1)} %convolution_convert_fusion.7), channel_id=1, source_target_pairs={{0,16},{1,9},{2,18},{3,11},{4,20},{5,13},{6,22},{7,15},{8,24},{9,1... | collective-permute-start | bytes 3145736 | tf_op jit(solution)/shard_map/ppermute | solution.py:406
  371.6 60.0 %collective-permute-start.23 = (bf16[256,2048]{1,0:T(8,128)(2,1)}, bf16[256,2048]{1,0:T(8,128)(2,1)}, u32[]{:S(2)}, u32[]{:S(2)}) collective-permute-start(bf16[256,2048]{1,0:T(8,128)(2,1)} %add_convert_fusion.4), channel_id=1, source_target_pairs={{0,2},{2,4},{7,5},{5,3},{8,10},{10,12},{15,13},{13,11},{16,18},{18... | collective-permute-start | bytes 3145736 | tf_op jit(solution)/shard_map/ppermute | solution.py:382
  400.0 56.6 %all-to-all-start.2 = ((bf16[8,64,2048]{2,1,0:T(8,128)(2,1)}), bf16[8,64,2048]{2,1,0:T(8,128)(2,1)}, u32[]{:S(2)}, u32[]{:S(2)}) async-start(bf16[8,64,2048]{2,1,0:T(8,128)(2,1)} %bitcast.91), calls=%async_computation.4 | async-start | bytes 4194304 | tf_op jit(solution)/shard_map/all_to_all | solution.py:438
  404.4 127.2 %reduce-scatter.8.cloned.1.call-start = ((), (), s32[]{:S(2)}) async-start(), calls=%async_computation.13 | async-start | bytes 4718592 | tf_op jit(solution)/shard_map/reduce_scatter | solution.py:376
  421.0 10.6 %collective-permute-start.21 = (bf16[64,2048]{1,0:T(8,128)(2,1)S(1)}, bf16[64,2048]{1,0:T(8,128)(2,1)S(1)}, u32[]{:S(2)}, u32[]{:S(2)}) collective-permute-start(bf16[64,2048]{1,0:T(8,128)(2,1)S(1)} %get-tuple-element.136), channel_id=1, source_target_pairs={{0,16},{1,9},{2,18},{3,11},{4,20},{5,13},{6,22},{7,15},{8,24},{9,1... | collective-permute-start | bytes 786440 | tf_op jit(solution)/shard_map/ppermute | solution.py:406
  427.2 19.2 %collective-permute-start.26 = (bf16[256,2048]{1,0:T(8,128)(2,1)}, bf16[256,2048]{1,0:T(8,128)(2,1)}, u32[]{:S(2)}, u32[]{:S(2)}) collective-permute-start(bf16[256,2048]{1,0:T(8,128)(2,1)} %add_convert_fusion.3), channel_id=1, source_target_pairs={{0,8},{1,17},{2,10},{3,19},{4,12},{5,21},{6,14},{7,23},{8,0},{9,25... | collective-permute-start | bytes 3145736 | tf_op jit(solution)/shard_map/ppermute | solution.py:406
  433.9 4.0 collective-permute-start.24
  434.7 11.7 %collective-permute-start.25 = (bf16[64,2048]{1,0:T(8,128)(2,1)}, bf16[64,2048]{1,0:T(8,128)(2,1)}, u32[]{:S(2)}, u32[]{:S(2)}) collective-permute-start(bf16[64,2048]{1,0:T(8,128)(2,1)} %add_convert_fusion.9), channel_id=1, source_target_pairs={{0,8},{1,17},{2,10},{3,19},{4,12},{5,21},{6,14},{7,23},{8,0},{9,25... | collective-permute-start | bytes 786440 | tf_op jit(solution)/shard_map/ppermute | solution.py:406
  459.7 9.4 %collective-permute-start.28 = (bf16[512,512]{1,0:T(8,128)(2,1)}, bf16[512,512]{1,0:T(8,128)(2,1)S(1)}, u32[]{:S(2)}, u32[]{:S(2)}) collective-permute-start(bf16[512,512]{1,0:T(8,128)(2,1)} %convolution_convert_fusion.11), channel_id=1, source_target_pairs={{0,16},{1,9},{2,18},{3,11},{4,20},{5,13},{6,22},{7,15},{8,24},{9,1... | collective-permute-start | bytes 1572872 | tf_op jit(solution)/shard_map/ppermute | solution.py:406
  461.7 32.1 %collective-permute-start.14 = (bf16[256,2048]{1,0:T(8,128)(2,1)}, bf16[256,2048]{1,0:T(8,128)(2,1)}, u32[]{:S(2)}, u32[]{:S(2)}) collective-permute-start(bf16[256,2048]{1,0:T(8,128)(2,1)} %get-tuple-element.128), channel_id=1, source_target_pairs={{0,1},{1,0},{2,3},{3,2},{4,5},{5,4},{6,7},{7,6},{8,9},{9,8},{10,11... | collective-permute-start | bytes 3145736 | tf_op jit(solution)/shard_map/ppermute | solution.py:368
  466.0 13.1 %collective-permute-start.27 = (bf16[512,512]{1,0:T(8,128)(2,1)S(1)}, bf16[512,512]{1,0:T(8,128)(2,1)S(1)}, u32[]{:S(2)}, u32[]{:S(2)}) collective-permute-start(bf16[512,512]{1,0:T(8,128)(2,1)S(1)} %convolution_convert_fusion.12), channel_id=1, source_target_pairs={{0,16},{1,9},{2,18},{3,11},{4,20},{5,13},{6,22},{7,15},{8,24},{9,1... | collective-permute-start | bytes 1572872 | tf_op jit(solution)/shard_map/ppermute | solution.py:406
  471.5 11.4 %collective-permute-start.29 = (bf16[512,512]{1,0:T(8,128)(2,1)S(1)}, bf16[512,512]{1,0:T(8,128)(2,1)S(1)}, u32[]{:S(2)}, u32[]{:S(2)}) collective-permute-start(bf16[512,512]{1,0:T(8,128)(2,1)S(1)} %add_convert_fusion.7), channel_id=1, source_target_pairs={{0,8},{1,17},{2,10},{3,19},{4,12},{5,21},{6,14},{7,23},{8,0},{9,25... | collective-permute-start | bytes 1572872 | tf_op jit(solution)/shard_map/ppermute | solution.py:406
  477.1 29.2 %collective-permute-start.34 = (bf16[256,2048]{1,0:T(8,128)(2,1)}, bf16[256,2048]{1,0:T(8,128)(2,1)}, u32[]{:S(2)}, u32[]{:S(2)}) collective-permute-start(bf16[256,2048]{1,0:T(8,128)(2,1)} %convolution_convert_fusion.6), channel_id=1, source_target_pairs={{0,16},{1,9},{2,18},{3,11},{4,20},{5,13},{6,22},{7,15},{8,24},{9,1... | collective-permute-start | bytes 3145736 | tf_op jit(solution)/shard_map/ppermute | solution.py:406
  478.8 23.6 %collective-permute-start.32 = (bf16[64,2048]{1,0:T(8,128)(2,1)S(1)}, bf16[64,2048]{1,0:T(8,128)(2,1)}, u32[]{:S(2)}, u32[]{:S(2)}) collective-permute-start(bf16[64,2048]{1,0:T(8,128)(2,1)S(1)} %copy-done.45), channel_id=1, source_target_pairs={{0,16},{1,9},{2,18},{3,11},{4,20},{5,13},{6,22},{7,15},{8,24},{9,1... | collective-permute-start | bytes 786440 | tf_op jit(solution)/shard_map/ppermute | solution.py:406
  485.8 29.0 %all-to-all-start.3 = ((bf16[8,64,512]{2,1,0:T(8,128)(2,1)}), bf16[8,64,512]{2,1,0:T(8,128)(2,1)S(1)}, u32[]{:S(2)}, u32[]{:S(2)}) async-start(bf16[8,64,512]{2,1,0:T(8,128)(2,1)} %bitcast.105), calls=%async_computation.6 | async-start | bytes 1048576 | tf_op jit(solution)/shard_map/all_to_all | solution.py:438
  497.4 21.7 %collective-permute-start.30 = (bf16[256,2048]{1,0:T(8,128)(2,1)}, bf16[256,2048]{1,0:T(8,128)(2,1)}, u32[]{:S(2)}, u32[]{:S(2)}) collective-permute-start(bf16[256,2048]{1,0:T(8,128)(2,1)} %add_convert_fusion.2), channel_id=1, source_target_pairs={{0,2},{2,4},{4,6},{7,5},{5,3},{3,1},{8,10},{10,12},{12,14},{15,13}... | collective-permute-start | bytes 3145736 | tf_op jit(solution)/shard_map/ppermute | solution.py:382
  504.4 10.4 %collective-permute-start.33 = (bf16[64,2048]{1,0:T(8,128)(2,1)}, bf16[64,2048]{1,0:T(8,128)(2,1)S(1)}, u32[]{:S(2)}, u32[]{:S(2)}) collective-permute-start(bf16[64,2048]{1,0:T(8,128)(2,1)} %add_convert_fusion.8), channel_id=1, source_target_pairs={{0,0},{8,1},{16,2},{24,3},{1,4},{9,5},{17,6},{25,7},{2,8},{10,9},{... | collective-permute-start | bytes 786440 | tf_op jit(solution)/shard_map/ppermute | solution.py:753
  523.9 9.3 %collective-permute-start.31 = (bf16[128,2048]{1,0:T(8,128)(2,1)}, bf16[128,2048]{1,0:T(8,128)(2,1)S(1)}, u32[]{:S(2)}, u32[]{:S(2)}) collective-permute-start(bf16[128,2048]{1,0:T(8,128)(2,1)} %select_convert_fusion), channel_id=1, source_target_pairs={{0,1},{1,0},{2,3},{3,2},{4,5},{5,4},{6,7},{7,6},{8,9},{9,8},{10,11... | collective-permute-start | bytes 1572872 | tf_op jit(solution)/shard_map/ppermute | solution.py:368
  (53 other events, 365.0 us)
Sparse Core Ops, SparseCore 0:
  10.2 73.3 all-gather.4
  85.2 84.4 all-gather.6
  172.0 48.4 reduce-scatter.3
  225.2 45.2 all-gather.8
  298.9 55.5 reduce-scatter.5
  357.7 56.7 all-gather.10
  446.5 53.6 reduce-scatter.7

commit v5 on v4

--- a/solution.py
+++ b/solution.py
@@ -706,12 +706,17 @@
 
     gate_up_source = gate_up_sum.reshape(2 * N_Z, rows, 2 * width)
     gate_up_sum = exchange_ctx(gate_up_source)
-    all_branch, down_across = lax.optimization_barrier((all_branch, down_across, gate_up_source))[:2]
+    down_across, down_far = lax.optimization_barrier((down_across, down_far, gate_up_source))[:2]
+    down_relay = (down_block(near_bit()) + down_across.astype(wide)).astype(low)
+    down_own_sum = down_block(0) + down_far.astype(wide)
+    all_branch, down_relay, down_own_sum = lax.optimization_barrier(
+        (all_branch, down_relay, down_own_sum, gate_up_source)
+    )[:3]
+    down_near = send_dp(down_relay, 1, 2)
 
     def out_block(j):
         return lax.dynamic_slice_in_dim(head_part, (d ^ j) * rows, rows, 0)
 
-    down_near = send_dp((down_block(near_bit()) + down_across.astype(wide)).astype(low), 1, 2)
     d_attn = dot_t(all_branch, out_w).astype(low)
     head_part = t_dot(attn, after(all_branch, d_attn))
     out_across = send_dp(out_block(3).astype(low), 2, 1)
@@ -733,7 +738,7 @@
         (e1_part, out_near, down_near, carried)
     )
     e1 = turned(scatter_ctx(e1_part))
-    d_proj, gate_up_sum = lax.optimization_barrier((d_proj, gate_up_sum, e1_part))[:2]
+    d_proj = after(d_proj, e1_part)
 
     def proj_block(j):
         return t_dot(block_columns(all_hat1, j), d_proj)
@@ -741,6 +746,7 @@
     proj_across = send_dp(proj_block(3).astype(low), 2, 1)
     proj_far = send_dp(proj_block(3 - near_bit()).astype(low), 2, 1)
     relayed = (proj_block(near_bit()) + proj_across.astype(wide)).astype(low)
+    relayed, gate_up_sum = lax.optimization_barrier((relayed, gate_up_sum))
     proj_near = send_dp(relayed, 1, 2)
     proj_sum = proj_block(0) + proj_far.astype(wide) + proj_near.astype(wide)
     proj_source = proj_sum.astype(low).reshape(2 * N_Z, rows, cols)
@@ -755,7 +761,7 @@
     )
     out_branch = sum_end(out_slots, carried)
     output = (middle + out_branch).astype(low)[None]
-    down_sum = down_block(0) + down_far.astype(wide) + down_near.astype(wide)
+    down_sum = down_own_sum + down_near.astype(wide)
     out_sum, proj_sum = lax.optimization_barrier((out_sum, proj_sum))
     out_sum = out_sum.astype(wide)
 

time: 552 us -> 549 us (level)
  waiting for transfers between devices: 219 us -> 226 us
  starting transfers between devices: 81.4 us -> 74.6 us
    ppermute x24, waiting for transfers between devices: 69 us -> 90.8 us  [send_dp(): return lax.ppermute(values, ('dp', 'ctx'), moves)]
    all_gather x4, waiting for transfers between devices: 28 us -> 17.9 us  [gather_ctx(): return lax.all_gather(rows, 'ctx', axis=0, tiled=True)]
    all_to_all x4, waiting for transfers between devices: 59.8 us -> 51.1 us  [exchange_ctx(): return lax.all_to_all(blocks, 'ctx', 0, 0, tiled=True)]
  transfers between devices with their start and end apart: 46 -> 46, of which waited for: 17 -> 19; matrix products, arithmetic and copies ran while one was open for 34% -> 34% of each run, Pallas kernels for 1% -> 1%
where the time goes in v5:
time: 549 us; the launch traced here: 543 us
  waiting for transfers between devices  226 us (41%)
  matrix products  101 us (18%)
  other arithmetic  75.2 us (14%)
  starting transfers between devices  74.6 us (14%)
  local copies, waits for them, and re-layouts  30.9 us (6%)
  Pallas kernels  19 us (3%)
  between operations  16.5 us (3%)
    ppermute x24, waiting for transfers between devices, send_dp(): return lax.ppermute(values, ('dp', 'ctx'), moves)  90.8 us
    reduce_scatter x3, waiting for transfers between devices, scatter_ctx(): lax.psum_scatter(partial, 'ctx', scatter_dimension=0, tiled=True)  61.1 us
    dot_general x15, matrix products, t_dot(): lax.dot_general(left, right, (((0,), (0,)), ((), ())), preferred_element_...  51.7 us
    all_to_all x4, waiting for transfers between devices, exchange_ctx(): return lax.all_to_all(blocks, 'ctx', 0, 0, tiled=True)  51.1 us
    dot_general x6, matrix products, dot_t(): lax.dot_general(left, right, (((1,), (1,)), ((), ())), preferred_element_...  29.8 us
    ppermute x24, starting transfers between devices, send_dp(): return lax.ppermute(values, ('dp', 'ctx'), moves)  27.9 us
    all_to_all x4, starting transfers between devices, exchange_ctx(): return lax.all_to_all(blocks, 'ctx', 0, 0, tiled=True)  20 us
    dot_general x8, matrix products, dot(): return jnp.dot(left, right, preferred_element_type=wide)  19.3 us
  transfers between devices with their start and end apart: 46, of which 19 were waited for; matrix products, arithmetic and copies ran while one was open for 34% of the time, Pallas kernels for 1%

profile of v5, /device:TPU:0, one launch (start us, length us, event | category | flops | bytes accessed | tf_op | source)
XLA Modules:
  0.0 543.1 jit_solution(2267251572714084230)
XLA Ops:
  14.4 6.3 %all-to-all-start = ((bf16[8,64,512]{2,1,0:T(8,128)(2,1)}), bf16[8,64,512]{2,1,0:T(8,128)(2,1)}, u32[]{:S(2)}, u32[]{:S(2)}) async-start(bf16[8,64,512]{2,1,0:T(8,128)(2,1)} %bitcast.10), calls=%async_computation | async-start | bytes 1048576 | tf_op jit(solution)/shard_map/all_to_all | solution.py:438
  25.8 30.0 %all-to-all-done = bf16[8,64,512]{2,1,0:T(8,128)(2,1)} async-done(((bf16[8,64,512]{2,1,0:T(8,128)(2,1)}), bf16[8,64,512]{2,1,0:T(8,128)(2,1)}, u32[]{:S(2)}, u32[]{:S(2)}) %all-to-all-start) | async-done | bytes 524320 | tf_op jit(solution)/shard_map/all_to_all | solution.py:438
  75.8 8.2 %all-gather.5.cloned.1.call-done = bf16[1024,2048]{1,0:T(8,128)(2,1)} async-done(((bf16[128,2048]{1,0:T(8,128)(2,1)}), bf16[1024,2048]{1,0:T(8,128)(2,1)}) %all-gather.5.cloned.1.call-update) | async-done | bytes 4194320 | tf_op jit(solution)/shard_map/all_gather | solution.py:372
  84.7 4.3 all-to-all-start.1
  94.8 4.0 collective-permute-done.3
  98.8 3.7 fusion.99
  111.5 5.1 collective-permute-done.5
  119.5 19.5 %collective-permute-done.9 = bf16[256,2048]{1,0:T(8,128)(2,1)} collective-permute-done((bf16[256,2048]{1,0:T(8,128)(2,1)}, bf16[256,2048]{1,0:T(8,128)(2,1)}, u32[]{:S(2)}, u32[]{:S(2)}) %collective-permute-start.9) | collective-permute-done | bytes 1048608 | tf_op jit(solution)/shard_map/ppermute | solution.py:406
  142.7 3.2 convolution_convert_fusion.2
  145.9 8.2 %collective-permute-done.10 = bf16[256,2048]{1,0:T(8,128)(2,1)} collective-permute-done((bf16[256,2048]{1,0:T(8,128)(2,1)}, bf16[256,2048]{1,0:T(8,128)(2,1)}, u32[]{:S(2)}, u32[]{:S(2)}) %collective-permute-start.10) | collective-permute-done | bytes 1048608 | tf_op jit(solution)/shard_map/ppermute | solution.py:406
  154.1 17.7 %all-to-all-done.1 = bf16[8,64,2048]{2,1,0:T(8,128)(2,1)} async-done(((bf16[8,64,2048]{2,1,0:T(8,128)(2,1)}), bf16[8,64,2048]{2,1,0:T(8,128)(2,1)}, u32[]{:S(2)}, u32[]{:S(2)}) %all-to-all-start.1) | async-done | bytes 2097184 | tf_op jit(solution)/shard_map/all_to_all | solution.py:438
  174.3 45.9 %reduce-scatter.4.cloned.1.call-done = bf16[128,2048]{1,0:T(8,128)(2,1)} async-done(((bf16[1024,2048]{1,0:T(8,128)(2,1)}), bf16[128,2048]{1,0:T(8,128)(2,1)}) %reduce-scatter.4.cloned.1.call-update) | async-done | bytes 524304 | tf_op jit(solution)/shard_map/reduce_scatter | solution.py:376
  232.9 6.1 %fusion.126.grad_ref = f32[1024,1024]{1,0:T(8,128)} fusion(bf16[1024,2048]{1,0:T(8,128)(2,1)S(1)} %copy-done.14, bf16[1024,2048]{1,0:T(8,128)(2,1)S(1)} %constant_dynamic-update-slice_fusion), kind=kOutput, calls=%fused_computation.226 | convolution fusion | flops 4294967296 | bytes 12582912 | tf_op jit(solution)/shard_map/dot_general | solution.py:555
  241.6 13.3 %collective-permute-done.13 = bf16[512,2048]{1,0:T(8,128)(2,1)S(1)} collective-permute-done((bf16[512,2048]{1,0:T(8,128)(2,1)}, bf16[512,2048]{1,0:T(8,128)(2,1)S(1)}, u32[]{:S(2)}, u32[]{:S(2)}) %collective-permute-start.13) | collective-permute-done | bytes 2097184 | tf_op jit(solution)/shard_map/ppermute | solution.py:406
  254.9 5.7 %pad_maximum_fusion.gate_ref.up_ref = bf16[2048,2048]{1,0:T(8,128)(2,1)} fusion(bf16[512,2048]{1,0:T(8,128)(2,1)S(1)} %collective-permute-done.13, bf16[512,2048]{1,0:T(8,128)(2,1)S(1)} %get-tuple-element.138, bf16[512,2048]{1,0:T(8,128)(2,1)S(1)} %get-tuple-element.137, bf16[512,2048]{1,0:T(8,128)(2,1)} %bitcast.17), kind=kLoop, calls=%fused_computation.4 | loop fusion | flops 33554432 | bytes 16777216 | tf_op jit(solution)/shard_map/concatenate | solution.py:434
  260.5 9.7 %all-gather.9.cloned.1.call-done.hat_ref = bf16[1024,2048]{1,0:T(8,128)(2,1)} async-done(((bf16[128,2048]{1,0:T(8,128)(2,1)}), bf16[1024,2048]{1,0:T(8,128)(2,1)}) %all-gather.9.cloned.1.call-update) | async-done | bytes 4194320 | tf_op jit(solution)/shard_map/all_gather | solution.py:372
  270.2 14.5 %shard_map.203 = (bf16[1024,1024]{1,0:T(8,128)(2,1)S(1)}, bf16[1024,2048]{1,0:T(8,128)(2,1)S(1)}) custom-call(bf16[1024,2048]{1,0:T(8,128)(2,1)} %all-gather.9.cloned.1.call-done.hat_ref, bf16[2048,2048]{1,0:T(8,128)(2,1)} %pad_maximum_fusion.gate_ref.up_ref, bf16[2048,2048]{1,0:T(8,128)(2,1)} %pad_maximum_fusion.gate_ref.up_ref, f32[1024,1024]{1,0:T(8,128)} %fusion.126.grad_ref), custom_call_target="tpu_custom_call" | custom-call | flops 8589934592 | bytes 23068672 | tf_op jit(solution)/shard_map/pallas_call | solution.py:493
  288.0 10.5 %convolution_convert_fusion.1 = bf16[1024,2048]{1,0:T(8,128)(2,1)} fusion(bf16[1024,2048]{1,0:T(8,128)(2,1)S(1)} %get-tuple-element.98, bf16[2048,2048]{1,0:T(8,128)(2,1)S(1)} %copy-done.17), kind=kOutput, calls=%fused_computation.13 | convolution fusion | flops 8592031744 | bytes 16777216 | tf_op jit(solution)/shard_map/dot_general | solution.py:555
  299.1 6.4 %convolution_convert_fusion.4 = bf16[512,2048]{1,0:T(8,128)(2,1)} fusion(bf16[1024,2048]{1,0:T(8,128)(2,1)} %copy-done, bf16[1024,2048]{1,0:T(8,128)(2,1)} %all-gather.9.cloned.1.call-done.hat_ref), kind=kOutput, calls=%fused_computation.17 | convolution fusion | flops 2148532224 | bytes 7340032 | tf_op jit(solution)/shard_map/dot_general | solution.py:558
  310.9 6.3 %convolution_convert_fusion.3 = bf16[512,2048]{1,0:T(8,128)(2,1)} fusion(bf16[1024,2048]{1,0:T(8,128)(2,1)} %copy-done, bf16[1024,2048]{1,0:T(8,128)(2,1)} %all-gather.9.cloned.1.call-done.hat_ref, s32[]{:T(128)S(6)} %select_n.293), kind=kOutput, calls=%fused_computation.16 | convolution fusion | flops 2148532224 | bytes 7340036 | tf_op jit(solution)/shard_map/dot_general | solution.py:558
  318.6 4.8 convolution_convert_fusion.6
  323.4 3.4 add_convert_fusion.5
  326.8 3.3 collective-permute-start.18
  330.0 3.3 convolution_convert_fusion.7
  333.4 5.7 %add_convert_fusion.1 = bf16[512,2048]{1,0:T(8,128)(2,1)} fusion(bf16[512,2048]{1,0:T(8,128)(2,1)} %collective-permute-done.15, bf16[1024,2048]{1,0:T(8,128)(2,1)S(1)} %copy-done.1, bf16[1024,2048]{1,0:T(8,128)(2,1)} %all-gather.9.cloned.1.call-done.hat_ref, s32[]{:T(128)S(6)} %select_n.292), kind=kOutput, calls=%fused_computation.7 | convolution fusion | flops 2150629376 | bytes 9437188 | tf_op jit(solution)/shard_map/dot_general | solution.py:558
  339.1 15.1 %reduce-scatter.6.cloned.1.call-done = bf16[128,2048]{1,0:T(8,128)(2,1)} async-done(((bf16[1024,2048]{1,0:T(8,128)(2,1)}), bf16[128,2048]{1,0:T(8,128)(2,1)}) %reduce-scatter.6.cloned.1.call-update) | async-done | bytes 524304 | tf_op jit(solution)/shard_map/reduce_scatter | solution.py:376
  359.3 3.7 convolution_convert_fusion.5
  363.2 3.7 fusion.42
  371.6 3.4 collective-permute-start.24
  375.1 23.1 %collective-permute-done.21 = bf16[512,2048]{1,0:T(8,128)(2,1)} collective-permute-done((bf16[512,2048]{1,0:T(8,128)(2,1)}, bf16[512,2048]{1,0:T(8,128)(2,1)}, u32[]{:S(2)}, u32[]{:S(2)}) %collective-permute-start.21) | collective-permute-done | bytes 2097184 | tf_op jit(solution)/shard_map/ppermute | solution.py:406
  398.2 4.8 add_convert_fusion
  403.0 4.3 all-to-all-start.2
  407.4 5.1 add_convert_fusion.4
  412.5 4.0 convert_add_fusion.1
  416.5 4.2 fusion.24
  431.0 4.2 collective-permute-start.26
  443.4 5.4 %convolution_convert_fusion = bf16[1024,2048]{1,0:T(8,128)(2,1)} fusion(bf16[512,512]{1,0:T(8,128)(2,1)S(1)} %copy-done.55, bf16[512,512]{1,0:T(8,128)(2,1)S(1)} %copy-done.45, bf16[512,512]{1,0:T(8,128)(2,1)S(1)} %copy-done.43, bf16[512,512]{1,0:T(8,128)(2,1)} %bitcast.11, bf16[1024,256]{0,1:T(8,128)(2,1)S(1)} %fusion.40, ...), kind=kOutput, calls=%fused_computation.12 | convolution fusion | flops 2161115136 | bytes 7340032 | tf_op jit(solution)/shard_map/dot_general | solution.py:555
  456.3 5.6 %collective-permute-done.28 = bf16[512,512]{1,0:T(8,128)(2,1)S(1)} collective-permute-done((bf16[512,512]{1,0:T(8,128)(2,1)S(1)}, bf16[512,512]{1,0:T(8,128)(2,1)S(1)}, u32[]{:S(2)}, u32[]{:S(2)}) %collective-permute-start.28) | collective-permute-done | bytes 524320 | tf_op jit(solution)/shard_map/ppermute | solution.py:406
  465.5 3.4 collective-permute-done.29
  468.9 6.9 %collective-permute-done.30 = bf16[512,512]{1,0:T(8,128)(2,1)} collective-permute-done((bf16[512,512]{1,0:T(8,128)(2,1)}, bf16[512,512]{1,0:T(8,128)(2,1)}, u32[]{:S(2)}, u32[]{:S(2)}) %collective-permute-start.30) | collective-permute-done | bytes 524320 | tf_op jit(solution)/shard_map/ppermute | solution.py:406
  475.8 3.3 fusion.34
  479.1 5.0 all-to-all-start.3
  488.2 3.5 add_convert_fusion.2
  491.7 5.2 collective-permute-start.31
  499.7 4.5 shard_map.204
  504.9 3.4 all-to-all-done.3
  512.5 5.2 collective-permute-done.31
  522.6 8.7 %collective-permute-start.32 = (bf16[128,2048]{1,0:T(8,128)(2,1)}, bf16[128,2048]{1,0:T(8,128)(2,1)S(1)}, u32[]{:S(2)}, u32[]{:S(2)}) collective-permute-start(bf16[128,2048]{1,0:T(8,128)(2,1)} %select_convert_fusion), channel_id=1, source_target_pairs={{0,1},{1,0},{2,3},{3,2},{4,5},{5,4},{6,7},{7,6},{8,9},{9,8},{10,11... | collective-permute-start | bytes 1572872 | tf_op jit(solution)/shard_map/ppermute | solution.py:368
  (285 shorter events, 141.9 us)
Async XLA Ops:
  7.2 76.8 %all-gather.5.cloned.1.call-start = ((), (), s32[]{:S(2)}) async-start(), calls=%async_computation.7 | async-start | bytes 4718592 | tf_op jit(solution)/shard_map/all_gather | solution.py:372
  12.4 44.8 %copy-start.3 = (f32[64,8192]{1,0:T(8,128)S(1)}, f32[64,8192]{1,0:T(8,128)}, u32[]{:S(2)}) copy-start(f32[64,8192]{1,0:T(8,128)} %gate_ref.1) | copy-start | bytes 6291460
  14.4 41.4 %all-to-all-start = ((bf16[8,64,512]{2,1,0:T(8,128)(2,1)}), bf16[8,64,512]{2,1,0:T(8,128)(2,1)}, u32[]{:S(2)}, u32[]{:S(2)}) async-start(bf16[8,64,512]{2,1,0:T(8,128)(2,1)} %bitcast.10), calls=%async_computation | async-start | bytes 1048576 | tf_op jit(solution)/shard_map/all_to_all | solution.py:438
  20.7 151.1 %all-gather.7.cloned.1.call-start = ((), (), s32[]{:S(2)}) async-start(), calls=%async_computation.8 | async-start | bytes 4718592 | tf_op jit(solution)/shard_map/all_gather | solution.py:372
  21.5 54.3 %collective-permute-start = (bf16[64,2048]{1,0:T(8,128)(2,1)}, bf16[64,2048]{1,0:T(8,128)(2,1)S(1)}, u32[]{:S(2)}, u32[]{:S(2)}) collective-permute-start(bf16[64,2048]{1,0:T(8,128)(2,1)} %convert_element_type.316), channel_id=1, source_target_pairs={{0,0},{1,8},{2,16},{3,24},{4,1},{5,9},{6,17},{7,25},{8,2},{9,10},{... | collective-permute-start | bytes 786440 | tf_op jit(solution)/shard_map/ppermute | solution.py:581
  55.8 20.0 %collective-permute-start.2 = (bf16[512,512]{1,0:T(8,128)(2,1)}, bf16[512,512]{1,0:T(8,128)(2,1)}, u32[]{:S(2)}, u32[]{:S(2)}) collective-permute-start(bf16[512,512]{1,0:T(8,128)(2,1)} %bitcast.11), channel_id=1, source_target_pairs={{0,16},{1,9},{2,18},{3,11},{4,20},{5,13},{6,22},{7,15},{8,24},{9,1... | collective-permute-start | bytes 1572872 | tf_op jit(solution)/shard_map/ppermute | solution.py:406
  55.8 20.0 %collective-permute-start.1 = (bf16[512,512]{1,0:T(8,128)(2,1)}, bf16[512,512]{1,0:T(8,128)(2,1)}, u32[]{:S(2)}, u32[]{:S(2)}) collective-permute-start(bf16[512,512]{1,0:T(8,128)(2,1)} %bitcast.11), channel_id=1, source_target_pairs={{0,8},{1,17},{2,10},{3,19},{4,12},{5,21},{6,14},{7,23},{8,0},{9,25... | collective-permute-start | bytes 1572872 | tf_op jit(solution)/shard_map/ppermute | solution.py:406
  84.7 87.1 %all-to-all-start.1 = ((bf16[8,64,2048]{2,1,0:T(8,128)(2,1)}), bf16[8,64,2048]{2,1,0:T(8,128)(2,1)}, u32[]{:S(2)}, u32[]{:S(2)}) async-start(bf16[8,64,2048]{2,1,0:T(8,128)(2,1)} %bitcast.92), calls=%async_computation.1 | async-start | bytes 4194304 | tf_op jit(solution)/shard_map/all_to_all | solution.py:438
  89.1 131.2 %reduce-scatter.4.cloned.1.call-start = ((), (), s32[]{:S(2)}) async-start(), calls=%async_computation.9 | async-start | bytes 4718592 | tf_op jit(solution)/shard_map/reduce_scatter | solution.py:376
  89.3 9.5 %collective-permute-start.3 = (bf16[512,512]{1,0:T(8,128)(2,1)}, bf16[512,512]{1,0:T(8,128)(2,1)S(1)}, u32[]{:S(2)}, u32[]{:S(2)}) collective-permute-start(bf16[512,512]{1,0:T(8,128)(2,1)} %collective-permute-done.1), channel_id=1, source_target_pairs={{0,16},{1,9},{2,18},{3,11},{4,20},{5,13},{6,22},{7,15},{8,24},{9,1... | collective-permute-start | bytes 1572872 | tf_op jit(solution)/shard_map/ppermute | solution.py:406
  107.2 9.3 %collective-permute-start.5 = (bf16[64,2048]{1,0:T(8,128)(2,1)S(1)}, bf16[64,2048]{1,0:T(8,128)(2,1)}, u32[]{:S(2)}, u32[]{:S(2)}) collective-permute-start(bf16[64,2048]{1,0:T(8,128)(2,1)S(1)} %collective-permute-done), channel_id=1, source_target_pairs={{0,8},{1,17},{2,10},{3,19},{4,12},{5,21},{6,14},{7,23},{8,0},{9,25... | collective-permute-start | bytes 786440 | tf_op jit(solution)/shard_map/ppermute | solution.py:406
  107.5 10.2 %collective-permute-start.6 = (bf16[64,2048]{1,0:T(8,128)(2,1)S(1)}, bf16[64,2048]{1,0:T(8,128)(2,1)S(1)}, u32[]{:S(2)}, u32[]{:S(2)}) collective-permute-start(bf16[64,2048]{1,0:T(8,128)(2,1)S(1)} %collective-permute-done), channel_id=1, source_target_pairs={{0,16},{1,9},{2,18},{3,11},{4,20},{5,13},{6,22},{7,15},{8,24},{9,1... | collective-permute-start | bytes 786440 | tf_op jit(solution)/shard_map/ppermute | solution.py:406
  109.5 29.5 %collective-permute-start.9 = (bf16[256,2048]{1,0:T(8,128)(2,1)}, bf16[256,2048]{1,0:T(8,128)(2,1)}, u32[]{:S(2)}, u32[]{:S(2)}) collective-permute-start(bf16[256,2048]{1,0:T(8,128)(2,1)} %convert_element_type.317), channel_id=1, source_target_pairs={{0,8},{1,17},{2,10},{3,19},{4,12},{5,21},{6,14},{7,23},{8,0},{9,25... | collective-permute-start | bytes 3145736 | tf_op jit(solution)/shard_map/ppermute | solution.py:406
  109.6 36.3 %collective-permute-start.8 = (bf16[256,2048]{1,0:T(8,128)(2,1)}, bf16[256,2048]{1,0:T(8,128)(2,1)}, u32[]{:S(2)}, u32[]{:S(2)}) collective-permute-start(bf16[256,2048]{1,0:T(8,128)(2,1)} %convert_element_type.317), channel_id=1, source_target_pairs={{0,16},{1,9},{2,18},{3,11},{4,20},{5,13},{6,22},{7,15},{8,24},{9,1... | collective-permute-start | bytes 3145736 | tf_op jit(solution)/shard_map/ppermute | solution.py:406
  111.3 6.4 %collective-permute-start.4 = (bf16[1024,256]{0,1:T(8,128)(2,1)S(1)}, bf16[1024,256]{0,1:T(8,128)(2,1)S(1)}, u32[]{:S(2)}, u32[]{:S(2)}) collective-permute-start(bf16[1024,256]{0,1:T(8,128)(2,1)S(1)} %fusion.38), channel_id=1, source_target_pairs={{0,1},{1,0},{2,3},{3,2},{4,5},{5,4},{6,7},{7,6},{8,9},{9,8},{10,11... | collective-permute-start | bytes 1572872 | tf_op jit(solution)/shard_map/ppermute | solution.py:368
  116.5 23.8 %collective-permute-start.7 = (bf16[64,2048]{1,0:T(8,128)(2,1)}, bf16[64,2048]{1,0:T(8,128)(2,1)S(1)}, u32[]{:S(2)}, u32[]{:S(2)}) collective-permute-start(bf16[64,2048]{1,0:T(8,128)(2,1)} %collective-permute-done.5), channel_id=1, source_target_pairs={{0,16},{1,9},{2,18},{3,11},{4,20},{5,13},{6,22},{7,15},{8,24},{9,1... | collective-permute-start | bytes 786440 | tf_op jit(solution)/shard_map/ppermute | solution.py:406
  139.0 15.1 %collective-permute-start.10 = (bf16[256,2048]{1,0:T(8,128)(2,1)}, bf16[256,2048]{1,0:T(8,128)(2,1)}, u32[]{:S(2)}, u32[]{:S(2)}) collective-permute-start(bf16[256,2048]{1,0:T(8,128)(2,1)} %collective-permute-done.9), channel_id=1, source_target_pairs={{0,16},{1,9},{2,18},{3,11},{4,20},{5,13},{6,22},{7,15},{8,24},{9,1... | collective-permute-start | bytes 3145736 | tf_op jit(solution)/shard_map/ppermute | solution.py:406
  145.9 74.4 %copy-start.11 = (bf16[1,128,2048]{2,1,0:T(8,128)(2,1)S(1)}, bf16[1,128,2048]{2,1,0:T(8,128)(2,1)}, u32[]{:S(2)}) copy-start(bf16[1,128,2048]{2,1,0:T(8,128)(2,1)} %param.12) | copy-start | bytes 1572868
  171.8 98.4 %all-gather.9.cloned.1.call-start = ((), (), s32[]{:S(2)}) async-start(), calls=%async_computation.10 | async-start | bytes 4718592 | tf_op jit(solution)/shard_map/all_gather | solution.py:372
  171.9 52.9 %collective-permute-start.12 = (bf16[512,2048]{1,0:T(8,128)(2,1)}, bf16[512,2048]{1,0:T(8,128)(2,1)}, u32[]{:S(2)}, u32[]{:S(2)}) collective-permute-start(bf16[512,2048]{1,0:T(8,128)(2,1)} %bitcast.17), channel_id=1, source_target_pairs={{0,16},{1,9},{2,18},{3,11},{4,20},{5,13},{6,22},{7,15},{8,24},{9,1... | collective-permute-start | bytes 6291464 | tf_op jit(solution)/shard_map/ppermute | solution.py:406
  172.0 52.8 %collective-permute-start.11 = (bf16[512,2048]{1,0:T(8,128)(2,1)}, bf16[512,2048]{1,0:T(8,128)(2,1)}, u32[]{:S(2)}, u32[]{:S(2)}) collective-permute-start(bf16[512,2048]{1,0:T(8,128)(2,1)} %bitcast.17), channel_id=1, source_target_pairs={{0,8},{1,17},{2,10},{3,19},{4,12},{5,21},{6,14},{7,23},{8,0},{9,25... | collective-permute-start | bytes 6291464 | tf_op jit(solution)/shard_map/ppermute | solution.py:406
  224.8 129.4 %reduce-scatter.6.cloned.1.call-start = ((), (), s32[]{:S(2)}) async-start(), calls=%async_computation.11 | async-start | bytes 4718592 | tf_op jit(solution)/shard_map/reduce_scatter | solution.py:376
  228.6 26.3 %collective-permute-start.13 = (bf16[512,2048]{1,0:T(8,128)(2,1)}, bf16[512,2048]{1,0:T(8,128)(2,1)S(1)}, u32[]{:S(2)}, u32[]{:S(2)}) collective-permute-start(bf16[512,2048]{1,0:T(8,128)(2,1)} %collective-permute-done.11), channel_id=1, source_target_pairs={{0,16},{1,9},{2,18},{3,11},{4,20},{5,13},{6,22},{7,15},{8,24},{9,1... | collective-permute-start | bytes 6291464 | tf_op jit(solution)/shard_map/ppermute | solution.py:406
  298.5 118.0 %all-gather.11.cloned.1.call-start = ((), (), s32[]{:S(2)}) async-start(), calls=%async_computation.12 | async-start | bytes 4718592 | tf_op jit(solution)/shard_map/all_gather | solution.py:372
  305.5 27.9 %collective-permute-start.15 = (bf16[512,2048]{1,0:T(8,128)(2,1)}, bf16[512,2048]{1,0:T(8,128)(2,1)}, u32[]{:S(2)}, u32[]{:S(2)}) collective-permute-start(bf16[512,2048]{1,0:T(8,128)(2,1)} %convolution_convert_fusion.4), channel_id=1, source_target_pairs={{0,16},{1,9},{2,18},{3,11},{4,20},{5,13},{6,22},{7,15},{8,24},{9,1... | collective-permute-start | bytes 6291464 | tf_op jit(solution)/shard_map/ppermute | solution.py:406
  310.9 12.5 %collective-permute-start.17 = (bf16[256,2048]{1,0:T(8,128)(2,1)}, bf16[256,2048]{1,0:T(8,128)(2,1)}, u32[]{:S(2)}, u32[]{:S(2)}) collective-permute-start(bf16[256,2048]{1,0:T(8,128)(2,1)} %get-tuple-element.185), channel_id=1, source_target_pairs={{0,1},{1,0},{2,3},{3,2},{4,5},{5,4},{6,7},{7,6},{8,9},{9,8},{10,11... | collective-permute-start | bytes 3145736 | tf_op jit(solution)/shard_map/ppermute | solution.py:368
  317.1 38.4 %collective-permute-start.16 = (bf16[512,2048]{1,0:T(8,128)(2,1)}, bf16[512,2048]{1,0:T(8,128)(2,1)}, u32[]{:S(2)}, u32[]{:S(2)}) collective-permute-start(bf16[512,2048]{1,0:T(8,128)(2,1)} %convolution_convert_fusion.3), channel_id=1, source_target_pairs={{0,16},{1,9},{2,18},{3,11},{4,20},{5,13},{6,22},{7,15},{8,24},{9,1... | collective-permute-start | bytes 6291464 | tf_op jit(solution)/shard_map/ppermute | solution.py:406
  326.8 28.7 %collective-permute-start.18 = (bf16[256,2048]{1,0:T(8,128)(2,1)}, bf16[256,2048]{1,0:T(8,128)(2,1)}, u32[]{:S(2)}, u32[]{:S(2)}) collective-permute-start(bf16[256,2048]{1,0:T(8,128)(2,1)} %get-tuple-element.135), channel_id=1, source_target_pairs={{0,2},{7,5},{8,10},{15,13},{16,18},{23,21},{24,26},{31,29}} | collective-permute-start | bytes 3145736 | tf_op jit(solution)/shard_map/ppermute | solution.py:382
  357.3 40.9 %collective-permute-start.21 = (bf16[512,2048]{1,0:T(8,128)(2,1)}, bf16[512,2048]{1,0:T(8,128)(2,1)}, u32[]{:S(2)}, u32[]{:S(2)}) collective-permute-start(bf16[512,2048]{1,0:T(8,128)(2,1)} %add_convert_fusion.1), channel_id=1, source_target_pairs={{0,8},{1,17},{2,10},{3,19},{4,12},{5,21},{6,14},{7,23},{8,0},{9,25... | collective-permute-start | bytes 6291464 | tf_op jit(solution)/shard_map/ppermute | solution.py:406
  363.1 5.9 %collective-permute-start.23 = (bf16[256,2048]{1,0:T(8,128)(2,1)S(1)}, bf16[256,2048]{1,0:T(8,128)(2,1)S(1)}, u32[]{:S(2)}, u32[]{:S(2)}) collective-permute-start(bf16[256,2048]{1,0:T(8,128)(2,1)S(1)} %convolution_convert_fusion.5), channel_id=1, source_target_pairs={{0,1},{1,0},{2,3},{3,2},{4,5},{5,4},{6,7},{7,6},{8,9},{9,8},{10,11... | collective-permute-start | bytes 3145736 | tf_op jit(solution)/shard_map/ppermute | solution.py:368
  366.8 40.5 %collective-permute-start.19 = (bf16[256,2048]{1,0:T(8,128)(2,1)}, bf16[256,2048]{1,0:T(8,128)(2,1)}, u32[]{:S(2)}, u32[]{:S(2)}) collective-permute-start(bf16[256,2048]{1,0:T(8,128)(2,1)} %convolution_convert_fusion.7), channel_id=1, source_target_pairs={{0,16},{1,9},{2,18},{3,11},{4,20},{5,13},{6,22},{7,15},{8,24},{9,1... | collective-permute-start | bytes 3145736 | tf_op jit(solution)/shard_map/ppermute | solution.py:406
  368.7 38.7 %collective-permute-start.20 = (bf16[256,2048]{1,0:T(8,128)(2,1)}, bf16[256,2048]{1,0:T(8,128)(2,1)}, u32[]{:S(2)}, u32[]{:S(2)}) collective-permute-start(bf16[256,2048]{1,0:T(8,128)(2,1)} %convolution_convert_fusion.6), channel_id=1, source_target_pairs={{0,16},{1,9},{2,18},{3,11},{4,20},{5,13},{6,22},{7,15},{8,24},{9,1... | collective-permute-start | bytes 3145736 | tf_op jit(solution)/shard_map/ppermute | solution.py:406
  371.6 58.2 %collective-permute-start.24 = (bf16[256,2048]{1,0:T(8,128)(2,1)}, bf16[256,2048]{1,0:T(8,128)(2,1)}, u32[]{:S(2)}, u32[]{:S(2)}) collective-permute-start(bf16[256,2048]{1,0:T(8,128)(2,1)} %add_convert_fusion.3), channel_id=1, source_target_pairs={{0,2},{2,4},{7,5},{5,3},{8,10},{10,12},{15,13},{13,11},{16,18},{18... | collective-permute-start | bytes 3145736 | tf_op jit(solution)/shard_map/ppermute | solution.py:382
  403.0 60.5 %all-to-all-start.2 = ((bf16[8,64,2048]{2,1,0:T(8,128)(2,1)}), bf16[8,64,2048]{2,1,0:T(8,128)(2,1)}, u32[]{:S(2)}, u32[]{:S(2)}) async-start(bf16[8,64,2048]{2,1,0:T(8,128)(2,1)} %bitcast.91), calls=%async_computation.4 | async-start | bytes 4194304 | tf_op jit(solution)/shard_map/all_to_all | solution.py:438
  407.3 123.9 %reduce-scatter.8.cloned.1.call-start = ((), (), s32[]{:S(2)}) async-start(), calls=%async_computation.13 | async-start | bytes 4718592 | tf_op jit(solution)/shard_map/reduce_scatter | solution.py:376
  422.9 7.3 %collective-permute-start.22 = (bf16[64,2048]{1,0:T(8,128)(2,1)S(1)}, bf16[64,2048]{1,0:T(8,128)(2,1)S(1)}, u32[]{:S(2)}, u32[]{:S(2)}) collective-permute-start(bf16[64,2048]{1,0:T(8,128)(2,1)S(1)} %get-tuple-element.144), channel_id=1, source_target_pairs={{0,16},{1,9},{2,18},{3,11},{4,20},{5,13},{6,22},{7,15},{8,24},{9,1... | collective-permute-start | bytes 786440 | tf_op jit(solution)/shard_map/ppermute | solution.py:406
  424.6 24.3 %collective-permute-start.27 = (bf16[256,2048]{1,0:T(8,128)(2,1)}, bf16[256,2048]{1,0:T(8,128)(2,1)}, u32[]{:S(2)}, u32[]{:S(2)}) collective-permute-start(bf16[256,2048]{1,0:T(8,128)(2,1)} %add_convert_fusion.4), channel_id=1, source_target_pairs={{0,8},{1,17},{2,10},{3,19},{4,12},{5,21},{6,14},{7,23},{8,0},{9,25... | collective-permute-start | bytes 3145736 | tf_op jit(solution)/shard_map/ppermute | solution.py:406
  431.0 17.9 %collective-permute-start.26 = (bf16[64,2048]{1,0:T(8,128)(2,1)}, bf16[64,2048]{1,0:T(8,128)(2,1)}, u32[]{:S(2)}, u32[]{:S(2)}) collective-permute-start(bf16[64,2048]{1,0:T(8,128)(2,1)} %add_convert_fusion.9), channel_id=1, source_target_pairs={{0,8},{1,17},{2,10},{3,19},{4,12},{5,21},{6,14},{7,23},{8,0},{9,25... | collective-permute-start | bytes 786440 | tf_op jit(solution)/shard_map/ppermute | solution.py:406
  437.4 3.2 collective-permute-start.25
  452.7 9.2 %collective-permute-start.28 = (bf16[512,512]{1,0:T(8,128)(2,1)S(1)}, bf16[512,512]{1,0:T(8,128)(2,1)S(1)}, u32[]{:S(2)}, u32[]{:S(2)}) collective-permute-start(bf16[512,512]{1,0:T(8,128)(2,1)S(1)} %convolution_convert_fusion.12), channel_id=1, source_target_pairs={{0,16},{1,9},{2,18},{3,11},{4,20},{5,13},{6,22},{7,15},{8,24},{9,1... | collective-permute-start | bytes 1572872 | tf_op jit(solution)/shard_map/ppermute | solution.py:406
  456.1 12.8 %collective-permute-start.29 = (bf16[512,512]{1,0:T(8,128)(2,1)}, bf16[512,512]{1,0:T(8,128)(2,1)S(1)}, u32[]{:S(2)}, u32[]{:S(2)}) collective-permute-start(bf16[512,512]{1,0:T(8,128)(2,1)} %convolution_convert_fusion.11), channel_id=1, source_target_pairs={{0,16},{1,9},{2,18},{3,11},{4,20},{5,13},{6,22},{7,15},{8,24},{9,1... | collective-permute-start | bytes 1572872 | tf_op jit(solution)/shard_map/ppermute | solution.py:406
  463.5 12.3 %collective-permute-start.30 = (bf16[512,512]{1,0:T(8,128)(2,1)}, bf16[512,512]{1,0:T(8,128)(2,1)}, u32[]{:S(2)}, u32[]{:S(2)}) collective-permute-start(bf16[512,512]{1,0:T(8,128)(2,1)} %add_convert_fusion.7), channel_id=1, source_target_pairs={{0,8},{1,17},{2,10},{3,19},{4,12},{5,21},{6,14},{7,23},{8,0},{9,25... | collective-permute-start | bytes 1572872 | tf_op jit(solution)/shard_map/ppermute | solution.py:406
  463.5 24.7 %collective-permute-start.14 = (bf16[256,2048]{1,0:T(8,128)(2,1)}, bf16[256,2048]{1,0:T(8,128)(2,1)}, u32[]{:S(2)}, u32[]{:S(2)}) collective-permute-start(bf16[256,2048]{1,0:T(8,128)(2,1)} %get-tuple-element.136), channel_id=1, source_target_pairs={{0,1},{1,0},{2,3},{3,2},{4,5},{5,4},{6,7},{7,6},{8,9},{9,8},{10,11... | collective-permute-start | bytes 3145736 | tf_op jit(solution)/shard_map/ppermute | solution.py:368
  464.8 19.2 %collective-permute-start.33 = (bf16[64,2048]{1,0:T(8,128)(2,1)S(1)}, bf16[64,2048]{1,0:T(8,128)(2,1)}, u32[]{:S(2)}, u32[]{:S(2)}) collective-permute-start(bf16[64,2048]{1,0:T(8,128)(2,1)S(1)} %copy-done.49), channel_id=1, source_target_pairs={{0,16},{1,9},{2,18},{3,11},{4,20},{5,13},{6,22},{7,15},{8,24},{9,1... | collective-permute-start | bytes 786440 | tf_op jit(solution)/shard_map/ppermute | solution.py:406
  479.1 29.2 %all-to-all-start.3 = ((bf16[8,64,512]{2,1,0:T(8,128)(2,1)}), bf16[8,64,512]{2,1,0:T(8,128)(2,1)S(1)}, u32[]{:S(2)}, u32[]{:S(2)}) async-start(bf16[8,64,512]{2,1,0:T(8,128)(2,1)} %bitcast.105), calls=%async_computation.6 | async-start | bytes 1048576 | tf_op jit(solution)/shard_map/all_to_all | solution.py:438
  486.2 18.6 %collective-permute-start.34 = (bf16[64,2048]{1,0:T(8,128)(2,1)}, bf16[64,2048]{1,0:T(8,128)(2,1)S(1)}, u32[]{:S(2)}, u32[]{:S(2)}) collective-permute-start(bf16[64,2048]{1,0:T(8,128)(2,1)} %add_convert_fusion.8), channel_id=1, source_target_pairs={{0,0},{8,1},{16,2},{24,3},{1,4},{9,5},{17,6},{25,7},{2,8},{10,9},{... | collective-permute-start | bytes 786440 | tf_op jit(solution)/shard_map/ppermute | solution.py:759
  491.7 26.0 %collective-permute-start.31 = (bf16[256,2048]{1,0:T(8,128)(2,1)}, bf16[256,2048]{1,0:T(8,128)(2,1)}, u32[]{:S(2)}, u32[]{:S(2)}) collective-permute-start(bf16[256,2048]{1,0:T(8,128)(2,1)} %add_convert_fusion.2), channel_id=1, source_target_pairs={{0,2},{2,4},{4,6},{7,5},{5,3},{3,1},{8,10},{10,12},{12,14},{15,13}... | collective-permute-start | bytes 3145736 | tf_op jit(solution)/shard_map/ppermute | solution.py:382
  522.6 10.4 %collective-permute-start.32 = (bf16[128,2048]{1,0:T(8,128)(2,1)}, bf16[128,2048]{1,0:T(8,128)(2,1)S(1)}, u32[]{:S(2)}, u32[]{:S(2)}) collective-permute-start(bf16[128,2048]{1,0:T(8,128)(2,1)} %select_convert_fusion), channel_id=1, source_target_pairs={{0,1},{1,0},{2,3},{3,2},{4,5},{5,4},{6,7},{7,6},{8,9},{9,8},{10,11... | collective-permute-start | bytes 1572872 | tf_op jit(solution)/shard_map/ppermute | solution.py:368
  (55 other events, 421.6 us)
Sparse Core Ops, SparseCore 0:
  10.2 73.7 all-gather.4
  85.6 84.4 all-gather.6
  172.4 47.8 reduce-scatter.3
  224.9 45.2 all-gather.8
  298.6 55.5 reduce-scatter.5
  357.4 55.3 all-gather.10
  449.0 60.2 reduce-scatter.7
